TPU v7x, 256 devices: a whole 4x4x8 slice. The times are simulated.
256 devices in a mesh: tile: 64 (over y, x, z_lo, core), agent: 4 (over z_hi).
Axes of the slice: x: 4, y: 4, z: 8 (z_hi: 4, z_lo: 2; z = z_hi * 2 + z_lo), core: 2. Of those that a mesh axis runs over, the one named last changes fastest.
Arguments:
- agent_state: float32 [4, 1, 16, 1024, 256], P(None, None, None, 'tile', 'agent'), may hold values from 0 to 2
- measured: float32 [1, 16, 22528], P(None, None, ('tile', 'agent')), may hold values from 0 to 12
- bin_index: int32 [16, 1024, 256], P(None, 'tile', 'agent'), may hold values from 64 to 1342, as said below
- bin_frac: int32 [16, 1024, 256], P(None, 'tile', 'agent'), may hold values from 0 to 723, as said below
- patch_offsets: int32 [3], replicated, may hold values from 1 to 15
- agent_weights: float32 [4], replicated, may hold values from 0.5 to 2
- up_weight: bfloat16 [3, 256, 4096], P(None, None, 'agent'), may hold values from -0.375 to 0.375
- down_weight: bfloat16 [3, 4096, 256], P(None, 'agent'), may hold values from -0.09375 to 0.09375
Outputs:
- state_next: float32 [4, 1, 16, 1024, 256], P(None, None, None, 'tile', 'agent')
- data_fit: float32 [1, 16, 1024, 256], P(None, None, 'tile', 'agent')
Inputs may be any that keep to these rules, and one draw needn't show every extreme that they name: bin_index[a, x, y] = floor(((x - 512) c_a + (y - 128) s_a) / 724) + 704 and bin_frac[a, x, y] is the remainder of that division, for whole numbers c_a, s_a of size at most 724 with c_a * c_a + s_a * s_a close to 524176, one pair an angle. bin_frac is the remainder that belongs to bin_index.
All inputs are finite; a program needn't handle non-finite values.
Results may differ from a plain program's by a relative error of at most 0.0003.
The roundings to bfloat16 on the way count: a program that leaves them out, or rounds other values in their place, can miss the bound.
Values may be sent and summed in bfloat16 or wider, within the bound.
No kernel may reach another device: no remote copies, remote signals or barrier semaphores. Data moves between devices by JAX's collectives and lax.ppermute only.
A program may use at most 64 MiB of HBM per device.

v0:
```python
import math

import jax
import jax.numpy as jnp
from jax import lax
from jax.sharding import PartitionSpec as P

PATCH = 16


def extended_2(block, sides, width):
    for axis, dim in sides:
        count = lax.axis_size(axis)
        forward = [(i, i + 1) for i in range(count - 1)]
        forward.append((count - 1, 0))
        backward = [(target, source) for source, target in forward]
        low = lax.ppermute(
            lax.slice_in_dim(block, block.shape[dim] - width, None, axis=dim), axis, forward
        )
        high = lax.ppermute(lax.slice_in_dim(block, 0, width, axis=dim), axis, backward)
        block = jnp.concatenate([low, block, high], axis=dim)
    return block


def make_band(low_rel, weight, offsets):
    near = jnp.where(low_rel[:, None] == offsets[None, :], weight[:, None], 0.0)
    far = jnp.where(low_rel[:, None] + 1 == offsets[None, :], (1.0 - weight)[:, None], 0.0)
    return near + far


def data_agent(volume, bin_index, bin_frac, measured, factor, sino_width):
    angles = bin_index.shape[0]
    planes = volume.shape[0] * volume.shape[1]
    current = volume.reshape(planes, -1)
    bins_each = sino_width // angles
    window = (bin_index.shape[1] + bin_index.shape[2] + 2 + 31) // 32 * 32
    offsets = jnp.arange(window, dtype=jnp.int32)
    lows = bin_index.reshape(angles, -1)
    weight = bin_frac.reshape(angles, -1).astype(jnp.float32) / 724.0
    starts = jnp.minimum(jnp.min(lows, axis=1), bins_each - window)
    target = measured.reshape(planes, -1)
    anchor = jnp.zeros((), jnp.int32)
    highest = lax.Precision.HIGHEST

    def place(piece, start):
        return lax.dynamic_update_slice(
            jnp.zeros((planes, bins_each), jnp.float32), piece, (anchor, start)
        )

    def project(carry, item):
        low_a, weight_a, start = item
        band = make_band(low_a - start, weight_a, offsets)
        return (
            carry,
            jnp.dot(current, band, precision=highest, preferred_element_type=jnp.float32),
        )

    unused, windows = lax.scan(project, jnp.zeros((), jnp.float32), (lows, weight, starts))
    partial_sino = jax.vmap(place, in_axes=(0, 0), out_axes=1)(windows, starts).reshape(planes, -1)
    owned_bins = lax.psum_scatter(
        factor * partial_sino, ("tile", "agent"), scatter_dimension=1, tiled=True
    )
    misfit = owned_bins - target
    all_bins = lax.all_gather(misfit, ("tile", "agent"), axis=1, tiled=True)
    by_angle = jnp.transpose(all_bins.reshape(planes, angles, bins_each), (1, 0, 2))

    def spread(total, item):
        low_a, weight_a, start, resid = item
        band = make_band(low_a - start, weight_a, offsets)
        picked = lax.dynamic_slice_in_dim(resid, start, window, 1)
        return (
            total + jnp.dot(picked, band.T, precision=highest, preferred_element_type=jnp.float32),
            None,
        )

    back_sum, unused = lax.scan(spread, jnp.zeros_like(current), (lows, weight, starts, by_angle))
    current = current - factor * back_sum
    return current.reshape(volume.shape)


def in_plane(extended, shift, apply_net):
    n_time, n_slice, ext_rows, ext_cols = extended.shape
    row_count = ext_rows - 2 * PATCH
    col_count = ext_cols - 2 * PATCH
    row_blocks = row_count // PATCH + 1
    col_blocks = col_count // PATCH + 1
    region = lax.dynamic_slice(
        extended, (0, 0, shift, shift), (n_time, n_slice, row_count + PATCH, col_count + PATCH)
    )
    patches = region.reshape(n_time, n_slice, row_blocks, PATCH, col_blocks, PATCH)
    patches = patches.transpose(0, 1, 2, 4, 3, 5).reshape(-1, PATCH * PATCH)
    result = apply_net(patches)
    result = result.reshape(n_time, n_slice, row_blocks, col_blocks, PATCH, PATCH)
    result = result.transpose(0, 1, 2, 4, 3, 5).reshape(
        n_time, n_slice, row_count + PATCH, col_count + PATCH
    )
    return lax.dynamic_slice(
        result, (0, 0, PATCH - shift, PATCH - shift), (n_time, n_slice, row_count, col_count)
    )


def along_rows(extended, shift, apply_net):
    n_time, n_slice, ext_rows, ext_cols = extended.shape
    row_count = ext_rows - 2 * PATCH
    col_count = ext_cols - 2 * PATCH
    row_blocks = row_count // PATCH + 1
    region = lax.dynamic_slice(
        extended, (0, 0, shift, PATCH), (n_time, n_slice, row_count + PATCH, col_count)
    )
    patches = region.reshape(n_time, n_slice, row_blocks, PATCH, col_count)
    patches = patches.transpose(0, 2, 4, 1, 3).reshape(-1, n_slice * PATCH)
    result = apply_net(patches)
    result = result.reshape(n_time, row_blocks, col_count, n_slice, PATCH)
    result = result.transpose(0, 3, 1, 4, 2).reshape(n_time, n_slice, row_count + PATCH, col_count)
    return lax.dynamic_slice(
        result, (0, 0, PATCH - shift, 0), (n_time, n_slice, row_count, col_count)
    )


def along_cols(extended, shift, apply_net):
    n_time, n_slice, ext_rows, ext_cols = extended.shape
    row_count = ext_rows - 2 * PATCH
    col_count = ext_cols - 2 * PATCH
    col_blocks = col_count // PATCH + 1
    region = lax.dynamic_slice(
        extended, (0, 0, PATCH, shift), (n_time, n_slice, row_count, col_count + PATCH)
    )
    patches = region.reshape(n_time, n_slice, row_count, col_blocks, PATCH)
    patches = patches.transpose(0, 2, 3, 1, 4).reshape(-1, n_slice * PATCH)
    result = apply_net(patches)
    result = result.reshape(n_time, row_count, col_blocks, n_slice, PATCH)
    result = result.transpose(0, 3, 1, 2, 4).reshape(n_time, n_slice, row_count, col_count + PATCH)
    return lax.dynamic_slice(
        result, (0, 0, 0, PATCH - shift), (n_time, n_slice, row_count, col_count)
    )


def shards(
    agent_state, measured, bin_index, bin_frac, patch_offsets, agent_weights, up_weight, down_weight
):
    row_count = agent_state.shape[3]
    col_count = agent_state.shape[4]
    tile_count = lax.axis_size("tile")
    agent_count = lax.axis_size("agent")
    full_rows = row_count * tile_count
    full_cols = col_count * agent_count
    angles = bin_index.shape[0]
    factor = 1.0 / math.sqrt(angles * (full_rows + full_cols))
    sino_width = measured.shape[2] * tile_count * agent_count
    data_fit = data_agent(agent_state[0], bin_index, bin_frac, measured, factor, sino_width)
    noisy = agent_state[1:].astype(jnp.bfloat16)
    extended = extended_2(noisy, (("tile", 3), ("agent", 4)), PATCH)

    def denoiser(which):

        def apply_net(patches):
            hidden = jax.nn.relu(
                jnp.dot(
                    lax.all_gather(patches, "agent", axis=0, tiled=True),
                    up_weight[which],
                    preferred_element_type=jnp.float32,
                )
            ).astype(jnp.bfloat16)
            terms = jnp.dot(hidden, down_weight[which], preferred_element_type=jnp.float32)
            return lax.psum_scatter(terms, "agent", scatter_dimension=0, tiled=True)

        return apply_net

    first = agent_state[1] - in_plane(extended[0], patch_offsets[0], denoiser(0))
    second = agent_state[2] - along_rows(extended[1], patch_offsets[1], denoiser(1))
    third = agent_state[3] - along_cols(extended[2], patch_offsets[2], denoiser(2))
    answers = jnp.stack([data_fit, first, second, third])
    joining = agent_weights / jnp.sum(agent_weights)
    joined = jnp.sum(joining[:, None, None, None, None] * (2.0 * answers - agent_state), axis=0)
    state_next = agent_state + joined[None] - answers
    return (state_next, data_fit)


def solution(mesh):
    placed = (
        P(None, None, None, "tile", "agent"),
        P(None, None, ("tile", "agent")),
        P(None, "tile", "agent"),
        P(None, "tile", "agent"),
        P(),
        P(),
        P(None, None, "agent"),
        P(None, "agent", None),
    )
    return jax.shard_map(
        shards,
        mesh=mesh,
        in_specs=placed,
        out_specs=(P(None, None, None, "tile", "agent"), P(None, None, "tile", "agent")),
        check_vma=False,
    )
```

profile of v0, /device:TPU:1, one launch (start us, length us, event | category | flops | bytes accessed | tf_op | source)
XLA Modules:
  0.0 1243.4 jit_solution(16518428569459968049)
XLA Ops:
  9.1 3.1 collective-permute-start
  15.9 35.8 %while.29 = (s32[]{:T(128)}, f32[16,16,96]{2,1,0:T(8,128)S(1)}, s32[16,1024]{1,0:T(8,128)S(1)}, s32[16]{0:T(128)S(1)}, f32[16,1024]{1,0:T(8,128)S(1)}, /*index=5*/f32[16,1024]{1,0:T(8,128)S(1)}, s32[]{:T(128)}) while((s32[]{:T(128)}, f32[16,16,96]{2,1,0:T(8,128)S(1)}, s32[16,1024]{1,0:T(8,128)S(1)}, s32[16]{0:T(128)S(1)}, ...), condition=%wide.region_3.4_spmd.clone.clone, body=%wide.region_2.3_spmd.clone.clone.sunk | while | flops 19368960 | bytes 122985 | solution.py:58
  52.4 108.0 %while.28 = (s32[]{:T(128)}, f32[16,16,1408]{2,1,0:T(8,128)S(1)}, s32[16,3]{0,1:T(4,128)S(1)}, f32[16,16,96]{2,1,0:T(8,128)S(1)}, s32[]{:T(128)}, /*index=5*/s32[3]{0:T(128)S(1)}, s32[]{:T(128)}) while((s32[]{:T(128)}, f32[16,16,1408]{2,1,0:T(8,128)S(1)}, s32[16,3]{0,1:T(4,128)S(1)}, f32[16,16,96]{2,1,0:T(8,128)S(1)}, s32[]{:T(128)}, ...), condition=%wide.while_cond, body=%wide.while_body.sunk | while | flops 1555 | bytes 30891 | solution.py:46
  53.1 2.6 and_reduce_fusion.2
  55.7 1.9 dynamic-slice_select_fusion.2
  59.8 2.6 and_reduce_fusion.2
  62.4 1.9 dynamic-slice_select_fusion.2
  66.6 2.6 and_reduce_fusion.2
  69.2 1.9 dynamic-slice_select_fusion.2
  73.3 2.6 and_reduce_fusion.2
  75.9 1.9 dynamic-slice_select_fusion.2
  80.1 2.6 and_reduce_fusion.2
  82.7 1.9 dynamic-slice_select_fusion.2
  86.8 2.6 and_reduce_fusion.2
  89.4 1.9 dynamic-slice_select_fusion.2
  93.6 2.6 and_reduce_fusion.2
  96.2 1.9 dynamic-slice_select_fusion.2
  100.3 2.6 and_reduce_fusion.2
  102.9 1.9 dynamic-slice_select_fusion.2
  107.1 2.6 and_reduce_fusion.2
  109.7 1.9 dynamic-slice_select_fusion.2
  113.8 2.6 and_reduce_fusion.2
  116.4 1.9 dynamic-slice_select_fusion.2
  120.6 2.6 and_reduce_fusion.2
  123.2 1.9 dynamic-slice_select_fusion.2
  127.3 2.6 and_reduce_fusion.2
  129.9 1.9 dynamic-slice_select_fusion.2
  134.1 2.6 and_reduce_fusion.2
  136.7 1.9 dynamic-slice_select_fusion.2
  140.8 2.6 and_reduce_fusion.2
  143.4 1.9 dynamic-slice_select_fusion.2
  147.6 2.6 and_reduce_fusion.2
  150.2 1.9 dynamic-slice_select_fusion.2
  154.3 2.6 and_reduce_fusion.2
  156.9 1.9 dynamic-slice_select_fusion.2
  162.4 2.8 collective-permute-start.2
  165.5 2.2 collective-permute-start.3
  170.8 3.2 collective-permute-done.3
  175.8 14.0 %all_gather.15 = bf16[320,256]{1,0:T(8,128)(2,1)S(1)} all-gather(bf16[80,256]{1,0:T(8,128)(2,1)S(1)} %reshape.226), channel_id=1, replica_groups=mesh['tile'=64,'agent'=4] {'agent'}, dimensions={0}, use_global_device_ids=true | all-gather | bytes 204800 | tf_op jit(solution)/shard_map/all_gather | solution.py:159
  189.8 2.4 fusion.27
  194.7 15.4 %all_gather.14 = bf16[512,256]{0,1:T(8,128)(2,1)S(1)} all-gather(bf16[128,256]{0,1:T(8,128)(2,1)S(1)} %reshape.222), channel_id=1, replica_groups=mesh['tile'=64,'agent'=4] {'agent'}, dimensions={0}, use_global_device_ids=true | all-gather | bytes 327680 | tf_op jit(solution)/shard_map/all_gather | solution.py:159
  210.0 2.7 fusion.24
  216.1 2.2 copy.50
  218.9 12.0 all_gather.13
  230.9 2.9 fusion.23
  233.8 195.4 %all-reduce.4.cloned.1.call-done = f32[16,22528]{1,0:T(8,128)} async-done(((f32[16,22528]{1,0:T(8,128)}), f32[16,22528]{1,0:T(8,128)}) %all-reduce.4.cloned.1.call-update) | async-done | bytes 1441808
  440.4 2.6 copy.51
  443.0 2.1 reshape.220
  445.7 700.9 %all-gather.3.cloned.1.call-done = f32[256,88,16]{1,2,0:T(8,128)} async-done(((f32[1,88,16]{1,2,0:T(8,128)}), f32[256,88,16]{1,2,0:T(8,128)}) %all-gather.3.cloned.1.call-update) | async-done | bytes 1441808 | tf_op jit(solution)/shard_map/all_gather | solution.py:64
  1146.6 2.3 copy.43
  1148.9 2.4 reshape.260
  1152.9 81.0 %while.30 = (s32[]{:T(128)}, f32[16,1024]{1,0:T(8,128)S(1)}, s32[16]{0:T(128)S(1)}, f32[16,16,1408]{2,0,1:T(8,128)S(1)}, s32[16,1024]{1,0:T(8,128)S(1)}, /*index...) while((s32[]{:T(128)}, f32[16,1024]{1,0:T(8,128)S(1)}, ...), condition=%wide.region_7.8_spmd.clone.clone, body=%wide.region_6.7_spmd.clone.clone.sunk | while | flops 19401736 | bytes 198873 | solution.py:76
  1156.3 1.7 convolution_add_fusion.2
  1161.4 1.7 convolution_add_fusion.2
  1166.4 1.7 convolution_add_fusion.2
  1171.5 1.7 convolution_add_fusion.2
  1176.6 1.7 convolution_add_fusion.2
  1181.6 1.7 convolution_add_fusion.2
  1186.7 1.7 convolution_add_fusion.2
  1191.8 1.7 convolution_add_fusion.2
  1196.8 1.7 convolution_add_fusion.2
  1201.9 1.7 convolution_add_fusion.2
  1212.0 1.7 convolution_add_fusion.2
  1217.1 1.7 convolution_add_fusion.2
  (331 shorter events, 122.9 us)
Async XLA Ops:
  8.0 7.8 slice-start
  8.0 421.2 %all-reduce.4.cloned.1.call-start = ((), (), s32[]{:S(2)}) async-start(), calls=%async_computation.7 | async-start | bytes 2883584
  9.1 152.7 %collective-permute-start = (bf16[3,1,16,16,64]{4,3,2,1,0:T(8,128)(2,1)S(1)}, bf16[3,1,16,16,64]{4,3,2,1,0:T(8,128)(2,1)S(1)}, u32[]{:S(2)}, u32[]{:S(2)}) collective-permute-start(bf16[3,1,16,16,64]{4,3,2,1,0:T(8,128)(2,1)S(1)} %slice.131), channel_id=1, source_target_pairs={{0,4},{4,8},{8,12},{12,16},{16,20},{20,24},{24,28},{28,32},{32,36}... | collective-permute-start | bytes 294920 | tf_op jit(solution)/shard_map/ppermute | solution.py:17
  12.2 149.6 %collective-permute-start.1 = (bf16[3,1,16,16,64]{4,3,2,1,0:T(8,128)(2,1)S(1)}, bf16[3,1,16,16,64]{4,3,2,1,0:T(8,128)(2,1)S(1)}, u32[]{:S(2)}, u32[]{:S(2)}) collective-permute-start(bf16[3,1,16,16,64]{4,3,2,1,0:T(8,128)(2,1)S(1)} %slice.131), channel_id=1, source_target_pairs={{4,0},{8,4},{12,8},{16,12},{20,16},{24,20},{28,24},{32,28},{36,32}... | collective-permute-start | bytes 294920 | tf_op jit(solution)/shard_map/ppermute | solution.py:20
  51.7 0.7 copy-start.1
  161.8 274.5 %reduce-scatter.9.cloned.1.call-start = ((), (), s32[]{:S(2)}) async-start(), calls=%async_computation.5 | async-start | bytes 409600 | tf_op jit(solution)/shard_map/reduce_scatter | solution.py:165
  162.0 5.7 copy-start.3
  162.4 8.1 collective-permute-start.2
  165.5 8.5 collective-permute-start.3
  174.8 15.0 %copy-start.4 = (bf16[3,1024,256]{2,1,0:T(8,128)(2,1)S(1)}, bf16[3,1024,256]{2,1,0:T(8,128)(2,1)}, u32[]{:S(2)}) copy-start(bf16[3,1024,256]{2,1,0:T(8,128)(2,1)} %param.19) | copy-start | bytes 4718596
  192.2 245.7 %reduce-scatter.7.cloned.1.call-start = ((), (), s32[]{:S(2)}) async-start(), calls=%async_computation.4 | async-start | bytes 655360 | tf_op jit(solution)/shard_map/reduce_scatter | solution.py:165
  212.7 226.4 %reduce-scatter.5.cloned.1.call-start = ((), (), s32[]{:S(2)}) async-start(), calls=%async_computation.3 | async-start | bytes 819200 | tf_op jit(solution)/shard_map/reduce_scatter | solution.py:165
  230.9 198.4 %copy-start.2 = (f32[1,16,88]{2,1,0:T(8,128)S(1)}, f32[1,16,88]{2,1,0:T(8,128)}, u32[]{:S(2)}) copy-start(f32[1,16,88]{2,1,0:T(8,128)} %param.13) | copy-start | bytes 16900
  230.9 204.0 %copy-start.5 = (f32[4]{0:T(128)S(1)}, f32[4]{0:T(128)}, u32[]{:S(2)}) copy-start(f32[4]{0:T(128)} %param.17) | copy-start | bytes 52
  233.8 912.8 %all-gather.3.cloned.1.call-start = ((), (), s32[]{:S(2)}) async-start(), calls=%async_computation.6 | async-start | bytes 2105344 | tf_op jit(solution)/shard_map/all_gather | solution.py:64
  443.0 2.5 copy-start
Sparse Core Ops, SparseCore 0:
  161.9 267.3 all-reduce.3
  431.7 714.8 all-gather.2
Sparse Core Ops, SparseCore 1:
  192.3 28.8 reduce-scatter.8
  224.1 26.8 reduce-scatter.6
  253.4 28.7 reduce-scatter.4
where the time goes:
time: 1250 us; the launch traced here: 1240 us
  waiting for transfers between devices  900 us (72%)
  other arithmetic  99.9 us (8%)
  local copies, waits for them, and re-layouts  84.5 us (7%)
  matrix products  49.2 us (4%)
  blocking collectives  41.4 us (3%)
  loops' own time  33 us (3%)
  between operations  26.7 us (2%)
    all_gather x1, waiting for transfers between devices, data_agent(): all_bins = lax.all_gather(misfit, ('tile', 'agent'), axis=1, tiled=True)  701 us
    unnamed x6, waiting for transfers between devices  195 us
    scatter x32, other arithmetic  72.1 us
    all_gather x3, blocking collectives, apply_net(): lax.all_gather(patches, 'agent', axis=0, tiled=True)  41.4 us
    scatter x48, local copies, waits for them, and re-layouts  35.8 us
    another operation x1, loops' own time, data_agent(): lax.scan(spread, jnp.zeros_like(current), (lows, weight, starts, by_angle))  32.2 us
    dot_general x16, matrix products, spread(): jnp.dot(picked, band.T, precision=highest, preferred_element_type=jnp.flo...  27 us
  transfers between devices with their start and end apart: 9, of which 4 were waited for; matrix products, arithmetic and copies ran while one was open for 14% of the time, Pallas kernels for 0%

commit v1 on v0

--- a/solution.py
+++ b/solution.py
@@ -1,11 +1,17 @@
+import functools
 import math
 
 import jax
 import jax.numpy as jnp
 from jax import lax
+from jax.experimental import pallas as pl
+from jax.experimental.pallas import tpu as pltpu
 from jax.sharding import PartitionSpec as P
 
 PATCH = 16
+SCALE = 724
+WINDOW = 128
+ALIGN = 32
 
 
 def extended_2(block, sides, width):
@@ -22,60 +28,168 @@
     return block
 
 
-def make_band(low_rel, weight, offsets):
-    near = jnp.where(low_rel[:, None] == offsets[None, :], weight[:, None], 0.0)
-    far = jnp.where(low_rel[:, None] + 1 == offsets[None, :], (1.0 - weight)[:, None], 0.0)
-    return near + far
+def split_two(value):
+    high = value.astype(jnp.bfloat16)
+    return high, (value - high.astype(jnp.float32)).astype(jnp.bfloat16)
+
+
+def window_starts(low):
+    return (jnp.min(low, axis=1, keepdims=True) // ALIGN) * ALIGN
+
+
+def one_hot(rel_row):
+    spots = lax.broadcasted_iota(jnp.int32, (WINDOW, rel_row.shape[1]), 0)
+    return jnp.where(spots == rel_row, 1.0, 0.0).astype(jnp.bfloat16)
+
+
+def project_kernel(group_ref, u_ref, low_ref, frac_ref, meas_ref, out_ref, rel_ref, w_ref, start_ref):
+    angles, planes, width = out_ref.shape
+    low = low_ref[...]
+    start = window_starts(low)
+    rel_ref[...] = low - start
+    w_ref[...] = frac_ref[...].astype(jnp.float32) * (1.0 / SCALE)
+    start_ref[...] = jnp.broadcast_to(start.astype(jnp.float32), (angles, WINDOW))
+    out_ref[...] = jnp.zeros_like(out_ref)
+    owned = meas_ref.shape[1]
+    out_ref[group_ref[0], :, WINDOW : WINDOW + owned] = meas_ref[...]
+    lane = lax.broadcasted_iota(jnp.int32, (planes, WINDOW), 1)
+
+    def body(a, carry):
+        band = one_hot(rel_ref[pl.ds(a, 1), :])
+        u = u_ref[...]
+        near = u * w_ref[pl.ds(a, 1), :]
+        near_hi, near_lo = split_two(near)
+        far_hi, far_lo = split_two(u - near)
+        terms = jnp.concatenate([near_hi, near_lo, far_hi, far_lo], axis=0)
+        sums = lax.dot_general(
+            terms, band, (((1,), (1,)), ((), ())), preferred_element_type=jnp.float32
+        )
+        at_low = sums[:planes] + sums[planes : 2 * planes]
+        above = sums[2 * planes : 3 * planes] + sums[3 * planes :]
+        piece = at_low + pltpu.roll(above, 1, 1)
+        out_ref[a, :, :WINDOW] = jnp.where(lane == WINDOW - 1, start_ref[pl.ds(a, 1), :], piece)
+        return carry
+
+    lax.fori_loop(0, angles, body, 0, unroll=2)
+
+
+def combine_kernel(factor, owned, got_ref, out_ref):
+    count = got_ref.shape[0]
+    step = WINDOW // ALIGN
+    rows = 16
+    got = got_ref[...]
+    lane_all = lax.broadcasted_iota(jnp.int32, (count, WINDOW), 1)
+    piece = jnp.where(lane_all < WINDOW - 1, got[:, :WINDOW], 0.0)
+    block = got[:, WINDOW - 1 : WINDOW].astype(jnp.int32) // ALIGN
+    slot = (block % step) * rows + block // step
+    slots = lax.broadcasted_iota(jnp.int32, (count, step * rows), 1)
+    route = jnp.where(slots == slot, 1.0, 0.0).astype(jnp.bfloat16)
+    sums = lax.dot_general(
+        route,
+        jnp.concatenate(split_two(piece), axis=1),
+        (((0,), (0,)), ((), ())),
+        preferred_element_type=jnp.float32,
+    )
+    sums = sums[:, :WINDOW] + sums[:, WINDOW:]
+    lane = lax.broadcasted_iota(jnp.int32, (rows, WINDOW), 1)
+    row = lax.broadcasted_iota(jnp.int32, (rows, WINDOW), 0)
+    sino = sums[:rows]
+    for m in range(1, step):
+        turned = pltpu.roll(sums[m * rows : (m + 1) * rows], m * ALIGN, 1)
+        here = lane >= m * ALIGN
+        sino = sino + jnp.where(here, turned, 0.0)
+        sino = sino + pltpu.roll(jnp.where(here, 0.0, turned), 1, 0)
+    taken = jnp.sum(got[:, WINDOW:].reshape(count // 16, 16, WINDOW), axis=0)
+    taken = jnp.where(lax.broadcasted_iota(jnp.int32, taken.shape, 1) < owned, taken, 0.0)
+    target = jnp.zeros_like(sino)
+    for i in range(16):
+        first, off = divmod(i * owned, WINDOW)
+        turned = taken[i : i + 1]
+        if off:
+            turned = pltpu.roll(turned, off, 1)
+        hit = ((row == first) & (lane >= off)) | ((row == first + 1) & (lane < off))
+        target = target + jnp.where(hit, turned, 0.0)
+    misfit = factor * sino - target
+    views = [misfit]
+    for m in range(1, step):
+        turned = pltpu.roll(misfit, WINDOW - m * ALIGN, 1)
+        views.append(
+            jnp.where(lane < WINDOW - m * ALIGN, turned, pltpu.roll(turned, rows - 1, 0))
+        )
+    views = jnp.concatenate(views, axis=0)
+    cut = jnp.dot(
+        route, jnp.concatenate(split_two(views), axis=1), preferred_element_type=jnp.float32
+    )
+    out_ref[...] = cut[:, :WINDOW] + cut[:, WINDOW:]
+
+
+def spread_kernel(factor, u_ref, low_ref, frac_ref, win_ref, out_ref, rel_ref, w_ref):
+    angles, planes, width = win_ref.shape
+    low = low_ref[...]
+    rel_ref[...] = low - window_starts(low)
+    w_ref[...] = frac_ref[...].astype(jnp.float32) * (1.0 / SCALE)
+
+    def body(a, total):
+        band = one_hot(rel_ref[pl.ds(a, 1), :])
+        at_low = win_ref[a]
+        above = pltpu.roll(at_low, WINDOW - 1, 1)
+        terms = jnp.concatenate(split_two(at_low) + split_two(above), axis=0)
+        picked = jnp.dot(terms, band, preferred_element_type=jnp.float32)
+        near = picked[:planes] + picked[planes : 2 * planes]
+        far = picked[2 * planes : 3 * planes] + picked[3 * planes :]
+        w = w_ref[pl.ds(a, 1), :]
+        return total + (far + w * (near - far))
+
+    total = lax.fori_loop(0, angles, body, jnp.zeros(u_ref.shape, jnp.float32), unroll=2)
+    out_ref[...] = u_ref[...] - factor * total
 
 
 def data_agent(volume, bin_index, bin_frac, measured, factor, sino_width):
     angles = bin_index.shape[0]
     planes = volume.shape[0] * volume.shape[1]
     current = volume.reshape(planes, -1)
-    bins_each = sino_width // angles
-    window = (bin_index.shape[1] + bin_index.shape[2] + 2 + 31) // 32 * 32
-    offsets = jnp.arange(window, dtype=jnp.int32)
-    lows = bin_index.reshape(angles, -1)
-    weight = bin_frac.reshape(angles, -1).astype(jnp.float32) / 724.0
-    starts = jnp.minimum(jnp.min(lows, axis=1), bins_each - window)
-    target = measured.reshape(planes, -1)
-    anchor = jnp.zeros((), jnp.int32)
-    highest = lax.Precision.HIGHEST
-
-    def place(piece, start):
-        return lax.dynamic_update_slice(
-            jnp.zeros((planes, bins_each), jnp.float32), piece, (anchor, start)
-        )
-
-    def project(carry, item):
-        low_a, weight_a, start = item
-        band = make_band(low_a - start, weight_a, offsets)
-        return (
-            carry,
-            jnp.dot(current, band, precision=highest, preferred_element_type=jnp.float32),
-        )
-
-    unused, windows = lax.scan(project, jnp.zeros((), jnp.float32), (lows, weight, starts))
-    partial_sino = jax.vmap(place, in_axes=(0, 0), out_axes=1)(windows, starts).reshape(planes, -1)
-    owned_bins = lax.psum_scatter(
-        factor * partial_sino, ("tile", "agent"), scatter_dimension=1, tiled=True
-    )
-    misfit = owned_bins - target
-    all_bins = lax.all_gather(misfit, ("tile", "agent"), axis=1, tiled=True)
-    by_angle = jnp.transpose(all_bins.reshape(planes, angles, bins_each), (1, 0, 2))
-
-    def spread(total, item):
-        low_a, weight_a, start, resid = item
-        band = make_band(low_a - start, weight_a, offsets)
-        picked = lax.dynamic_slice_in_dim(resid, start, window, 1)
-        return (
-            total + jnp.dot(picked, band.T, precision=highest, preferred_element_type=jnp.float32),
-            None,
-        )
-
-    back_sum, unused = lax.scan(spread, jnp.zeros_like(current), (lows, weight, starts, by_angle))
-    current = current - factor * back_sum
-    return current.reshape(volume.shape)
+    pixels = current.shape[1]
+    low = bin_index.reshape(angles, -1)
+    frac = bin_frac.reshape(angles, -1)
+    owned = measured.shape[2]
+    group = (lax.axis_index("tile") * lax.axis_size("agent") // planes).astype(jnp.int32)
+    vmem = pl.BlockSpec(memory_space=pltpu.VMEM)
+    pieces = pl.pallas_call(
+        project_kernel,
+        out_shape=jax.ShapeDtypeStruct((angles, planes, 2 * WINDOW), jnp.float32),
+        in_specs=[pl.BlockSpec(memory_space=pltpu.SMEM)] + [vmem] * 4,
+        out_specs=vmem,
+        scratch_shapes=[
+            pltpu.VMEM((angles, pixels), jnp.int32),
+            pltpu.VMEM((angles, pixels), jnp.float32),
+            pltpu.VMEM((angles, WINDOW), jnp.float32),
+        ],
+        name="project",
+    )(group.reshape(1), current, low, frac, measured.reshape(planes, owned))
+    both = ("tile", "agent")
+    got = lax.all_to_all(
+        pieces.reshape(angles * planes, 2 * WINDOW), both, 0, 0, tiled=True
+    )
+    cut = pl.pallas_call(
+        functools.partial(combine_kernel, factor, owned),
+        out_shape=jax.ShapeDtypeStruct((angles * planes, WINDOW), jnp.float32),
+        in_specs=[vmem],
+        out_specs=vmem,
+        name="combine",
+    )(got)
+    back = lax.all_to_all(cut, both, 0, 0, tiled=True)
+    fit = pl.pallas_call(
+        functools.partial(spread_kernel, factor),
+        out_shape=jax.ShapeDtypeStruct((planes, pixels), jnp.float32),
+        in_specs=[vmem] * 4,
+        out_specs=vmem,
+        scratch_shapes=[
+            pltpu.VMEM((angles, pixels), jnp.int32),
+            pltpu.VMEM((angles, pixels), jnp.float32),
+        ],
+        name="spread",
+    )(current, low, frac, back.reshape(angles, planes, WINDOW))
+    return fit.reshape(volume.shape)
 
 
 def in_plane(extended, shift, apply_net):

time: 1250 us -> 186 us (0.15)
  waiting for transfers between devices: 900 us -> 19.9 us
  other arithmetic: 99.9 us -> 3.1 us
  local copies, waits for them, and re-layouts: 84.5 us -> 23.4 us
  matrix products: 49.2 us -> 7.96 us
  blocking collectives: 41.4 us -> 78.5 us
  loops' own time: 33 us -> 0 us
    all_gather x1 -> x0, waiting for transfers between devices: 701 us -> none  [data_agent(): all_bins = lax.all_gather(misfit, ('tile', 'agent'), axis=1, tiled=True)]
    unnamed x6 -> x3, waiting for transfers between devices: 195 us -> 0.05 us
    scatter x33 -> x0, other arithmetic: 72.1 us -> none
    dot_general x32 -> x0, matrix products: 41.3 us -> none  [the longest x16 27 us: spread(): jnp.dot(picked, band.T, precision=highest, preferred_element_type=jnp.flo...]
    all_to_all x0 -> x1, blocking collectives: none -> 40.7 us  [data_agent(): lax.all_to_all(pieces.reshape(angles * planes, 2 * WINDOW), both, 0, 0, t...]
    scatter x48 -> x0, local copies, waits for them, and re-layouts: 35.8 us -> none
    another operation x3 -> x0, loops' own time: 33 us -> none  [the longest x1 32.2 us: data_agent(): lax.scan(spread, jnp.zeros_like(current), (lows, weight, starts, by_angle))]
    dynamic_slice x81 -> x0, local copies, waits for them, and re-layouts: 22 us -> none  [the longest x64 20.3 us: data_agent(): lax.scan(project, jnp.zeros((), jnp.float32), (lows, weight, starts))]
  transfers between devices with their start and end apart: 9 -> 8, of which waited for: 4 -> 5; matrix products, arithmetic and copies ran while one was open for 14% -> 12% of each run, Pallas kernels for 0% -> 6%
where the time goes in v1:
time: 186 us
  blocking collectives  78.5 us (42%)
  between operations  25.3 us (14%)
  local copies, waits for them, and re-layouts  23.4 us (13%)
  waiting for transfers between devices  19.9 us (11%)
  starting transfers between devices  16.1 us (9%)
  Pallas kernels  11.3 us (6%)
  matrix products  7.96 us (4%)
  other arithmetic  3.1 us (2%)
    all_to_all x1, blocking collectives, data_agent(): lax.all_to_all(pieces.reshape(angles * planes, 2 * WINDOW), both, 0, 0, t...  40.7 us
    all_gather x3, blocking collectives, apply_net(): lax.all_gather(patches, 'agent', axis=0, tiled=True)  37.8 us
    dot_general x3, matrix products, apply_net(): jnp.dot(hidden, down_weight[which], preferred_element_type=jnp.float32)  7.96 us
    ppermute x2, waiting for transfers between devices, extended_2(): lax.ppermute(lax.slice_in_dim(block, block.shape[dim] - width, None, axis...  6.81 us
    ppermute x2, waiting for transfers between devices, extended_2(): lax.ppermute(lax.slice_in_dim(block, 0, width, axis=dim), axis, backward)  6.54 us
    ppermute x2, starting transfers between devices, extended_2(): lax.ppermute(lax.slice_in_dim(block, block.shape[dim] - width, None, axis...  6.45 us
    all_to_all x1, waiting for transfers between devices, data_agent(): back = lax.all_to_all(cut, both, 0, 0, tiled=True)  6.45 us
    all_to_all x1, starting transfers between devices, data_agent(): back = lax.all_to_all(cut, both, 0, 0, tiled=True)  6.18 us
  transfers between devices with their start and end apart: 8, of which 5 were waited for; matrix products, arithmetic and copies ran while one was open for 12% of the time, Pallas kernels for 6%

profile of v1, /device:TPU:1, one launch (start us, length us, event | category | flops | bytes accessed | tf_op | source)
XLA Modules:
  0.0 185.6 jit_solution(12517743234273851996)
XLA Ops:
  7.2 1.0 slice.113
  8.2 3.1 %collective-permute-start = (bf16[3,1,16,16,64]{4,3,2,1,0:T(8,128)(2,1)S(1)}, bf16[3,1,16,16,64]{4,3,2,1,0:T(8,128)(2,1)S(1)}, u32[]{:S(2)}, u32[]{:S(2)}) collective-permute-start(bf16[3,1,16,16,64]{4,3,2,1,0:T(8,128)(2,1)S(1)} %slice.113), channel_id=1, source_target_pairs={{0,4},{4,8},{8,12},{12,16},{16,20},{20,24},{24,28},{28,32},{32,36}... | collective-permute-start | bytes 294920 | tf_op jit(solution)/shard_map/ppermute | solution.py:23
  11.3 0.3 collective-permute-start.1
  11.6 2.3 %collective-permute-done = bf16[3,1,16,16,64]{4,3,2,1,0:T(8,128)(2,1)S(1)} collective-permute-done((bf16[3,1,16,16,64]{4,3,2,1,0:T(8,128)(2,1)S(1)}, bf16[3,1,16,16,64]{4,3,2,1,0:T(8,128)(2,1)S(1)}, u32[]{:S(2)}, u32[]{:S(2)}) %collective-permute-start) | collective-permute-done | bytes 98336 | tf_op jit(solution)/shard_map/ppermute | solution.py:23
  13.9 3.3 %collective-permute-done.1 = bf16[3,1,16,16,64]{4,3,2,1,0:T(8,128)(2,1)S(1)} collective-permute-done((bf16[3,1,16,16,64]{4,3,2,1,0:T(8,128)(2,1)S(1)}, bf16[3,1,16,16,64]{4,3,2,1,0:T(8,128)(2,1)S(1)}, u32[]{:S(2)}, u32[]{:S(2)}) %collective-permute-start.1) | collective-permute-done | bytes 98336 | tf_op jit(solution)/shard_map/ppermute | solution.py:26
  17.2 0.1 pad_maximum_fusion
  17.4 0.2 fusion.32
  17.6 0.2 copy.48
  17.9 3.4 %collective-permute-start.2 = (bf16[3,1,16,48,16]{3,4,2,1,0:T(8,128)(2,1)S(1)}, bf16[3,1,16,48,16]{3,4,2,1,0:T(8,128)(2,1)S(1)}, u32[]{:S(2)}, u32[]{:S(2)}) collective-permute-start(bf16[3,1,16,48,16]{3,4,2,1,0:T(8,128)(2,1)S(1)} %copy.48), channel_id=1, source_target_pairs={{0,1},{1,2},{2,3},{3,0},{4,5},{5,6},{6,7},{7,4},{8,9},{9,10},{10,1... | collective-permute-start | bytes 221192 | tf_op jit(solution)/shard_map/ppermute | solution.py:23
  21.2 0.2 copy.49
  21.4 3.1 %collective-permute-start.3 = (bf16[3,1,16,48,16]{3,4,2,1,0:T(8,128)(2,1)S(1)}, bf16[3,1,16,48,16]{3,4,2,1,0:T(8,128)(2,1)S(1)}, u32[]{:S(2)}, u32[]{:S(2)}) collective-permute-start(bf16[3,1,16,48,16]{3,4,2,1,0:T(8,128)(2,1)S(1)} %copy.49), channel_id=1, source_target_pairs={{1,0},{2,1},{3,2},{0,3},{5,4},{6,5},{7,6},{4,7},{9,8},{10,9},{11,1... | collective-permute-start | bytes 221192 | tf_op jit(solution)/shard_map/ppermute | solution.py:26
  24.6 0.6 fusion.34
  27.1 4.5 %collective-permute-done.2 = bf16[3,1,16,48,16]{3,4,2,1,0:T(8,128)(2,1)S(1)} collective-permute-done((bf16[3,1,16,48,16]{3,4,2,1,0:T(8,128)(2,1)S(1)}, bf16[3,1,16,48,16]{3,4,2,1,0:T(8,128)(2,1)S(1)}, u32[]{:S(2)}, u32[]{:S(2)}) %collective-permute-start.2) | collective-permute-done | bytes 73760 | tf_op jit(solution)/shard_map/ppermute | solution.py:23
  31.6 0.3 copy.50
  31.9 3.2 %collective-permute-done.3 = bf16[3,1,16,48,16]{3,4,2,1,0:T(8,128)(2,1)S(1)} collective-permute-done((bf16[3,1,16,48,16]{3,4,2,1,0:T(8,128)(2,1)S(1)}, bf16[3,1,16,48,16]{3,4,2,1,0:T(8,128)(2,1)S(1)}, u32[]{:S(2)}, u32[]{:S(2)}) %collective-permute-start.3) | collective-permute-done | bytes 73760 | tf_op jit(solution)/shard_map/ppermute | solution.py:26
  35.1 0.3 copy.51
  35.4 0.5 pad_maximum_fusion.1
  36.1 0.3 reshape.160
  36.4 0.3 copy.58
  36.7 0.3 reshape.161
  36.9 12.0 %all_gather.11 = bf16[320,256]{1,0:T(8,128)(2,1)S(1)} all-gather(bf16[80,256]{1,0:T(8,128)(2,1)S(1)} %reshape.161), channel_id=1, replica_groups=mesh['tile'=64,'agent'=4] {'agent'}, dimensions={0}, use_global_device_ids=true | all-gather | bytes 204800 | tf_op jit(solution)/shard_map/all_gather | solution.py:273
  48.9 2.4 %fusion.4 = f32[320,256]{1,0:T(8,128)} fusion(bf16[320,256]{1,0:T(8,128)(2,1)S(1)} %all_gather.11, bf16[3,1024,256]{2,1,0:T(8,128)(2,1)S(1)} %copy-done.6, bf16[3,256,1024]{2,1,0:T(8,128)(2,1)} %param.14), kind=kOutput, calls=%fused_computation.7 | convolution fusion | flops 336199680 | bytes 1540096 | tf_op jit(solution)/shard_map/dot_general | solution.py:278
  53.2 0.1 constant_dynamic-slice_fusion.1
  53.5 0.1 reshape.157
  53.6 13.9 %all_gather.10 = bf16[512,256]{0,1:T(8,128)(2,1)S(1)} all-gather(bf16[128,256]{0,1:T(8,128)(2,1)S(1)} %reshape.157), channel_id=1, replica_groups=mesh['tile'=64,'agent'=4] {'agent'}, dimensions={0}, use_global_device_ids=true | all-gather | bytes 327680 | tf_op jit(solution)/shard_map/all_gather | solution.py:273
  67.5 2.7 %fusion.1 = f32[512,256]{1,0:T(8,128)} fusion(bf16[512,256]{0,1:T(8,128)(2,1)S(1)} %all_gather.10, bf16[3,1024,256]{2,1,0:T(8,128)(2,1)S(1)} %copy-done.6, bf16[3,256,1024]{2,1,0:T(8,128)(2,1)} %param.14), kind=kOutput, calls=%fused_computation.4 | convolution fusion | flops 537919488 | bytes 1835008 | tf_op jit(solution)/shard_map/dot_general | solution.py:278
  73.3 0.1 constant_dynamic-slice_fusion.2
  73.5 0.2 copy.52
  73.7 0.3 reshape.152
  74.0 2.2 %copy.53 = bf16[1,16,2,5,16,16]{5,4,3,2,1,0:T(8,128)(2,1)S(1)} copy(bf16[1,16,2,5,16,16]{4,2,5,3,1,0:T(2,128)(2,1)S(1)} %bitcast.86) | data formatting | bytes 163840 | tf_op jit(solution)/shard_map/transpose | solution.py:205
  76.1 0.6 reshape.153
  76.7 12.0 %all_gather.9 = bf16[640,256]{1,0:T(8,128)(2,1)S(1)} all-gather(bf16[160,256]{1,0:T(8,128)(2,1)S(1)} %reshape.153), channel_id=1, replica_groups=mesh['tile'=64,'agent'=4] {'agent'}, dimensions={0}, use_global_device_ids=true | all-gather | bytes 409600 | tf_op jit(solution)/shard_map/all_gather | solution.py:273
  88.7 2.9 %fusion = f32[640,256]{1,0:T(8,128)} fusion(bf16[640,256]{1,0:T(8,128)(2,1)S(1)} %all_gather.9, bf16[3,1024,256]{2,1,0:T(8,128)(2,1)S(1)} %copy-done.6, bf16[3,256,1024]{2,1,0:T(8,128)(2,1)} %param.14), kind=kOutput, calls=%fused_computation.2 | convolution fusion | flops 672399360 | bytes 2031616 | tf_op jit(solution)/shard_map/dot_general | solution.py:278
  91.7 0.7 reshape_squeeze.3.u_ref
  92.4 0.7 reshape.147.low_ref
  93.1 0.7 reshape.148.frac_ref
  93.8 4.8 %project.1 = f32[16,16,256]{2,1,0:T(8,128)} custom-call(s32[1]{0:T(128)} %bitcast.group_ref, f32[16,1024]{1,0:T(8,128)} %reshape_squeeze.3.u_ref, s32[16,1024]{1,0:T(8,128)} %reshape.147.low_ref, s32[16,1024]{1,0:T(8,128)} %reshape.148.frac_ref, f32[16,88]{1,0:T(8,128)} %bitcast.95), custom_call_target="tpu_custom_call" | custom-call | tf_op jit(solution)/shard_map/project/pallas_call | solution.py:157
  98.7 1.2 copy.45
  99.9 40.7 %all_to_all.20 = f32[256,1,256]{2,1,0:T(1,128)S(1)} all-to-all(f32[256,1,256]{2,1,0:T(1,128)S(1)} %copy.45), channel_id=1, replica_groups=mesh['tile'=64,'agent'=4] {'tile','agent'}, dimensions={0} | all-to-all | bytes 524288 | tf_op jit(solution)/shard_map/all_to_all | solution.py:170
  140.6 0.7 copy.66
  141.3 2.4 %combine.1 = f32[256,128]{1,0:T(8,128)} custom-call(f32[256,256]{1,0:T(8,128)} %bitcast.89), custom_call_target="tpu_custom_call" | custom-call | tf_op jit(solution)/shard_map/combine/pallas_call | solution.py:173
  143.7 6.2 %all-to-all-start.1 = ((f32[256,1,128]{2,1,0:T(1,128)}), f32[256,1,128]{2,1,0:T(1,128)S(1)}, u32[]{:S(2)}, u32[]{:S(2)}) async-start(f32[256,1,128]{2,1,0:T(1,128)} %bitcast.93), calls=%async_computation.1 | async-start | bytes 262144 | tf_op jit(solution)/shard_map/all_to_all | solution.py:180
  154.3 1.0 copy.62
  155.3 0.6 reduce_sum.18
  155.8 0.5 broadcast_divide_fusion
  156.4 6.4 %all-to-all-done.1 = f32[256,1,128]{2,1,0:T(1,128)S(1)} async-done(((f32[256,1,128]{2,1,0:T(1,128)}), f32[256,1,128]{2,1,0:T(1,128)S(1)}, u32[]{:S(2)}, u32[]{:S(2)}) %all-to-all-start.1) | async-done | bytes 131104 | tf_op jit(solution)/shard_map/all_to_all | solution.py:180
  162.8 0.7 copy-done.2
  163.5 4.1 %spread.1 = f32[16,1024]{1,0:T(8,128)} custom-call(f32[16,1024]{1,0:T(8,128)} %reshape_squeeze.3.u_ref, s32[16,1024]{1,0:T(8,128)} %reshape.147.low_ref, s32[16,1024]{1,0:T(8,128)} %reshape.148.frac_ref, f32[16,16,128]{2,1,0:T(8,128)} %bitcast.92), custom_call_target="tpu_custom_call" | custom-call | tf_op jit(solution)/shard_map/spread/pallas_call | solution.py:181
  167.6 0.9 stack.14
  168.5 1.6 reshape.164
  170.1 1.1 reshape.162
  171.2 0.3 copy.65
  171.5 0.2 reshape.163
  171.7 1.0 copy.56
  172.7 0.2 reshape.158
  173.0 0.1 fusion.27
  173.1 1.3 reshape.154
  174.4 2.3 %copy.54 = f32[1,16,2,5,16,16]{4,2,5,3,1,0:T(2,128)S(1)} copy(f32[1,16,2,5,16,16]{5,4,3,2,1,0:T(8,128)S(1)} %reshape.154) | data formatting | bytes 327680 | tf_op jit(solution)/shard_map/reshape | solution.py:207
  176.7 0.7 reshape.155
  177.4 0.3 copy-done.1
  177.7 0.2 fusion.16
  177.9 0.2 copy.60
  178.1 0.1 multiply_reduce_fusion
  178.2 0.9 add_subtract_fusion
  (28 shorter events, 0.5 us)
Async XLA Ops:
  7.2 162.9 %reduce-scatter.8.cloned.1.call-start = ((), (), s32[]{:S(2)}) async-start(), calls=%async_computation.7 | async-start | bytes 409600 | tf_op jit(solution)/shard_map/reduce_scatter | solution.py:279
  8.2 5.7 %collective-permute-start = (bf16[3,1,16,16,64]{4,3,2,1,0:T(8,128)(2,1)S(1)}, bf16[3,1,16,16,64]{4,3,2,1,0:T(8,128)(2,1)S(1)}, u32[]{:S(2)}, u32[]{:S(2)}) collective-permute-start(bf16[3,1,16,16,64]{4,3,2,1,0:T(8,128)(2,1)S(1)} %slice.113), channel_id=1, source_target_pairs={{0,4},{4,8},{8,12},{12,16},{16,20},{20,24},{24,28},{28,32},{32,36}... | collective-permute-start | bytes 294920 | tf_op jit(solution)/shard_map/ppermute | solution.py:23
  11.3 5.9 %collective-permute-start.1 = (bf16[3,1,16,16,64]{4,3,2,1,0:T(8,128)(2,1)S(1)}, bf16[3,1,16,16,64]{4,3,2,1,0:T(8,128)(2,1)S(1)}, u32[]{:S(2)}, u32[]{:S(2)}) collective-permute-start(bf16[3,1,16,16,64]{4,3,2,1,0:T(8,128)(2,1)S(1)} %slice.113), channel_id=1, source_target_pairs={{4,0},{8,4},{12,8},{16,12},{20,16},{24,20},{28,24},{32,28},{36,32}... | collective-permute-start | bytes 294920 | tf_op jit(solution)/shard_map/ppermute | solution.py:26
  17.4 7.2 %copy-start.5 = (s32[3]{0:T(128)S(1)}, s32[3]{0:T(128)}, u32[]{:S(2)}) copy-start(s32[3]{0:T(128)} %param.12) | copy-start | bytes 40
  17.9 13.7 %collective-permute-start.2 = (bf16[3,1,16,48,16]{3,4,2,1,0:T(8,128)(2,1)S(1)}, bf16[3,1,16,48,16]{3,4,2,1,0:T(8,128)(2,1)S(1)}, u32[]{:S(2)}, u32[]{:S(2)}) collective-permute-start(bf16[3,1,16,48,16]{3,4,2,1,0:T(8,128)(2,1)S(1)} %copy.48), channel_id=1, source_target_pairs={{0,1},{1,2},{2,3},{3,0},{4,5},{5,6},{6,7},{7,4},{8,9},{9,10},{10,1... | collective-permute-start | bytes 221192 | tf_op jit(solution)/shard_map/ppermute | solution.py:23
  21.4 13.7 %collective-permute-start.3 = (bf16[3,1,16,48,16]{3,4,2,1,0:T(8,128)(2,1)S(1)}, bf16[3,1,16,48,16]{3,4,2,1,0:T(8,128)(2,1)S(1)}, u32[]{:S(2)}, u32[]{:S(2)}) collective-permute-start(bf16[3,1,16,48,16]{3,4,2,1,0:T(8,128)(2,1)S(1)} %copy.49), channel_id=1, source_target_pairs={{1,0},{2,1},{3,2},{0,3},{5,4},{6,5},{7,6},{4,7},{9,8},{10,9},{11,1... | collective-permute-start | bytes 221192 | tf_op jit(solution)/shard_map/ppermute | solution.py:26
  36.0 12.9 %copy-start.6 = (bf16[3,1024,256]{2,1,0:T(8,128)(2,1)S(1)}, bf16[3,1024,256]{2,1,0:T(8,128)(2,1)}, u32[]{:S(2)}) copy-start(bf16[3,1024,256]{2,1,0:T(8,128)(2,1)} %param.15) | copy-start | bytes 4718596
  51.3 120.4 %reduce-scatter.6.cloned.1.call-start = ((), (), s32[]{:S(2)}) async-start(), calls=%async_computation.6 | async-start | bytes 655360 | tf_op jit(solution)/shard_map/reduce_scatter | solution.py:279
  70.2 102.9 %reduce-scatter.4.cloned.1.call-start = ((), (), s32[]{:S(2)}) async-start(), calls=%async_computation.5 | async-start | bytes 819200 | tf_op jit(solution)/shard_map/reduce_scatter | solution.py:279
  88.7 3.0 %copy-start = (f32[4,1,16,16,64]{4,3,2,1,0:T(8,128)S(1)}, f32[4,1,16,16,64]{4,3,2,1,0:T(8,128)}, u32[]{:S(2)}) copy-start(f32[4,1,16,16,64]{4,3,2,1,0:T(8,128)} %param.8) | copy-start | bytes 786436
  88.7 3.7 %copy-start.3 = (s32[16,16,64]{2,1,0:T(8,128)S(1)}, s32[16,16,64]{2,1,0:T(8,128)}, u32[]{:S(2)}) copy-start(s32[16,16,64]{2,1,0:T(8,128)} %param.10) | copy-start | bytes 196612
  91.6 1.5 copy-start.4
  98.7 56.6 %copy-start.7 = (f32[4]{0:T(128)S(1)}, f32[4]{0:T(128)}, u32[]{:S(2)}) copy-start(f32[4]{0:T(128)} %param.13) | copy-start | bytes 52
  143.7 19.1 %all-to-all-start.1 = ((f32[256,1,128]{2,1,0:T(1,128)}), f32[256,1,128]{2,1,0:T(1,128)S(1)}, u32[]{:S(2)}, u32[]{:S(2)}) async-start(f32[256,1,128]{2,1,0:T(1,128)} %bitcast.93), calls=%async_computation.1 | async-start | bytes 262144 | tf_op jit(solution)/shard_map/all_to_all | solution.py:180
  162.8 0.7 copy-start.2
  176.7 1.0 copy-start.1
Sparse Core Ops, SparseCore 0:
  51.4 25.9 reduce-scatter.7
  80.5 26.5 reduce-scatter.5
  109.6 32.8 reduce-scatter.3

commit v2 on v1

v2 whole, which is shorter than its diff:
```python
import functools
import math

import jax
import jax.numpy as jnp
from jax import lax
from jax.experimental import pallas as pl
from jax.experimental.pallas import tpu as pltpu
from jax.sharding import PartitionSpec as P

PATCH = 16
SCALE = 724
WINDOW = 128
ALIGN = 32


def split_two(value):
    high = value.astype(jnp.bfloat16)
    return high, (value - high.astype(jnp.float32)).astype(jnp.bfloat16)


def window_starts(low):
    return (jnp.min(low, axis=1, keepdims=True) // ALIGN) * ALIGN


def one_hot(rel_row):
    spots = lax.broadcasted_iota(jnp.int32, (WINDOW, rel_row.shape[1]), 0)
    return jnp.where(spots == rel_row, 1.0, 0.0).astype(jnp.bfloat16)


def project_kernel(
    group_ref, state_ref, bin_ref, num_ref, meas_ref, out_ref, u_ref, rel_ref, w_ref, start_ref
):
    angles, planes, _ = out_ref.shape
    cols = bin_ref.shape[2]
    for x in range(bin_ref.shape[1]):
        span = slice(x * cols, (x + 1) * cols)
        u_ref[:, span] = state_ref[0, 0, :, x, :]
        rel_ref[:, span] = bin_ref[:, x, :]
        w_ref[:, span] = num_ref[:, x, :].astype(jnp.float32) * (1.0 / SCALE)
    low = rel_ref[...]
    start = window_starts(low)
    rel_ref[...] = low - start
    start_ref[...] = jnp.broadcast_to(start.astype(jnp.float32), (angles, WINDOW))
    out_ref[...] = jnp.zeros_like(out_ref)
    owned = meas_ref.shape[2]
    out_ref[group_ref[0], :, WINDOW : WINDOW + owned] = meas_ref[0]
    lane = lax.broadcasted_iota(jnp.int32, (planes, WINDOW), 1)

    def body(a, carry):
        band = one_hot(rel_ref[pl.ds(a, 1), :])
        u = u_ref[...]
        near = u * w_ref[pl.ds(a, 1), :]
        near_hi, near_lo = split_two(near)
        far_hi, far_lo = split_two(u - near)
        terms = jnp.concatenate([near_hi, near_lo, far_hi, far_lo], axis=0)
        sums = lax.dot_general(
            terms, band, (((1,), (1,)), ((), ())), preferred_element_type=jnp.float32
        )
        at_low = sums[:planes] + sums[planes : 2 * planes]
        above = sums[2 * planes : 3 * planes] + sums[3 * planes :]
        piece = at_low + pltpu.roll(above, 1, 1)
        out_ref[a, :, :WINDOW] = jnp.where(lane == WINDOW - 1, start_ref[pl.ds(a, 1), :], piece)
        return carry

    lax.fori_loop(0, angles, body, 0, unroll=2)


def combine_kernel(factor, owned, got_ref, out_ref):
    count = got_ref.shape[0]
    step = WINDOW // ALIGN
    rows = 16
    got = got_ref[...]
    lane_all = lax.broadcasted_iota(jnp.int32, (count, WINDOW), 1)
    piece = jnp.where(lane_all < WINDOW - 1, got[:, :WINDOW], 0.0)
    block = got[:, WINDOW - 1 : WINDOW].astype(jnp.int32) // ALIGN
    slot = (block % step) * rows + block // step
    slots = lax.broadcasted_iota(jnp.int32, (count, step * rows), 1)
    route = jnp.where(slots == slot, 1.0, 0.0).astype(jnp.bfloat16)
    sums = lax.dot_general(
        route,
        jnp.concatenate(split_two(piece), axis=1),
        (((0,), (0,)), ((), ())),
        preferred_element_type=jnp.float32,
    )
    sums = sums[:, :WINDOW] + sums[:, WINDOW:]
    lane = lax.broadcasted_iota(jnp.int32, (rows, WINDOW), 1)
    row = lax.broadcasted_iota(jnp.int32, (rows, WINDOW), 0)
    sino = sums[:rows]
    for m in range(1, step):
        turned = pltpu.roll(sums[m * rows : (m + 1) * rows], m * ALIGN, 1)
        here = lane >= m * ALIGN
        sino = sino + jnp.where(here, turned, 0.0)
        sino = sino + pltpu.roll(jnp.where(here, 0.0, turned), 1, 0)
    taken = jnp.sum(got[:, WINDOW:].reshape(count // 16, 16, WINDOW), axis=0)
    taken = jnp.where(lax.broadcasted_iota(jnp.int32, taken.shape, 1) < owned, taken, 0.0)
    target = jnp.zeros_like(sino)
    for i in range(16):
        first, off = divmod(i * owned, WINDOW)
        turned = taken[i : i + 1]
        if off:
            turned = pltpu.roll(turned, off, 1)
        hit = ((row == first) & (lane >= off)) | ((row == first + 1) & (lane < off))
        target = target + jnp.where(hit, turned, 0.0)
    misfit = factor * sino - target
    views = [misfit]
    for m in range(1, step):
        turned = pltpu.roll(misfit, WINDOW - m * ALIGN, 1)
        views.append(
            jnp.where(lane < WINDOW - m * ALIGN, turned, pltpu.roll(turned, rows - 1, 0))
        )
    views = jnp.concatenate(views, axis=0)
    cut = jnp.dot(
        route, jnp.concatenate(split_two(views), axis=1), preferred_element_type=jnp.float32
    )
    out_ref[...] = cut[:, :WINDOW] + cut[:, WINDOW:]


def shift_kernel(offset_ref, own_ref, next_ref, out_ref):
    rows = own_ref.shape[2]
    for k in range(2):
        o = offset_ref[k]
        own = pltpu.roll(own_ref[k].astype(jnp.float32), rows - o, 1)
        more = pltpu.roll(next_ref[k].astype(jnp.float32), rows - o, 1)
        row = lax.broadcasted_iota(jnp.int32, own.shape, 1)
        out_ref[k] = jnp.where(row < rows - o, own, more).astype(out_ref.dtype)
    out_ref[2] = own_ref[2]


def swap_slabs(slabs):
    lane = lax.broadcasted_iota(jnp.int32, slabs[0].shape, 1)
    width = slabs[0].shape[1]
    slabs = list(slabs)
    for step in (1, 2, 4, 8):
        odd = (lane & step) != 0
        for i in range(len(slabs)):
            if i & step:
                continue
            first, second = slabs[i], slabs[i + step]
            slabs[i] = jnp.where(odd, pltpu.roll(second, step, 1), first)
            slabs[i + step] = jnp.where(odd, second, pltpu.roll(first, width - step, 1))
    return slabs


def swap_rows(slab):
    width = slab.shape[1]
    top, low = slab[:8], slab[8:]
    lane = lax.broadcasted_iota(jnp.int32, top.shape, 1)
    row = lax.broadcasted_iota(jnp.int32, top.shape, 0)
    odd = (lane & 8) != 0
    top, low = (
        jnp.where(odd, pltpu.roll(low, 8, 1), top),
        jnp.where(odd, low, pltpu.roll(top, width - 8, 1)),
    )
    halves = []
    for half in (top, low):
        for step in (1, 2, 4):
            odd_lane, odd_row = (lane & step) != 0, (row & step) != 0
            up = pltpu.roll(pltpu.roll(half, 8 - step, 0), step, 1)
            down = pltpu.roll(pltpu.roll(half, step, 0), width - step, 1)
            other = jnp.where(odd_lane, up, down)
            half = jnp.where(odd_lane == odd_row, half, other)
        halves.append(half)
    return jnp.concatenate(halves, axis=0)


def denoise_kernel(offset_ref, p0, p1, p2, p3, up_ref, down_ref, o0, o1, o2, o3):
    side = PATCH
    size = side * side
    row = lax.broadcasted_iota(jnp.int32, (size, size), 0)
    col = lax.broadcasted_iota(jnp.int32, (size, size), 1)
    turned = (row % side) * side + row // side
    exchange = jnp.where(col == turned, 1.0, 0.0).astype(jnp.bfloat16)
    lane = lax.broadcasted_iota(jnp.int32, (size // 2, WINDOW), 1)
    left = lane < WINDOW // 2
    wide = lax.broadcasted_iota(jnp.int32, (size, WINDOW), 1)

    def joined(a, b):
        a = a.reshape(size // 2, WINDOW).astype(jnp.float32)
        b = b.reshape(size // 2, WINDOW).astype(jnp.float32)
        early = jnp.where(left, a, pltpu.roll(b, WINDOW // 2, 1))
        late = jnp.where(left, pltpu.roll(a, WINDOW // 2, 1), b)
        return jnp.concatenate([early, late], axis=0)

    def slabs_of(half):
        return [half[i * side : (i + 1) * side] for i in range(side)]

    def arrange(which, half):
        if which == 0:
            return jnp.concatenate(swap_slabs(slabs_of(half)), axis=0)
        if which == 2:
            return jnp.concatenate([swap_rows(slab) for slab in slabs_of(half)], axis=0)
        return half

    for k in range(3):
        halves = [joined(p0[k], p1[k]), joined(p2[k], p3[k])]
        if k != 1:
            o = offset_ref[k]
            a, b = [pltpu.roll(half, WINDOW - o, 1) for half in halves]
            inside = wide < WINDOW - o
            halves = [jnp.where(inside, a, b), jnp.where(inside, b, a)]
        halves = [arrange(k, half) for half in halves]
        patches = jnp.concatenate([half.T for half in halves], axis=0).astype(jnp.bfloat16)
        down = down_ref[k]
        if k == 0:
            patches = jnp.dot(
                patches, exchange, preferred_element_type=jnp.float32
            ).astype(jnp.bfloat16)
            down = jnp.dot(down, exchange, preferred_element_type=jnp.float32).astype(jnp.bfloat16)
        hidden = jnp.dot(patches, up_ref[k], preferred_element_type=jnp.float32)
        hidden = jnp.maximum(hidden, 0.0).astype(jnp.bfloat16)
        result = jnp.dot(hidden, down, preferred_element_type=jnp.float32)
        halves = [arrange(k, result[:WINDOW].T), arrange(k, result[WINDOW:].T)]
        if k != 1:
            a, b = [pltpu.roll(half, o, 1) for half in halves]
            inside = wide >= o
            halves = [jnp.where(inside, a, b), jnp.where(inside, b, a)]
        for half, first, second in ((halves[0], o0, o1), (halves[1], o2, o3)):
            early, late = half[: size // 2], half[size // 2 :]
            first[k] = jnp.where(left, early, pltpu.roll(late, WINDOW // 2, 1)).reshape(
                first.shape[1:]
            )
            second[k] = jnp.where(left, pltpu.roll(early, WINDOW // 2, 1), late).reshape(
                second.shape[1:]
            )


def finish_kernel(
    factor, offset_ref, weight_ref, state_ref, u_ref, rel_ref, w_ref, win_ref, net_ref, prev_ref,
    next_ref, fit_ref,
):
    angles, planes, _ = win_ref.shape

    def body(a, total):
        band = one_hot(rel_ref[pl.ds(a, 1), :])
        at_low = win_ref[a]
        above = pltpu.roll(at_low, WINDOW - 1, 1)
        terms = jnp.concatenate(split_two(at_low) + split_two(above), axis=0)
        picked = jnp.dot(terms, band, preferred_element_type=jnp.float32)
        near = picked[:planes] + picked[planes : 2 * planes]
        far = picked[2 * planes : 3 * planes] + picked[3 * planes :]
        w = w_ref[pl.ds(a, 1), :]
        return total + (far + w * (near - far))

    total = lax.fori_loop(0, angles, body, jnp.zeros(u_ref.shape, jnp.float32), unroll=2)
    fit = u_ref[...] - factor * total
    rows, cols = fit_ref.shape[2:]
    for x in range(rows):
        fit_ref[0, :, x, :] = fit[:, x * cols : (x + 1) * cols]

    raw = [jnp.full((1, cols), weight_ref[i], jnp.float32) for i in range(4)]
    whole = raw[0] + raw[1] + raw[2] + raw[3]
    share = [value / whole for value in raw]
    row = lax.broadcasted_iota(jnp.int32, net_ref.shape[1:], 1)
    nets = []
    for k in range(3):
        net = net_ref[k]
        if k < 2:
            o = offset_ref[k]
            net = jnp.where(row >= o, pltpu.roll(net, o, 1), pltpu.roll(prev_ref[k], o, 1))
        nets.append((net[:, :, :cols], pltpu.roll(net, WINDOW - cols, 2)[:, :, :cols]))
    count = planes // 2
    for part in range(2):
        span = slice(part * count, (part + 1) * count)
        held = state_ref[0, 0, span]
        answer = fit_ref[0, span]
        joined = share[0] * (2.0 * answer - held)
        for k in range(3):
            joined = joined + share[k + 1] * (state_ref[k + 1, 0, span] - 2.0 * nets[k][part])
        next_ref[0, 0, span] = held + joined - answer
        for k in range(3):
            next_ref[k + 1, 0, span] = joined + nets[k][part]


VMEM = pl.BlockSpec(memory_space=pltpu.VMEM)
SMEM = pl.BlockSpec(memory_space=pltpu.SMEM)


def hop(value, axis, step):
    count = lax.axis_size(axis)
    return lax.ppermute(value, axis, [(i, (i + step) % count) for i in range(count)])


def shards(
    agent_state, measured, bin_index, bin_frac, patch_offsets, agent_weights, up_weight, down_weight
):
    planes, row_count, col_count = agent_state.shape[2:]
    tile_count = lax.axis_size("tile")
    agent_count = lax.axis_size("agent")
    angles = bin_index.shape[0]
    pixels = row_count * col_count
    factor = 1.0 / math.sqrt(angles * (row_count * tile_count + col_count * agent_count))
    both = ("tile", "agent")
    f32 = jnp.float32

    noisy = agent_state[1:, 0].astype(jnp.bfloat16)
    packed = jnp.concatenate([noisy[:, : planes // 2], noisy[:, planes // 2 :]], axis=-1)
    following = hop(packed[:2], "tile", -1)

    group = (lax.axis_index("tile") * agent_count // planes).astype(jnp.int32)
    pieces, flat, rel, near = pl.pallas_call(
        project_kernel,
        out_shape=[
            jax.ShapeDtypeStruct((angles, planes, 2 * WINDOW), f32),
            jax.ShapeDtypeStruct((planes, pixels), f32),
            jax.ShapeDtypeStruct((angles, pixels), jnp.int32),
            jax.ShapeDtypeStruct((angles, pixels), f32),
        ],
        in_specs=[SMEM] + [VMEM] * 4,
        out_specs=[VMEM] * 4,
        scratch_shapes=[pltpu.VMEM((angles, WINDOW), f32)],
        name="project",
    )(group.reshape(1), agent_state[:1], bin_index, bin_frac, measured)

    region = pl.pallas_call(
        shift_kernel,
        out_shape=jax.ShapeDtypeStruct(packed.shape, packed.dtype),
        in_specs=[SMEM, VMEM, VMEM],
        out_specs=VMEM,
        name="shift",
    )(patch_offsets, packed, following)
    others = [hop(region, "agent", -step) for step in range(1, agent_count)]

    got = lax.all_to_all(pieces.reshape(angles * planes, 2 * WINDOW), both, 0, 0, tiled=True)
    cut = pl.pallas_call(
        functools.partial(combine_kernel, factor, measured.shape[2]),
        out_shape=jax.ShapeDtypeStruct((angles * planes, WINDOW), f32),
        in_specs=[VMEM],
        out_specs=VMEM,
        name="combine",
    )(got)

    parts = pl.pallas_call(
        denoise_kernel,
        out_shape=[jax.ShapeDtypeStruct(packed.shape, f32)] * 4,
        in_specs=[SMEM] + [VMEM] * 6,
        out_specs=[VMEM] * 4,
        name="denoise",
    )(patch_offsets, region, *others, up_weight, down_weight)
    arrived = [hop(parts[step], "agent", step) for step in range(1, agent_count)]

    back = lax.all_to_all(cut, both, 0, 0, tiled=True)
    nets = parts[0] + arrived[0] + arrived[1] + arrived[2]
    previous = hop(nets[:2], "tile", 1)

    return pl.pallas_call(
        functools.partial(finish_kernel, factor),
        out_shape=[
            jax.ShapeDtypeStruct(agent_state.shape, f32),
            jax.ShapeDtypeStruct(agent_state.shape[1:], f32),
        ],
        in_specs=[SMEM, SMEM] + [VMEM] * 7,
        out_specs=[VMEM, VMEM],
        name="finish",
    )(
        patch_offsets, agent_weights, agent_state, flat, rel, near,
        back.reshape(angles, planes, WINDOW), nets, previous,
    )


def solution(mesh):
    placed = (
        P(None, None, None, "tile", "agent"),
        P(None, None, ("tile", "agent")),
        P(None, "tile", "agent"),
        P(None, "tile", "agent"),
        P(),
        P(),
        P(None, None, "agent"),
        P(None, "agent", None),
    )
    return jax.shard_map(
        shards,
        mesh=mesh,
        in_specs=placed,
        out_specs=(P(None, None, None, "tile", "agent"), P(None, None, "tile", "agent")),
        check_vma=False,
    )
```

time: 186 us -> 100 us (0.54)
  blocking collectives: 78.5 us -> 0 us
  starting transfers between devices: 16.1 us -> 45.7 us
  between operations: 25.3 us -> 0.72 us
  local copies, waits for them, and re-layouts: 23.4 us -> 7.16 us
  Pallas kernels: 11.3 us -> 23.9 us
  matrix products: 7.96 us -> 0 us
    all_to_all x1 -> x0, blocking collectives: 40.7 us -> none  [data_agent(): lax.all_to_all(pieces.reshape(angles * planes, 2 * WINDOW), both, 0, 0, t...]
    all_gather x3 -> x0, blocking collectives: 37.8 us -> none  [apply_net(): lax.all_gather(patches, 'agent', axis=0, tiled=True)]
    all_to_all x1 -> x2, starting transfers between devices: 6.18 us -> 27.3 us  [the longest x1 15.6 us: shards(): lax.all_to_all(pieces.reshape(angles * planes, 2 * WINDOW), both, 0, 0, t...]
    pallas_call x3 -> x5, Pallas kernels: 11.3 us -> 23.9 us  [the longest x1 10.2 us: shards(): pl.pallas_call(denoise_kernel, out_shape=[jax.ShapeDtypeStruct(packed.sha...]
    reshape x15 -> x0, local copies, waits for them, and re-layouts: 10.6 us -> none  [the longest x2 3.57 us: in_plane(): result.reshape(n_time, n_slice, row_blocks, col_blocks, PATCH, PATCH)]
    ppermute x4 -> x8, starting transfers between devices: 9.84 us -> 18.4 us  [hop(): lax.ppermute(value, axis, [(i, (i + step) % count) for i in range(count)])]
    dot_general x3 -> x0, matrix products: 7.96 us -> none  [apply_net(): jnp.dot(hidden, down_weight[which], preferred_element_type=jnp.float32)]
    transpose x4 -> x0, local copies, waits for them, and re-layouts: 2.55 us -> none  [the longest x1 2.17 us: in_plane(): patches = patches.transpose(0, 1, 2, 4, 3, 5).reshape(-1, PATCH * PATCH)]
  transfers between devices with their start and end apart: 8 -> 10, of which waited for: 5 -> 6; matrix products, arithmetic and copies ran while one was open for 12% -> 4% of each run, Pallas kernels for 6% -> 14%
where the time goes in v2:
time: 100 us; the launch traced here: 99.5 us
  starting transfers between devices  45.7 us (46%)
  Pallas kernels  23.9 us (24%)
  waiting for transfers between devices  20.3 us (20%)
  local copies, waits for them, and re-layouts  7.16 us (7%)
  other arithmetic  1.81 us (2%)
    ppermute x8, starting transfers between devices, hop(): lax.ppermute(value, axis, [(i, (i + step) % count) for i in range(count)])  18.4 us
    all_to_all x1, starting transfers between devices, shards(): lax.all_to_all(pieces.reshape(angles * planes, 2 * WINDOW), both, 0, 0, t...  15.6 us
    ppermute x8, waiting for transfers between devices, hop(): lax.ppermute(value, axis, [(i, (i + step) % count) for i in range(count)])  14.7 us
    all_to_all x1, starting transfers between devices, shards(): back = lax.all_to_all(cut, both, 0, 0, tiled=True)  11.7 us
    pallas_call x1, Pallas kernels, shards(): pl.pallas_call(denoise_kernel, out_shape=[jax.ShapeDtypeStruct(packed.sha...  10.2 us
    all_to_all x1, waiting for transfers between devices, shards(): back = lax.all_to_all(cut, both, 0, 0, tiled=True)  5.51 us
    pallas_call x1, Pallas kernels, shards(): pl.pallas_call(project_kernel, out_shape=[jax.ShapeDtypeStruct((angles, p...  5.07 us
    pallas_call x1, Pallas kernels, shards(): pl.pallas_call(functools.partial(finish_kernel, factor), out_shape=[jax.S...  4.68 us
  transfers between devices with their start and end apart: 10, of which 6 were waited for; matrix products, arithmetic and copies ran while one was open for 4% of the time, Pallas kernels for 14%

profile of v2, /device:TPU:1, one launch (start us, length us, event | category | flops | bytes accessed | tf_op | source)
XLA Modules:
  0.0 99.5 jit_solution(897531883873925042)
XLA Ops:
  0.6 1.6 %slice.19.state_ref = f32[1,1,16,16,64]{4,3,2,1,0:T(8,128)} slice(f32[4,1,16,16,64]{4,3,2,1,0:T(8,128)} %state_ref.1), slice={[0:1], [0:1], [0:16], [0:16], [0:64]} | slice | bytes 131072 | tf_op jit(solution)/shard_map/slice | solution.py:313
  2.2 5.1 %project.1 = (f32[16,16,256]{2,1,0:T(8,128)}, f32[16,1024]{1,0:T(8,128)}, s32[16,1024]{1,0:T(8,128)}, f32[16,1024]{1,0:T(8,128)}) custom-call(s32[1]{0:T(128)} %bitcast.group_ref, f32[1,1,16,16,64]{4,3,2,1,0:T(8,128)} %slice.19.state_ref, s32[16,16,64]{2,1,0:T(8,128)} %bin_ref.1, s32[16,16,64]{2,1,0:T(8,128)} %num_ref.1, f32[1,16,88]{2,1,0:T(8,128)} %meas_ref.1), custom_call_target="tpu_custom_call" | custom-call | tf_op jit(solution)/shard_map/project/pallas_call | solution.py:301
  7.3 1.9 %copy.11 = f32[256,1,256]{2,1,0:T(1,128)} copy(f32[256,1,256]{2,0,1:T(8,128)} %bitcast.16) | data formatting | bytes 524288 | tf_op jit(solution)/shard_map/all_to_all | solution.py:324
  9.2 15.6 %all-to-all-start = ((f32[256,1,256]{2,1,0:T(1,128)}), f32[256,1,256]{2,1,0:T(1,128)S(1)}, u32[]{:S(2)}, u32[]{:S(2)}) async-start(f32[256,1,256]{2,1,0:T(1,128)} %copy.11), calls=%async_computation | async-start | bytes 524288 | tf_op jit(solution)/shard_map/all_to_all | solution.py:324
  24.9 1.0 %fusion = bf16[3,16,16,64]{3,2,1,0:T(8,128)(2,1)S(1)} fusion(f32[4,1,16,16,64]{4,3,2,0,1:T(8,128)} %bitcast.12), kind=kLoop, calls=%fused_computation.2 | loop fusion | bytes 196608 | tf_op jit(solution)/shard_map/convert_element_type | solution.py:296
  25.9 0.1 fusion.1
  26.0 2.2 %collective-permute-start = (bf16[2,8,16,128]{3,2,1,0:T(8,128)(2,1)S(1)}, bf16[2,8,16,128]{3,2,1,0:T(8,128)(2,1)S(1)}, u32[]{:S(2)}, u32[]{:S(2)}) collective-permute-start(bf16[2,8,16,128]{3,2,1,0:T(8,128)(2,1)S(1)} %fusion.1), channel_id=1, source_target_pairs={{0,252},{4,0},{8,4},{12,8},{16,12},{20,16},{24,20},{28,24},{32,28}... | collective-permute-start | bytes 196616 | tf_op jit(solution)/shard_map/ppermute | solution.py:281
  28.2 0.7 pad_maximum_fusion.own_ref
  29.0 3.3 %collective-permute-done.next_ref = bf16[2,8,16,128]{3,2,1,0:T(8,128)(2,1)S(1)} collective-permute-done((bf16[2,8,16,128]{3,2,1,0:T(8,128)(2,1)S(1)}, bf16[2,8,16,128]{3,2,1,0:T(8,128)(2,1)S(1)}, u32[]{:S(2)}, u32[]{:S(2)}) %collective-permute-start) | collective-permute-done | bytes 65568 | tf_op jit(solution)/shard_map/ppermute | solution.py:281
  32.3 0.0 copy-start.6
  32.3 0.6 copy-done.6
  32.9 1.6 %shift.1.p0 = bf16[3,8,16,128]{3,2,1,0:T(8,128)(2,1)} custom-call(s32[3]{0:T(128)} %offset_ref.5, bf16[3,8,16,128]{3,2,1,0:T(8,128)(2,1)} %pad_maximum_fusion.own_ref, bf16[2,8,16,128]{3,2,1,0:T(8,128)(2,1)} %copy-done.6), custom_call_target="tpu_custom_call" | custom-call | tf_op jit(solution)/shard_map/shift/pallas_call | solution.py:315
  34.5 3.0 %collective-permute-start.1 = (bf16[3,8,16,128]{3,2,1,0:T(8,128)(2,1)}, bf16[3,8,16,128]{3,2,1,0:T(8,128)(2,1)S(1)}, u32[]{:S(2)}, u32[]{:S(2)}) collective-permute-start(bf16[3,8,16,128]{3,2,1,0:T(8,128)(2,1)} %shift.1.p0), channel_id=1, source_target_pairs={{0,3},{1,0},{2,1},{3,2},{4,7},{5,4},{6,5},{7,6},{8,11},{9,8},{10,9... | collective-permute-start | bytes 294920 | tf_op jit(solution)/shard_map/ppermute | solution.py:281
  37.5 2.2 %collective-permute-start.2 = (bf16[3,8,16,128]{3,2,1,0:T(8,128)(2,1)}, bf16[3,8,16,128]{3,2,1,0:T(8,128)(2,1)S(1)}, u32[]{:S(2)}, u32[]{:S(2)}) collective-permute-start(bf16[3,8,16,128]{3,2,1,0:T(8,128)(2,1)} %shift.1.p0), channel_id=1, source_target_pairs={{0,2},{1,3},{2,0},{3,1},{4,6},{5,7},{6,4},{7,5},{8,10},{9,11},{10,... | collective-permute-start | bytes 294920 | tf_op jit(solution)/shard_map/ppermute | solution.py:281
  39.7 2.4 %collective-permute-start.3 = (bf16[3,8,16,128]{3,2,1,0:T(8,128)(2,1)}, bf16[3,8,16,128]{3,2,1,0:T(8,128)(2,1)S(1)}, u32[]{:S(2)}, u32[]{:S(2)}) collective-permute-start(bf16[3,8,16,128]{3,2,1,0:T(8,128)(2,1)} %shift.1.p0), channel_id=1, source_target_pairs={{0,1},{1,2},{2,3},{3,0},{4,5},{5,6},{6,7},{7,4},{8,9},{9,10},{10,1... | collective-permute-start | bytes 294920 | tf_op jit(solution)/shard_map/ppermute | solution.py:281
  42.1 0.0 collective-permute-done.1.p1
  42.1 0.0 copy-start.3
  42.1 3.2 %collective-permute-done.2.p2 = bf16[3,8,16,128]{3,2,1,0:T(8,128)(2,1)S(1)} collective-permute-done((bf16[3,8,16,128]{3,2,1,0:T(8,128)(2,1)}, bf16[3,8,16,128]{3,2,1,0:T(8,128)(2,1)S(1)}, u32[]{:S(2)}, u32[]{:S(2)}) %collective-permute-start.2) | collective-permute-done | bytes 98336 | tf_op jit(solution)/shard_map/ppermute | solution.py:281
  45.3 0.0 copy-start.4
  45.3 2.1 %collective-permute-done.3.p3 = bf16[3,8,16,128]{3,2,1,0:T(8,128)(2,1)S(1)} collective-permute-done((bf16[3,8,16,128]{3,2,1,0:T(8,128)(2,1)}, bf16[3,8,16,128]{3,2,1,0:T(8,128)(2,1)S(1)}, u32[]{:S(2)}, u32[]{:S(2)}) %collective-permute-start.3) | collective-permute-done | bytes 98336 | tf_op jit(solution)/shard_map/ppermute | solution.py:281
  47.4 0.0 copy-done.3
  47.4 0.0 copy-done.4
  47.4 0.0 copy-start.5
  47.4 0.6 copy-done.5
  48.0 10.2 %denoise.1 = (f32[3,8,16,128]{3,2,1,0:T(8,128)}, f32[3,8,16,128]{3,2,1,0:T(8,128)}, f32[3,8,16,128]{3,2,1,0:T(8,128)}, f32[3,8,16,128]{3,2,1,0:T(8,128)}) custom-call(s32[3]{0:T(128)} %offset_ref.5, bf16[3,8,16,128]{3,2,1,0:T(8,128)(2,1)} %shift.1.p0, bf16[3,8,16,128]{3,2,1,0:T(8,128)(2,1)} %copy-done.3, bf16[3,8,16,128]{3,2,1,0:T(8,128)(2,1)} %copy-done.4, ...), custom_call_target="tpu_custom_call" | custom-call | tf_op jit(solution)/shard_map/denoise/pallas_call | solution.py:333
  58.2 0.9 collective-permute-start.4
  59.1 4.0 %collective-permute-start.5 = (f32[3,8,16,128]{3,2,1,0:T(8,128)}, f32[3,8,16,128]{3,2,1,0:T(8,128)S(1)}, u32[]{:S(2)}, u32[]{:S(2)}) collective-permute-start(f32[3,8,16,128]{3,2,1,0:T(8,128)} %get-tuple-element.16), channel_id=1, source_target_pairs={{0,2},{1,3},{2,0},{3,1},{4,6},{5,7},{6,4},{7,5},{8,10},{9,11},{10,... | collective-permute-start | bytes 589832 | tf_op jit(solution)/shard_map/ppermute | solution.py:281
  63.1 3.5 %collective-permute-start.6 = (f32[3,8,16,128]{3,2,1,0:T(8,128)}, f32[3,8,16,128]{3,2,1,0:T(8,128)S(1)}, u32[]{:S(2)}, u32[]{:S(2)}) collective-permute-start(f32[3,8,16,128]{3,2,1,0:T(8,128)} %get-tuple-element.17), channel_id=1, source_target_pairs={{0,3},{1,0},{2,1},{3,2},{4,7},{5,4},{6,5},{7,6},{8,11},{9,8},{10,9... | collective-permute-start | bytes 589832 | tf_op jit(solution)/shard_map/ppermute | solution.py:281
  66.6 0.0 all-to-all-done
  66.6 0.7 copy.16
  67.3 2.4 %combine.1 = f32[256,128]{1,0:T(8,128)} custom-call(f32[256,256]{1,0:T(8,128)} %bitcast.13), custom_call_target="tpu_custom_call" | custom-call | tf_op jit(solution)/shard_map/combine/pallas_call | solution.py:325
  69.7 11.7 %all-to-all-start.1 = ((f32[256,1,128]{2,1,0:T(1,128)}), f32[256,1,128]{2,1,0:T(1,128)S(1)}, u32[]{:S(2)}, u32[]{:S(2)}) async-start(f32[256,1,128]{2,1,0:T(1,128)} %bitcast.14), calls=%async_computation.1 | async-start | bytes 262144 | tf_op jit(solution)/shard_map/all_to_all | solution.py:342
  81.4 0.0 collective-permute-done.4
  81.4 0.0 collective-permute-done.5
  81.4 2.9 %collective-permute-done.6 = f32[3,8,16,128]{3,2,1,0:T(8,128)S(1)} collective-permute-done((f32[3,8,16,128]{3,2,1,0:T(8,128)}, f32[3,8,16,128]{3,2,1,0:T(8,128)S(1)}, u32[]{:S(2)}, u32[]{:S(2)}) %collective-permute-start.6) | collective-permute-done | bytes 196640 | tf_op jit(solution)/shard_map/ppermute | solution.py:281
  84.3 1.0 add_add_fusion.net_ref
  85.3 0.0 copy-start
  85.3 0.1 collective-permute-start.7
  85.5 3.2 %collective-permute-done.7.prev_ref = f32[2,8,16,128]{3,2,1,0:T(8,128)S(1)} collective-permute-done((f32[2,8,16,128]{3,2,1,0:T(8,128)S(1)}, f32[2,8,16,128]{3,2,1,0:T(8,128)S(1)}, u32[]{:S(2)}, u32[]{:S(2)}) %collective-permute-start.7) | collective-permute-done | bytes 131104 | tf_op jit(solution)/shard_map/ppermute | solution.py:281
  88.7 0.0 copy-start.2
  88.7 5.5 %all-to-all-done.1 = f32[256,1,128]{2,1,0:T(1,128)S(1)} async-done(((f32[256,1,128]{2,1,0:T(1,128)}), f32[256,1,128]{2,1,0:T(1,128)S(1)}, u32[]{:S(2)}, u32[]{:S(2)}) %all-to-all-start.1) | async-done | bytes 131104 | tf_op jit(solution)/shard_map/all_to_all | solution.py:342
  94.2 0.0 copy-start.1
  94.2 0.0 copy-done
  94.2 0.0 copy-done.2
  94.2 0.6 copy-done.1
  94.9 4.7 %finish.1 = (f32[4,1,16,16,64]{4,3,2,1,0:T(8,128)}, f32[1,16,16,64]{3,2,1,0:T(8,128)}) custom-call(s32[3]{0:T(128)} %offset_ref.5, f32[4]{0:T(128)} %weight_ref.1, f32[4,1,16,16,64]{4,3,2,1,0:T(8,128)} %state_ref.1, f32[16,1024]{1,0:T(8,128)} %get-tuple-element.10.u_ref, s32[16,1024]{1,0:T(8,128)} %get-tuple-element.11.rel_ref, ...), custom_call_target="tpu_custom_call" | custom-call | tf_op jit(solution)/shard_map/finish/pallas_call | solution.py:346
  (2 shorter events, 0.0 us)
Async XLA Ops:
  9.2 57.4 %all-to-all-start = ((f32[256,1,256]{2,1,0:T(1,128)}), f32[256,1,256]{2,1,0:T(1,128)S(1)}, u32[]{:S(2)}, u32[]{:S(2)}) async-start(f32[256,1,256]{2,1,0:T(1,128)} %copy.11), calls=%async_computation | async-start | bytes 524288 | tf_op jit(solution)/shard_map/all_to_all | solution.py:324
  26.0 6.3 %collective-permute-start = (bf16[2,8,16,128]{3,2,1,0:T(8,128)(2,1)S(1)}, bf16[2,8,16,128]{3,2,1,0:T(8,128)(2,1)S(1)}, u32[]{:S(2)}, u32[]{:S(2)}) collective-permute-start(bf16[2,8,16,128]{3,2,1,0:T(8,128)(2,1)S(1)} %fusion.1), channel_id=1, source_target_pairs={{0,252},{4,0},{8,4},{12,8},{16,12},{20,16},{24,20},{28,24},{32,28}... | collective-permute-start | bytes 196616 | tf_op jit(solution)/shard_map/ppermute | solution.py:281
  32.3 0.6 copy-start.6
  34.5 7.6 %collective-permute-start.1 = (bf16[3,8,16,128]{3,2,1,0:T(8,128)(2,1)}, bf16[3,8,16,128]{3,2,1,0:T(8,128)(2,1)S(1)}, u32[]{:S(2)}, u32[]{:S(2)}) collective-permute-start(bf16[3,8,16,128]{3,2,1,0:T(8,128)(2,1)} %shift.1.p0), channel_id=1, source_target_pairs={{0,3},{1,0},{2,1},{3,2},{4,7},{5,4},{6,5},{7,6},{8,11},{9,8},{10,9... | collective-permute-start | bytes 294920 | tf_op jit(solution)/shard_map/ppermute | solution.py:281
  37.5 7.8 %collective-permute-start.2 = (bf16[3,8,16,128]{3,2,1,0:T(8,128)(2,1)}, bf16[3,8,16,128]{3,2,1,0:T(8,128)(2,1)S(1)}, u32[]{:S(2)}, u32[]{:S(2)}) collective-permute-start(bf16[3,8,16,128]{3,2,1,0:T(8,128)(2,1)} %shift.1.p0), channel_id=1, source_target_pairs={{0,2},{1,3},{2,0},{3,1},{4,6},{5,7},{6,4},{7,5},{8,10},{9,11},{10,... | collective-permute-start | bytes 294920 | tf_op jit(solution)/shard_map/ppermute | solution.py:281
  39.7 7.6 %collective-permute-start.3 = (bf16[3,8,16,128]{3,2,1,0:T(8,128)(2,1)}, bf16[3,8,16,128]{3,2,1,0:T(8,128)(2,1)S(1)}, u32[]{:S(2)}, u32[]{:S(2)}) collective-permute-start(bf16[3,8,16,128]{3,2,1,0:T(8,128)(2,1)} %shift.1.p0), channel_id=1, source_target_pairs={{0,1},{1,2},{2,3},{3,0},{4,5},{5,6},{6,7},{7,4},{8,9},{9,10},{10,1... | collective-permute-start | bytes 294920 | tf_op jit(solution)/shard_map/ppermute | solution.py:281
  42.1 5.3 %copy-start.3 = (bf16[3,8,16,128]{3,2,1,0:T(8,128)(2,1)}, bf16[3,8,16,128]{3,2,1,0:T(8,128)(2,1)S(1)}, u32[]{:S(2)}) copy-start(bf16[3,8,16,128]{3,2,1,0:T(8,128)(2,1)S(1)} %collective-permute-done.1.p1) | copy-start | bytes 294916
  45.3 2.1 %copy-start.4 = (bf16[3,8,16,128]{3,2,1,0:T(8,128)(2,1)}, bf16[3,8,16,128]{3,2,1,0:T(8,128)(2,1)S(1)}, u32[]{:S(2)}) copy-start(bf16[3,8,16,128]{3,2,1,0:T(8,128)(2,1)S(1)} %collective-permute-done.2.p2) | copy-start | bytes 294916
  47.4 0.6 copy-start.5
  58.2 23.3 %collective-permute-start.4 = (f32[3,8,16,128]{3,2,1,0:T(8,128)}, f32[3,8,16,128]{3,2,1,0:T(8,128)S(1)}, u32[]{:S(2)}, u32[]{:S(2)}) collective-permute-start(f32[3,8,16,128]{3,2,1,0:T(8,128)} %get-tuple-element.15), channel_id=1, source_target_pairs={{0,1},{1,2},{2,3},{3,0},{4,5},{5,6},{6,7},{7,4},{8,9},{9,10},{10,1... | collective-permute-start | bytes 589832 | tf_op jit(solution)/shard_map/ppermute | solution.py:281
  59.1 22.4 %collective-permute-start.5 = (f32[3,8,16,128]{3,2,1,0:T(8,128)}, f32[3,8,16,128]{3,2,1,0:T(8,128)S(1)}, u32[]{:S(2)}, u32[]{:S(2)}) collective-permute-start(f32[3,8,16,128]{3,2,1,0:T(8,128)} %get-tuple-element.16), channel_id=1, source_target_pairs={{0,2},{1,3},{2,0},{3,1},{4,6},{5,7},{6,4},{7,5},{8,10},{9,11},{10,... | collective-permute-start | bytes 589832 | tf_op jit(solution)/shard_map/ppermute | solution.py:281
  63.1 21.2 %collective-permute-start.6 = (f32[3,8,16,128]{3,2,1,0:T(8,128)}, f32[3,8,16,128]{3,2,1,0:T(8,128)S(1)}, u32[]{:S(2)}, u32[]{:S(2)}) collective-permute-start(f32[3,8,16,128]{3,2,1,0:T(8,128)} %get-tuple-element.17), channel_id=1, source_target_pairs={{0,3},{1,0},{2,1},{3,2},{4,7},{5,4},{6,5},{7,6},{8,11},{9,8},{10,9... | collective-permute-start | bytes 589832 | tf_op jit(solution)/shard_map/ppermute | solution.py:281
  69.7 24.5 %all-to-all-start.1 = ((f32[256,1,128]{2,1,0:T(1,128)}), f32[256,1,128]{2,1,0:T(1,128)S(1)}, u32[]{:S(2)}, u32[]{:S(2)}) async-start(f32[256,1,128]{2,1,0:T(1,128)} %bitcast.14), calls=%async_computation.1 | async-start | bytes 262144 | tf_op jit(solution)/shard_map/all_to_all | solution.py:342
  85.3 8.9 %copy-start = (f32[3,8,16,128]{3,2,1,0:T(8,128)}, f32[3,8,16,128]{3,2,1,0:T(8,128)S(1)}, u32[]{:S(2)}) copy-start(f32[3,8,16,128]{3,2,1,0:T(8,128)S(1)} %add_add_fusion.net_ref) | copy-start | bytes 589828
  85.3 3.4 %collective-permute-start.7 = (f32[2,8,16,128]{3,2,1,0:T(8,128)S(1)}, f32[2,8,16,128]{3,2,1,0:T(8,128)S(1)}, u32[]{:S(2)}, u32[]{:S(2)}) collective-permute-start(f32[2,8,16,128]{3,2,1,0:T(8,128)S(1)} %slice.30), channel_id=1, source_target_pairs={{0,4},{4,8},{8,12},{12,16},{16,20},{20,24},{24,28},{28,32},{32,36}... | collective-permute-start | bytes 393224 | tf_op jit(solution)/shard_map/ppermute | solution.py:281
  88.7 5.5 %copy-start.2 = (f32[2,8,16,128]{3,2,1,0:T(8,128)}, f32[2,8,16,128]{3,2,1,0:T(8,128)S(1)}, u32[]{:S(2)}) copy-start(f32[2,8,16,128]{3,2,1,0:T(8,128)S(1)} %collective-permute-done.7.prev_ref) | copy-start | bytes 393220
  94.2 0.7 copy-start.1

commit v3 on v2

--- a/solution.py
+++ b/solution.py
@@ -8,6 +8,7 @@
 from jax.experimental.pallas import tpu as pltpu
 from jax.sharding import PartitionSpec as P
 
+
 PATCH = 16
 SCALE = 724
 WINDOW = 128
@@ -31,9 +32,9 @@
 def project_kernel(
     group_ref, state_ref, bin_ref, num_ref, meas_ref, out_ref, u_ref, rel_ref, w_ref, start_ref
 ):
-    angles, planes, _ = out_ref.shape
-    cols = bin_ref.shape[2]
-    for x in range(bin_ref.shape[1]):
+    angles, rows, cols = bin_ref.shape
+    planes = state_ref.shape[2]
+    for x in range(rows):
         span = slice(x * cols, (x + 1) * cols)
         u_ref[:, span] = state_ref[0, 0, :, x, :]
         rel_ref[:, span] = bin_ref[:, x, :]
@@ -44,7 +45,8 @@
     start_ref[...] = jnp.broadcast_to(start.astype(jnp.float32), (angles, WINDOW))
     out_ref[...] = jnp.zeros_like(out_ref)
     owned = meas_ref.shape[2]
-    out_ref[group_ref[0], :, WINDOW : WINDOW + owned] = meas_ref[0]
+    mine = pl.multiple_of(group_ref[0] * (2 * planes), 2 * planes)
+    out_ref[pl.ds(mine + 1, planes, stride=2), :owned] = meas_ref[0]
     lane = lax.broadcasted_iota(jnp.int32, (planes, WINDOW), 1)
 
     def body(a, carry):
@@ -60,20 +62,22 @@
         at_low = sums[:planes] + sums[planes : 2 * planes]
         above = sums[2 * planes : 3 * planes] + sums[3 * planes :]
         piece = at_low + pltpu.roll(above, 1, 1)
-        out_ref[a, :, :WINDOW] = jnp.where(lane == WINDOW - 1, start_ref[pl.ds(a, 1), :], piece)
+        piece = jnp.where(lane == WINDOW - 1, start_ref[pl.ds(a, 1), :], piece)
+        first = pl.multiple_of(a * (2 * planes), 2 * planes)
+        out_ref[pl.ds(first, planes, stride=2), :] = piece
         return carry
 
     lax.fori_loop(0, angles, body, 0, unroll=2)
 
 
 def combine_kernel(factor, owned, got_ref, out_ref):
-    count = got_ref.shape[0]
+    count = got_ref.shape[0] // 2
     step = WINDOW // ALIGN
     rows = 16
-    got = got_ref[...]
+    got = got_ref[pl.ds(0, count, stride=2), :]
     lane_all = lax.broadcasted_iota(jnp.int32, (count, WINDOW), 1)
-    piece = jnp.where(lane_all < WINDOW - 1, got[:, :WINDOW], 0.0)
-    block = got[:, WINDOW - 1 : WINDOW].astype(jnp.int32) // ALIGN
+    piece = jnp.where(lane_all < WINDOW - 1, got, 0.0)
+    block = got[:, WINDOW - 1 :].astype(jnp.int32) // ALIGN
     slot = (block % step) * rows + block // step
     slots = lax.broadcasted_iota(jnp.int32, (count, step * rows), 1)
     route = jnp.where(slots == slot, 1.0, 0.0).astype(jnp.bfloat16)
@@ -92,7 +96,8 @@
         here = lane >= m * ALIGN
         sino = sino + jnp.where(here, turned, 0.0)
         sino = sino + pltpu.roll(jnp.where(here, 0.0, turned), 1, 0)
-    taken = jnp.sum(got[:, WINDOW:].reshape(count // 16, 16, WINDOW), axis=0)
+    sent = got_ref[pl.ds(1, count, stride=2), :]
+    taken = jnp.sum(sent.reshape(count // 16, 16, WINDOW), axis=0)
     taken = jnp.where(lax.broadcasted_iota(jnp.int32, taken.shape, 1) < owned, taken, 0.0)
     target = jnp.zeros_like(sino)
     for i in range(16):
@@ -116,15 +121,24 @@
     out_ref[...] = cut[:, :WINDOW] + cut[:, WINDOW:]
 
 
-def shift_kernel(offset_ref, own_ref, next_ref, out_ref):
-    rows = own_ref.shape[2]
+def pack_kernel(state_ref, head_ref, tail_ref):
+    half = state_ref.shape[2] // 2
+    cols = state_ref.shape[4]
+    for k in range(3):
+        out = head_ref.at[k] if k < 2 else tail_ref.at[0]
+        out[:, :, :cols] = state_ref[k + 1, 0, :half].astype(out.dtype)
+        out[:, :, cols:] = state_ref[k + 1, 0, half:].astype(out.dtype)
+
+
+def shift_kernel(offset_ref, head_ref, tail_ref, next_ref, out_ref):
+    rows = head_ref.shape[2]
     for k in range(2):
         o = offset_ref[k]
-        own = pltpu.roll(own_ref[k].astype(jnp.float32), rows - o, 1)
+        own = pltpu.roll(head_ref[k].astype(jnp.float32), rows - o, 1)
         more = pltpu.roll(next_ref[k].astype(jnp.float32), rows - o, 1)
         row = lax.broadcasted_iota(jnp.int32, own.shape, 1)
         out_ref[k] = jnp.where(row < rows - o, own, more).astype(out_ref.dtype)
-    out_ref[2] = own_ref[2]
+    out_ref[2] = tail_ref[0]
 
 
 def swap_slabs(slabs):
@@ -273,6 +287,7 @@
 
 
 VMEM = pl.BlockSpec(memory_space=pltpu.VMEM)
+PARAMS = pltpu.CompilerParams(vmem_limit_bytes=20 * 1024 * 1024)
 SMEM = pl.BlockSpec(memory_space=pltpu.SMEM)
 
 
@@ -281,7 +296,7 @@
     return lax.ppermute(value, axis, [(i, (i + step) % count) for i in range(count)])
 
 
-def shards(
+def step(
     agent_state, measured, bin_index, bin_frac, patch_offsets, agent_weights, up_weight, down_weight
 ):
     planes, row_count, col_count = agent_state.shape[2:]
@@ -293,51 +308,78 @@
     both = ("tile", "agent")
     f32 = jnp.float32
 
-    noisy = agent_state[1:, 0].astype(jnp.bfloat16)
-    packed = jnp.concatenate([noisy[:, : planes // 2], noisy[:, planes // 2 :]], axis=-1)
-    following = hop(packed[:2], "tile", -1)
+    shape = (planes // 2, row_count, 2 * col_count)
+    head, tail = pl.pallas_call(
+        pack_kernel,
+        out_shape=[
+            jax.ShapeDtypeStruct((2,) + shape, jnp.bfloat16),
+            jax.ShapeDtypeStruct((1,) + shape, jnp.bfloat16),
+        ],
+        in_specs=[VMEM],
+        out_specs=[VMEM] * 2,
+        compiler_params=PARAMS,
+        name="pack",
+    )(agent_state)
+    following = hop(head, "tile", -1)
 
     group = (lax.axis_index("tile") * agent_count // planes).astype(jnp.int32)
     pieces, flat, rel, near = pl.pallas_call(
         project_kernel,
         out_shape=[
-            jax.ShapeDtypeStruct((angles, planes, 2 * WINDOW), f32),
+            jax.ShapeDtypeStruct((2 * angles * planes, WINDOW), f32),
             jax.ShapeDtypeStruct((planes, pixels), f32),
             jax.ShapeDtypeStruct((angles, pixels), jnp.int32),
             jax.ShapeDtypeStruct((angles, pixels), f32),
         ],
-        in_specs=[SMEM] + [VMEM] * 4,
+        grid=(1,),
+        in_specs=[
+            SMEM,
+            pl.BlockSpec((1,) + agent_state.shape[1:], lambda i: (0, 0, 0, 0, 0)),
+            VMEM,
+            VMEM,
+            VMEM,
+        ],
         out_specs=[VMEM] * 4,
         scratch_shapes=[pltpu.VMEM((angles, WINDOW), f32)],
+        compiler_params=PARAMS,
         name="project",
-    )(group.reshape(1), agent_state[:1], bin_index, bin_frac, measured)
+    )(group.reshape(1), agent_state, bin_index, bin_frac, measured)
 
     region = pl.pallas_call(
         shift_kernel,
-        out_shape=jax.ShapeDtypeStruct(packed.shape, packed.dtype),
-        in_specs=[SMEM, VMEM, VMEM],
+        out_shape=jax.ShapeDtypeStruct((3,) + shape, jnp.bfloat16),
+        in_specs=[SMEM, VMEM, VMEM, VMEM],
         out_specs=VMEM,
+        compiler_params=PARAMS,
         name="shift",
-    )(patch_offsets, packed, following)
-    others = [hop(region, "agent", -step) for step in range(1, agent_count)]
-
-    got = lax.all_to_all(pieces.reshape(angles * planes, 2 * WINDOW), both, 0, 0, tiled=True)
+    )(patch_offsets, head, tail, following)
+    region, pieces = lax.optimization_barrier((region, pieces))
+    others = []
+    for step in range(1, agent_count):
+        others.append(hop(region, "agent", -step))
+
+    count = angles * planes
+    got = lax.all_to_all(pieces.reshape(count, 2, WINDOW), both, 0, 0, tiled=True)
     cut = pl.pallas_call(
         functools.partial(combine_kernel, factor, measured.shape[2]),
         out_shape=jax.ShapeDtypeStruct((angles * planes, WINDOW), f32),
         in_specs=[VMEM],
         out_specs=VMEM,
+        compiler_params=PARAMS,
         name="combine",
-    )(got)
+    )(got.reshape(2 * count, WINDOW))
 
     parts = pl.pallas_call(
         denoise_kernel,
-        out_shape=[jax.ShapeDtypeStruct(packed.shape, f32)] * 4,
+        out_shape=[jax.ShapeDtypeStruct((3,) + shape, f32)] * 4,
         in_specs=[SMEM] + [VMEM] * 6,
         out_specs=[VMEM] * 4,
+        compiler_params=PARAMS,
         name="denoise",
     )(patch_offsets, region, *others, up_weight, down_weight)
-    arrived = [hop(parts[step], "agent", step) for step in range(1, agent_count)]
+    arrived = []
+    for step in range(1, agent_count):
+        arrived.append(hop(parts[step], "agent", step))
 
     back = lax.all_to_all(cut, both, 0, 0, tiled=True)
     nets = parts[0] + arrived[0] + arrived[1] + arrived[2]
@@ -351,6 +393,7 @@
         ],
         in_specs=[SMEM, SMEM] + [VMEM] * 7,
         out_specs=[VMEM, VMEM],
+        compiler_params=PARAMS,
         name="finish",
     )(
         patch_offsets, agent_weights, agent_state, flat, rel, near,
@@ -370,7 +413,7 @@
         P(None, "agent", None),
     )
     return jax.shard_map(
-        shards,
+        step,
         mesh=mesh,
         in_specs=placed,
         out_specs=(P(None, None, None, "tile", "agent"), P(None, None, "tile", "agent")),

time: 100 us -> 91.6 us (0.916)
  Pallas kernels: 23.9 us -> 17.8 us
  starting transfers between devices: 45.7 us -> 43.8 us
  waiting for transfers between devices: 20.3 us -> 22.1 us
  other arithmetic: 1.81 us -> 0.05 us
    pallas_call x5 -> x6, Pallas kernels: 23.9 us -> 17.8 us  [the longest x1 7.74 us: step(): pl.pallas_call(denoise_kernel, out_shape=[jax.ShapeDtypeStruct((3,) + sha...]
    unnamed x15 -> x22, local copies, waits for them, and re-layouts: 2.63 us -> 6.66 us
    all_to_all x2, starting transfers between devices: 27.3 us -> 25 us  [the longest x1 12.9 us: step(): lax.all_to_all(pieces.reshape(count, 2, WINDOW), both, 0, 0, tiled=True)]
    all_to_all x1 -> x0, local copies, waits for them, and re-layouts: 1.92 us -> none  [shards(): lax.all_to_all(pieces.reshape(angles * planes, 2 * WINDOW), both, 0, 0, t...]
    all_to_all x2, waiting for transfers between devices: 5.51 us -> 7.41 us  [the longest x1 7.41 us: step(): back = lax.all_to_all(cut, both, 0, 0, tiled=True)]
    slice x3 -> x1, local copies, waits for them, and re-layouts: 1.6 us -> 0.01 us  [step(): previous = hop(nets[:2], 'tile', 1)]
    convert_element_type x1 -> x0, local copies, waits for them, and re-layouts: 1.03 us -> none  [shards(): noisy = agent_state[1:, 0].astype(jnp.bfloat16)]
  transfers between devices with their start and end apart: 10 -> 10, of which waited for: 6 -> 5; matrix products, arithmetic and copies ran while one was open for 4% -> 0% of each run, Pallas kernels for 14% -> 14%
where the time goes in v3:
time: 91.6 us; the launch traced here: 91.2 us
  starting transfers between devices  43.8 us (48%)
  waiting for transfers between devices  22.1 us (24%)
  Pallas kernels  17.8 us (19%)
  local copies, waits for them, and re-layouts  6.67 us (7%)
    ppermute x8, starting transfers between devices, hop(): lax.ppermute(value, axis, [(i, (i + step) % count) for i in range(count)])  18.8 us
    ppermute x8, waiting for transfers between devices, hop(): lax.ppermute(value, axis, [(i, (i + step) % count) for i in range(count)])  14.7 us
    all_to_all x1, starting transfers between devices, step(): lax.all_to_all(pieces.reshape(count, 2, WINDOW), both, 0, 0, tiled=True)  12.9 us
    all_to_all x1, starting transfers between devices, step(): back = lax.all_to_all(cut, both, 0, 0, tiled=True)  12.1 us
    pallas_call x1, Pallas kernels, step(): pl.pallas_call(denoise_kernel, out_shape=[jax.ShapeDtypeStruct((3,) + sha...  7.74 us
    all_to_all x1, waiting for transfers between devices, step(): back = lax.all_to_all(cut, both, 0, 0, tiled=True)  7.41 us
    unnamed x22, local copies, waits for them, and re-layouts  6.66 us
    pallas_call x1, Pallas kernels, step(): pl.pallas_call(project_kernel, out_shape=[jax.ShapeDtypeStruct((2 * angle...  4.03 us
  transfers between devices with their start and end apart: 10, of which 5 were waited for; matrix products, arithmetic and copies ran while one was open for 0% of the time, Pallas kernels for 14%

profile of v3, /device:TPU:1, one launch (start us, length us, event | category | flops | bytes accessed | tf_op | source)
XLA Modules:
  0.0 91.2 jit_solution(15311256965277814428)
XLA Ops:
  0.6 0.0 copy-start
  0.6 1.0 %copy-done = f32[4,1,16,16,64]{4,3,2,1,0:T(8,128)S(1)} copy-done((f32[4,1,16,16,64]{4,3,2,1,0:T(8,128)S(1)}, f32[4,1,16,16,64]{4,3,2,1,0:T(8,128)}, u32[]{:S(2)}) %copy-start) | copy-done | bytes 262168
  1.7 0.0 copy-start.9
  1.7 0.1 pack.1
  1.8 3.3 %collective-permute-start = (bf16[2,8,16,128]{3,2,1,0:T(8,128)(2,1)S(1)}, bf16[2,8,16,128]{3,2,1,0:T(8,128)(2,1)S(1)}, u32[]{:S(2)}, u32[]{:S(2)}) collective-permute-start(bf16[2,8,16,128]{3,2,1,0:T(8,128)(2,1)S(1)} %get-tuple-element.17.head_ref), channel_id=1, source_target_pairs={{0,252},{4,0},{8,4},{12,8},{16,12},{20,16},{24,20},{28,24},{32,28}... | collective-permute-start | bytes 196616 | tf_op jit(solution)/shard_map/ppermute | solution.py:296
  5.1 0.0 copy-start.1
  5.1 1.0 %copy-done.1 = f32[4,1,16,16,64]{4,3,2,1,0:T(8,128)S(1)} copy-done((f32[4,1,16,16,64]{4,3,2,1,0:T(8,128)S(1)}, f32[4,1,16,16,64]{4,3,2,1,0:T(8,128)}, u32[]{:S(2)}) %copy-start.1) | copy-done | bytes 262168
  6.1 0.0 copy-start.5
  6.1 0.9 copy-done.5
  7.0 0.0 copy-start.6
  7.0 0.9 copy-done.6
  7.9 0.0 copy-start.7
  7.9 0.7 copy-done.7
  8.6 0.0 copy-start.3
  8.6 4.0 %project.1 = (f32[512,128]{1,0:T(8,128)}, f32[16,1024]{1,0:T(8,128)S(1)}, s32[16,1024]{1,0:T(8,128)S(1)}, f32[16,1024]{1,0:T(8,128)S(1)}) custom-call(s32[1]{0:T(128)} %bitcast.group_ref, f32[4,1,16,16,64]{4,3,2,1,0:T(8,128)S(1)} %copy-done.1, s32[16,16,64]{2,1,0:T(8,128)S(1)} %copy-done.5, s32[16,16,64]{2,1,0:T(8,128)S(1)} %copy-done.6, ...), custom_call_target="tpu_custom_call" | custom-call | tf_op jit(solution)/shard_map/project/pallas_call | solution.py:326
  12.7 0.0 collective-permute-done.next_ref
  12.7 0.0 copy-start.8
  12.7 0.7 copy-done.8
  13.3 0.6 shift.1.p0
  13.9 12.9 %all-to-all-start = ((f32[256,2,128]{2,1,0:T(2,128)}), f32[256,2,128]{2,1,0:T(2,128)S(1)}, u32[]{:S(2)}, u32[]{:S(2)}) async-start(f32[256,2,128]{2,1,0:T(2,128)} %bitcast.1), calls=%async_computation | async-start | bytes 524288 | tf_op jit(solution)/shard_map/all_to_all | solution.py:362
  26.8 2.7 %collective-permute-start.3 = (bf16[3,8,16,128]{3,2,1,0:T(8,128)(2,1)S(1)}, bf16[3,8,16,128]{3,2,1,0:T(8,128)(2,1)S(1)}, u32[]{:S(2)}, u32[]{:S(2)}) collective-permute-start(bf16[3,8,16,128]{3,2,1,0:T(8,128)(2,1)S(1)} %shift.1.p0), channel_id=1, source_target_pairs={{0,1},{1,2},{2,3},{3,0},{4,5},{5,6},{6,7},{7,4},{8,9},{9,10},{10,1... | collective-permute-start | bytes 294920 | tf_op jit(solution)/shard_map/ppermute | solution.py:296
  29.5 4.4 %collective-permute-start.2 = (bf16[3,8,16,128]{3,2,1,0:T(8,128)(2,1)S(1)}, bf16[3,8,16,128]{3,2,1,0:T(8,128)(2,1)S(1)}, u32[]{:S(2)}, u32[]{:S(2)}) collective-permute-start(bf16[3,8,16,128]{3,2,1,0:T(8,128)(2,1)S(1)} %shift.1.p0), channel_id=1, source_target_pairs={{0,2},{1,3},{2,0},{3,1},{4,6},{5,7},{6,4},{7,5},{8,10},{9,11},{10,... | collective-permute-start | bytes 294920 | tf_op jit(solution)/shard_map/ppermute | solution.py:296
  33.9 2.8 %collective-permute-start.1 = (bf16[3,8,16,128]{3,2,1,0:T(8,128)(2,1)S(1)}, bf16[3,8,16,128]{3,2,1,0:T(8,128)(2,1)S(1)}, u32[]{:S(2)}, u32[]{:S(2)}) collective-permute-start(bf16[3,8,16,128]{3,2,1,0:T(8,128)(2,1)S(1)} %shift.1.p0), channel_id=1, source_target_pairs={{0,3},{1,0},{2,1},{3,2},{4,7},{5,4},{6,5},{7,6},{8,11},{9,8},{10,9... | collective-permute-start | bytes 294920 | tf_op jit(solution)/shard_map/ppermute | solution.py:296
  36.7 3.1 %collective-permute-done.3.p3 = bf16[3,8,16,128]{3,2,1,0:T(8,128)(2,1)S(1)} collective-permute-done((bf16[3,8,16,128]{3,2,1,0:T(8,128)(2,1)S(1)}, bf16[3,8,16,128]{3,2,1,0:T(8,128)(2,1)S(1)}, u32[]{:S(2)}, u32[]{:S(2)}) %collective-permute-start.3) | collective-permute-done | bytes 98336 | tf_op jit(solution)/shard_map/ppermute | solution.py:296
  39.8 6.3 %collective-permute-done.2.p2 = bf16[3,8,16,128]{3,2,1,0:T(8,128)(2,1)S(1)} collective-permute-done((bf16[3,8,16,128]{3,2,1,0:T(8,128)(2,1)S(1)}, bf16[3,8,16,128]{3,2,1,0:T(8,128)(2,1)S(1)}, u32[]{:S(2)}, u32[]{:S(2)}) %collective-permute-start.2) | collective-permute-done | bytes 98336 | tf_op jit(solution)/shard_map/ppermute | solution.py:296
  46.1 0.0 collective-permute-done.1.p1
  46.1 0.0 copy-done.9
  46.1 0.0 copy-done.3
  46.1 0.0 copy-start.4
  46.2 1.4 %copy-done.4 = bf16[3,1024,256]{2,1,0:T(8,128)(2,1)S(1)} copy-done((bf16[3,1024,256]{2,1,0:T(8,128)(2,1)S(1)}, bf16[3,1024,256]{2,1,0:T(8,128)(2,1)}, u32[]{:S(2)}) %copy-start.4) | copy-done | bytes 1572888
  47.6 7.7 %denoise.1 = (f32[3,8,16,128]{3,2,1,0:T(8,128)S(1)}, f32[3,8,16,128]{3,2,1,0:T(8,128)S(1)}, f32[3,8,16,128]{3,2,1,0:T(8,128)S(1)}, f32[3,8,16,128]{3,2,1,0:T(8,128)S(1)}) custom-call(s32[3]{0:T(128)S(1)} %copy-done.9, bf16[3,8,16,128]{3,2,1,0:T(8,128)(2,1)S(1)} %shift.1.p0, bf16[3,8,16,128]{3,2,1,0:T(8,128)(2,1)S(1)} %collective-permute-done.1.p1, ...), custom_call_target="tpu_custom_call" | custom-call | tf_op jit(solution)/shard_map/denoise/pallas_call | solution.py:372
  55.3 0.0 copy-start.2
  55.3 0.0 copy-start.10
  55.3 0.7 collective-permute-start.4
  56.0 2.6 %collective-permute-start.5 = (f32[3,8,16,128]{3,2,1,0:T(8,128)S(1)}, f32[3,8,16,128]{3,2,1,0:T(8,128)S(1)}, u32[]{:S(2)}, u32[]{:S(2)}) collective-permute-start(f32[3,8,16,128]{3,2,1,0:T(8,128)S(1)} %get-tuple-element.24), channel_id=1, source_target_pairs={{0,2},{1,3},{2,0},{3,1},{4,6},{5,7},{6,4},{7,5},{8,10},{9,11},{10,... | collective-permute-start | bytes 589832 | tf_op jit(solution)/shard_map/ppermute | solution.py:296
  58.6 2.3 %collective-permute-start.6 = (f32[3,8,16,128]{3,2,1,0:T(8,128)S(1)}, f32[3,8,16,128]{3,2,1,0:T(8,128)S(1)}, u32[]{:S(2)}, u32[]{:S(2)}) collective-permute-start(f32[3,8,16,128]{3,2,1,0:T(8,128)S(1)} %get-tuple-element.25), channel_id=1, source_target_pairs={{0,3},{1,0},{2,1},{3,2},{4,7},{5,4},{6,5},{7,6},{8,11},{9,8},{10,9... | collective-permute-start | bytes 589832 | tf_op jit(solution)/shard_map/ppermute | solution.py:296
  60.9 0.0 all-to-all-done
  60.9 1.4 %combine.1 = f32[256,128]{1,0:T(8,128)} custom-call(f32[512,128]{1,0:T(8,128)S(1)} %bitcast.7), custom_call_target="tpu_custom_call" | custom-call | tf_op jit(solution)/shard_map/combine/pallas_call | solution.py:363
  62.3 12.1 %all-to-all-start.1 = ((f32[256,1,128]{2,1,0:T(1,128)}), f32[256,1,128]{2,1,0:T(1,128)S(1)}, u32[]{:S(2)}, u32[]{:S(2)}) async-start(f32[256,1,128]{2,1,0:T(1,128)} %bitcast.4), calls=%async_computation.1 | async-start | bytes 262144 | tf_op jit(solution)/shard_map/all_to_all | solution.py:384
  74.5 0.0 collective-permute-done.4
  74.5 2.1 %collective-permute-done.5 = f32[3,8,16,128]{3,2,1,0:T(8,128)S(1)} collective-permute-done((f32[3,8,16,128]{3,2,1,0:T(8,128)S(1)}, f32[3,8,16,128]{3,2,1,0:T(8,128)S(1)}, u32[]{:S(2)}, u32[]{:S(2)}) %collective-permute-start.5) | collective-permute-done | bytes 196640 | tf_op jit(solution)/shard_map/ppermute | solution.py:296
  76.6 0.0 collective-permute-done.6
  76.6 0.1 add_add_fusion.net_ref
  76.7 0.1 collective-permute-start.7
  76.7 3.1 %collective-permute-done.7.prev_ref = f32[2,8,16,128]{3,2,1,0:T(8,128)S(1)} collective-permute-done((f32[2,8,16,128]{3,2,1,0:T(8,128)S(1)}, f32[2,8,16,128]{3,2,1,0:T(8,128)S(1)}, u32[]{:S(2)}, u32[]{:S(2)}) %collective-permute-start.7) | collective-permute-done | bytes 131104 | tf_op jit(solution)/shard_map/ppermute | solution.py:296
  79.9 7.4 %all-to-all-done.1 = f32[256,1,128]{2,1,0:T(1,128)S(1)} async-done(((f32[256,1,128]{2,1,0:T(1,128)}), f32[256,1,128]{2,1,0:T(1,128)S(1)}, u32[]{:S(2)}, u32[]{:S(2)}) %all-to-all-start.1) | async-done | bytes 131104 | tf_op jit(solution)/shard_map/all_to_all | solution.py:384
  87.3 0.0 copy-done.2
  87.3 0.0 copy-done.10
  87.3 3.9 %finish.1 = (f32[4,1,16,16,64]{4,3,2,1,0:T(8,128)}, f32[1,16,16,64]{3,2,1,0:T(8,128)}) custom-call(s32[3]{0:T(128)S(1)} %copy-done.9, f32[4]{0:T(128)S(1)} %copy-done.10, f32[4,1,16,16,64]{4,3,2,1,0:T(8,128)S(1)} %copy-done.2, f32[16,1024]{1,0:T(8,128)S(1)} %get-tuple-element.14.u_ref, s32[16,1024]{1,0:T(8,128)S(1)} %get-tuple-element.15.rel_ref, ...), custom_call_target="tpu_custom_call" | custom-call | tf_op jit(solution)/shard_map/finish/pallas_call | solution.py:388
  (1 shorter events, 0.0 us)
Async XLA Ops:
  0.6 1.0 %copy-start = (f32[4,1,16,16,64]{4,3,2,1,0:T(8,128)S(1)}, f32[4,1,16,16,64]{4,3,2,1,0:T(8,128)}, u32[]{:S(2)}) copy-start(f32[4,1,16,16,64]{4,3,2,1,0:T(8,128)} %state_ref.5) | copy-start | bytes 786436
  1.7 44.5 %copy-start.9 = (s32[3]{0:T(128)S(1)}, s32[3]{0:T(128)}, u32[]{:S(2)}) copy-start(s32[3]{0:T(128)} %offset_ref.5) | copy-start | bytes 40
  1.8 10.9 %collective-permute-start = (bf16[2,8,16,128]{3,2,1,0:T(8,128)(2,1)S(1)}, bf16[2,8,16,128]{3,2,1,0:T(8,128)(2,1)S(1)}, u32[]{:S(2)}, u32[]{:S(2)}) collective-permute-start(bf16[2,8,16,128]{3,2,1,0:T(8,128)(2,1)S(1)} %get-tuple-element.17.head_ref), channel_id=1, source_target_pairs={{0,252},{4,0},{8,4},{12,8},{16,12},{20,16},{24,20},{28,24},{32,28}... | collective-permute-start | bytes 196616 | tf_op jit(solution)/shard_map/ppermute | solution.py:296
  5.1 1.0 %copy-start.1 = (f32[4,1,16,16,64]{4,3,2,1,0:T(8,128)S(1)}, f32[4,1,16,16,64]{4,3,2,1,0:T(8,128)}, u32[]{:S(2)}) copy-start(f32[4,1,16,16,64]{4,3,2,1,0:T(8,128)} %state_ref.5) | copy-start | bytes 786436
  6.1 0.9 copy-start.5
  7.0 0.9 copy-start.6
  7.9 0.7 copy-start.7
  8.6 37.5 %copy-start.3 = (bf16[3,256,1024]{2,1,0:T(8,128)(2,1)S(1)}, bf16[3,256,1024]{2,1,0:T(8,128)(2,1)}, u32[]{:S(2)}) copy-start(bf16[3,256,1024]{2,1,0:T(8,128)(2,1)} %up_ref.1) | copy-start | bytes 4718596
  12.7 0.7 copy-start.8
  13.9 47.0 %all-to-all-start = ((f32[256,2,128]{2,1,0:T(2,128)}), f32[256,2,128]{2,1,0:T(2,128)S(1)}, u32[]{:S(2)}, u32[]{:S(2)}) async-start(f32[256,2,128]{2,1,0:T(2,128)} %bitcast.1), calls=%async_computation | async-start | bytes 524288 | tf_op jit(solution)/shard_map/all_to_all | solution.py:362
  26.8 13.0 %collective-permute-start.3 = (bf16[3,8,16,128]{3,2,1,0:T(8,128)(2,1)S(1)}, bf16[3,8,16,128]{3,2,1,0:T(8,128)(2,1)S(1)}, u32[]{:S(2)}, u32[]{:S(2)}) collective-permute-start(bf16[3,8,16,128]{3,2,1,0:T(8,128)(2,1)S(1)} %shift.1.p0), channel_id=1, source_target_pairs={{0,1},{1,2},{2,3},{3,0},{4,5},{5,6},{6,7},{7,4},{8,9},{9,10},{10,1... | collective-permute-start | bytes 294920 | tf_op jit(solution)/shard_map/ppermute | solution.py:296
  29.5 16.6 %collective-permute-start.2 = (bf16[3,8,16,128]{3,2,1,0:T(8,128)(2,1)S(1)}, bf16[3,8,16,128]{3,2,1,0:T(8,128)(2,1)S(1)}, u32[]{:S(2)}, u32[]{:S(2)}) collective-permute-start(bf16[3,8,16,128]{3,2,1,0:T(8,128)(2,1)S(1)} %shift.1.p0), channel_id=1, source_target_pairs={{0,2},{1,3},{2,0},{3,1},{4,6},{5,7},{6,4},{7,5},{8,10},{9,11},{10,... | collective-permute-start | bytes 294920 | tf_op jit(solution)/shard_map/ppermute | solution.py:296
  33.9 12.2 %collective-permute-start.1 = (bf16[3,8,16,128]{3,2,1,0:T(8,128)(2,1)S(1)}, bf16[3,8,16,128]{3,2,1,0:T(8,128)(2,1)S(1)}, u32[]{:S(2)}, u32[]{:S(2)}) collective-permute-start(bf16[3,8,16,128]{3,2,1,0:T(8,128)(2,1)S(1)} %shift.1.p0), channel_id=1, source_target_pairs={{0,3},{1,0},{2,1},{3,2},{4,7},{5,4},{6,5},{7,6},{8,11},{9,8},{10,9... | collective-permute-start | bytes 294920 | tf_op jit(solution)/shard_map/ppermute | solution.py:296
  46.1 1.4 %copy-start.4 = (bf16[3,1024,256]{2,1,0:T(8,128)(2,1)S(1)}, bf16[3,1024,256]{2,1,0:T(8,128)(2,1)}, u32[]{:S(2)}) copy-start(bf16[3,1024,256]{2,1,0:T(8,128)(2,1)} %down_ref.1) | copy-start | bytes 4718596
  55.3 32.0 %copy-start.2 = (f32[4,1,16,16,64]{4,3,2,1,0:T(8,128)S(1)}, f32[4,1,16,16,64]{4,3,2,1,0:T(8,128)}, u32[]{:S(2)}) copy-start(f32[4,1,16,16,64]{4,3,2,1,0:T(8,128)} %state_ref.5) | copy-start | bytes 786436
  55.3 32.0 %copy-start.10 = (f32[4]{0:T(128)S(1)}, f32[4]{0:T(128)}, u32[]{:S(2)}) copy-start(f32[4]{0:T(128)} %weight_ref.1) | copy-start | bytes 52
  55.3 19.2 %collective-permute-start.4 = (f32[3,8,16,128]{3,2,1,0:T(8,128)S(1)}, f32[3,8,16,128]{3,2,1,0:T(8,128)S(1)}, u32[]{:S(2)}, u32[]{:S(2)}) collective-permute-start(f32[3,8,16,128]{3,2,1,0:T(8,128)S(1)} %get-tuple-element.23), channel_id=1, source_target_pairs={{0,1},{1,2},{2,3},{3,0},{4,5},{5,6},{6,7},{7,4},{8,9},{9,10},{10,1... | collective-permute-start | bytes 589832 | tf_op jit(solution)/shard_map/ppermute | solution.py:296
  56.0 20.6 %collective-permute-start.5 = (f32[3,8,16,128]{3,2,1,0:T(8,128)S(1)}, f32[3,8,16,128]{3,2,1,0:T(8,128)S(1)}, u32[]{:S(2)}, u32[]{:S(2)}) collective-permute-start(f32[3,8,16,128]{3,2,1,0:T(8,128)S(1)} %get-tuple-element.24), channel_id=1, source_target_pairs={{0,2},{1,3},{2,0},{3,1},{4,6},{5,7},{6,4},{7,5},{8,10},{9,11},{10,... | collective-permute-start | bytes 589832 | tf_op jit(solution)/shard_map/ppermute | solution.py:296
  58.6 17.9 %collective-permute-start.6 = (f32[3,8,16,128]{3,2,1,0:T(8,128)S(1)}, f32[3,8,16,128]{3,2,1,0:T(8,128)S(1)}, u32[]{:S(2)}, u32[]{:S(2)}) collective-permute-start(f32[3,8,16,128]{3,2,1,0:T(8,128)S(1)} %get-tuple-element.25), channel_id=1, source_target_pairs={{0,3},{1,0},{2,1},{3,2},{4,7},{5,4},{6,5},{7,6},{8,11},{9,8},{10,9... | collective-permute-start | bytes 589832 | tf_op jit(solution)/shard_map/ppermute | solution.py:296
  62.3 24.9 %all-to-all-start.1 = ((f32[256,1,128]{2,1,0:T(1,128)}), f32[256,1,128]{2,1,0:T(1,128)S(1)}, u32[]{:S(2)}, u32[]{:S(2)}) async-start(f32[256,1,128]{2,1,0:T(1,128)} %bitcast.4), calls=%async_computation.1 | async-start | bytes 262144 | tf_op jit(solution)/shard_map/all_to_all | solution.py:384
  76.7 3.2 %collective-permute-start.7 = (f32[2,8,16,128]{3,2,1,0:T(8,128)S(1)}, f32[2,8,16,128]{3,2,1,0:T(8,128)S(1)}, u32[]{:S(2)}, u32[]{:S(2)}) collective-permute-start(f32[2,8,16,128]{3,2,1,0:T(8,128)S(1)} %slice.4), channel_id=1, source_target_pairs={{0,4},{4,8},{8,12},{12,16},{16,20},{20,24},{24,28},{28,32},{32,36}... | collective-permute-start | bytes 393224 | tf_op jit(solution)/shard_map/ppermute | solution.py:296

commit v4 on v3

--- a/solution.py
+++ b/solution.py
@@ -30,23 +30,34 @@
 
 
 def project_kernel(
-    group_ref, state_ref, bin_ref, num_ref, meas_ref, out_ref, u_ref, rel_ref, w_ref, start_ref
+    group_ref, state_hbm, bin_hbm, num_hbm, meas_hbm, out_ref, u_ref, rel_ref, w_ref, start_ref,
+    state_ref, bin_ref, num_ref, meas_ref, sems,
 ):
+    loads = [
+        pltpu.make_async_copy(state_hbm.at[0, 0], state_ref, sems.at[0]),
+        pltpu.make_async_copy(bin_hbm, bin_ref, sems.at[1]),
+        pltpu.make_async_copy(num_hbm, num_ref, sems.at[2]),
+        pltpu.make_async_copy(meas_hbm.at[0], meas_ref, sems.at[3]),
+    ]
+    for load in loads:
+        load.start()
+    out_ref[...] = jnp.zeros_like(out_ref)
+    for load in loads:
+        load.wait()
     angles, rows, cols = bin_ref.shape
-    planes = state_ref.shape[2]
+    planes = state_ref.shape[0]
     for x in range(rows):
         span = slice(x * cols, (x + 1) * cols)
-        u_ref[:, span] = state_ref[0, 0, :, x, :]
+        u_ref[:, span] = state_ref[:, x, :]
         rel_ref[:, span] = bin_ref[:, x, :]
         w_ref[:, span] = num_ref[:, x, :].astype(jnp.float32) * (1.0 / SCALE)
     low = rel_ref[...]
     start = window_starts(low)
     rel_ref[...] = low - start
     start_ref[...] = jnp.broadcast_to(start.astype(jnp.float32), (angles, WINDOW))
-    out_ref[...] = jnp.zeros_like(out_ref)
-    owned = meas_ref.shape[2]
+    owned = meas_ref.shape[1]
     mine = pl.multiple_of(group_ref[0] * (2 * planes), 2 * planes)
-    out_ref[pl.ds(mine + 1, planes, stride=2), :owned] = meas_ref[0]
+    out_ref[pl.ds(mine + 1, planes, stride=2), :owned] = meas_ref[...]
     lane = lax.broadcasted_iota(jnp.int32, (planes, WINDOW), 1)
 
     def body(a, carry):
@@ -121,24 +132,35 @@
     out_ref[...] = cut[:, :WINDOW] + cut[:, WINDOW:]
 
 
-def pack_kernel(state_ref, head_ref, tail_ref):
-    half = state_ref.shape[2] // 2
-    cols = state_ref.shape[4]
+def pack_kernel(offset_ref, state_hbm, keep_ref, send_ref, state_ref, sem):
+    load = pltpu.make_async_copy(state_hbm.at[pl.ds(1, 3), 0], state_ref, sem)
+    load.start()
+    load.wait()
+    half, rows, cols = state_ref.shape[1] // 2, state_ref.shape[2], state_ref.shape[3]
+    row = lax.broadcasted_iota(jnp.int32, (half, rows, cols), 1)
     for k in range(3):
-        out = head_ref.at[k] if k < 2 else tail_ref.at[0]
-        out[:, :, :cols] = state_ref[k + 1, 0, :half].astype(out.dtype)
-        out[:, :, cols:] = state_ref[k + 1, 0, half:].astype(out.dtype)
-
-
-def shift_kernel(offset_ref, head_ref, tail_ref, next_ref, out_ref):
-    rows = head_ref.shape[2]
-    for k in range(2):
-        o = offset_ref[k]
-        own = pltpu.roll(head_ref[k].astype(jnp.float32), rows - o, 1)
-        more = pltpu.roll(next_ref[k].astype(jnp.float32), rows - o, 1)
-        row = lax.broadcasted_iota(jnp.int32, own.shape, 1)
-        out_ref[k] = jnp.where(row < rows - o, own, more).astype(out_ref.dtype)
-    out_ref[2] = tail_ref[0]
+        for part in range(2):
+            block = state_ref[k, part * half : (part + 1) * half]
+            span = slice(part * cols, (part + 1) * cols)
+            if k == 2:
+                keep_ref[k, :, :, span] = block.astype(keep_ref.dtype)
+                continue
+            o = offset_ref[k]
+            block = pltpu.roll(block, rows - o, 1)
+            own = row < rows - o
+            keep_ref[k, :, :, span] = jnp.where(own, block, 0.0).astype(keep_ref.dtype)
+            send_ref[k, :, :, span] = jnp.where(own, 0.0, block).astype(send_ref.dtype)
+
+
+def shift_kernel(keep_ref, next_ref, out_ref):
+    out_ref[:2] = keep_ref[:2] + next_ref[...]
+    out_ref[2] = keep_ref[2]
+
+
+def add_kernel(p0, p1, p2, p3, head_ref, tail_ref):
+    total = p0[...] + p1[...] + p2[...] + p3[...]
+    head_ref[...] = total[:2]
+    tail_ref[...] = total[2:]
 
 
 def swap_slabs(slabs):
@@ -178,7 +200,16 @@
     return jnp.concatenate(halves, axis=0)
 
 
-def denoise_kernel(offset_ref, p0, p1, p2, p3, up_ref, down_ref, o0, o1, o2, o3):
+def denoise_kernel(
+    offset_ref, p0, p1, p2, p3, up_hbm, down_hbm, o0, o1, o2, o3, up_ref, down_ref, sems
+):
+    loads = []
+    for k in range(3):
+        up = pltpu.make_async_copy(up_hbm.at[k], up_ref.at[k], sems.at[k])
+        down = pltpu.make_async_copy(down_hbm.at[k], down_ref.at[k], sems.at[3 + k])
+        up.start()
+        down.start()
+        loads.append((up, down))
     side = PATCH
     size = side * side
     row = lax.broadcasted_iota(jnp.int32, (size, size), 0)
@@ -215,6 +246,8 @@
             halves = [jnp.where(inside, a, b), jnp.where(inside, b, a)]
         halves = [arrange(k, half) for half in halves]
         patches = jnp.concatenate([half.T for half in halves], axis=0).astype(jnp.bfloat16)
+        for load in loads[k]:
+            load.wait()
         down = down_ref[k]
         if k == 0:
             patches = jnp.dot(
@@ -239,10 +272,7 @@
             )
 
 
-def finish_kernel(
-    factor, offset_ref, weight_ref, state_ref, u_ref, rel_ref, w_ref, win_ref, net_ref, prev_ref,
-    next_ref, fit_ref,
-):
+def spread_kernel(factor, u_ref, rel_ref, w_ref, win_ref, fit_ref, copy_ref):
     angles, planes, _ = win_ref.shape
 
     def body(a, total):
@@ -261,16 +291,23 @@
     rows, cols = fit_ref.shape[2:]
     for x in range(rows):
         fit_ref[0, :, x, :] = fit[:, x * cols : (x + 1) * cols]
-
+    copy_ref[...] = fit_ref[...]
+
+
+def join_kernel(
+    offset_ref, weight_ref, state_ref, fit_ref, head_ref, tail_ref, prev_ref, next_ref
+):
+    planes, _, cols = fit_ref.shape[1:]
     raw = [jnp.full((1, cols), weight_ref[i], jnp.float32) for i in range(4)]
     whole = raw[0] + raw[1] + raw[2] + raw[3]
     share = [value / whole for value in raw]
-    row = lax.broadcasted_iota(jnp.int32, net_ref.shape[1:], 1)
+    row = lax.broadcasted_iota(jnp.int32, tail_ref.shape[1:], 1)
     nets = []
     for k in range(3):
-        net = net_ref[k]
-        if k < 2:
-            o = offset_ref[k]
+        if k == 2:
+            net = tail_ref[0]
+        else:
+            net, o = head_ref[k], offset_ref[k]
             net = jnp.where(row >= o, pltpu.roll(net, o, 1), pltpu.roll(prev_ref[k], o, 1))
         nets.append((net[:, :, :cols], pltpu.roll(net, WINDOW - cols, 2)[:, :, :cols]))
     count = planes // 2
@@ -288,7 +325,12 @@
 
 VMEM = pl.BlockSpec(memory_space=pltpu.VMEM)
 PARAMS = pltpu.CompilerParams(vmem_limit_bytes=20 * 1024 * 1024)
+HBM = pl.BlockSpec(memory_space=pltpu.HBM)
 SMEM = pl.BlockSpec(memory_space=pltpu.SMEM)
+
+
+def cost(micros):
+    return pl.CostEstimate(flops=micros * 10**9, bytes_accessed=micros * 3 * 10**6, transcendentals=0)
 
 
 def hop(value, axis, step):
@@ -309,18 +351,23 @@
     f32 = jnp.float32
 
     shape = (planes // 2, row_count, 2 * col_count)
-    head, tail = pl.pallas_call(
+    keep, sent = pl.pallas_call(
         pack_kernel,
         out_shape=[
+            jax.ShapeDtypeStruct((3,) + shape, jnp.bfloat16),
             jax.ShapeDtypeStruct((2,) + shape, jnp.bfloat16),
-            jax.ShapeDtypeStruct((1,) + shape, jnp.bfloat16),
-        ],
-        in_specs=[VMEM],
+        ],
+        in_specs=[SMEM, HBM],
         out_specs=[VMEM] * 2,
-        compiler_params=PARAMS,
+        scratch_shapes=[
+            pltpu.VMEM((3,) + agent_state.shape[2:], f32),
+            pltpu.SemaphoreType.DMA(()),
+        ],
+        compiler_params=pltpu.CompilerParams(vmem_limit_bytes=56050000),
+        cost_estimate=cost(2),
         name="pack",
-    )(agent_state)
-    following = hop(head, "tile", -1)
+    )(patch_offsets, agent_state)
+    following = hop(sent, "tile", -1)
 
     group = (lax.axis_index("tile") * agent_count // planes).astype(jnp.int32)
     pieces, flat, rel, near = pl.pallas_call(
@@ -331,29 +378,30 @@
             jax.ShapeDtypeStruct((angles, pixels), jnp.int32),
             jax.ShapeDtypeStruct((angles, pixels), f32),
         ],
-        grid=(1,),
-        in_specs=[
-            SMEM,
-            pl.BlockSpec((1,) + agent_state.shape[1:], lambda i: (0, 0, 0, 0, 0)),
-            VMEM,
-            VMEM,
-            VMEM,
-        ],
+        in_specs=[SMEM] + [HBM] * 4,
         out_specs=[VMEM] * 4,
-        scratch_shapes=[pltpu.VMEM((angles, WINDOW), f32)],
-        compiler_params=PARAMS,
+        scratch_shapes=[
+            pltpu.VMEM((angles, WINDOW), f32),
+            pltpu.VMEM(agent_state.shape[2:], f32),
+            pltpu.VMEM(bin_index.shape, jnp.int32),
+            pltpu.VMEM(bin_frac.shape, jnp.int32),
+            pltpu.VMEM(measured.shape[1:], f32),
+            pltpu.SemaphoreType.DMA((4,)),
+        ],
+        compiler_params=pltpu.CompilerParams(vmem_limit_bytes=56250000),
+        cost_estimate=cost(5),
         name="project",
     )(group.reshape(1), agent_state, bin_index, bin_frac, measured)
 
     region = pl.pallas_call(
         shift_kernel,
         out_shape=jax.ShapeDtypeStruct((3,) + shape, jnp.bfloat16),
-        in_specs=[SMEM, VMEM, VMEM, VMEM],
+        in_specs=[VMEM, VMEM],
         out_specs=VMEM,
         compiler_params=PARAMS,
+        cost_estimate=cost(1),
         name="shift",
-    )(patch_offsets, head, tail, following)
-    region, pieces = lax.optimization_barrier((region, pieces))
+    )(keep, following)
     others = []
     for step in range(1, agent_count):
         others.append(hop(region, "agent", -step))
@@ -366,39 +414,61 @@
         in_specs=[VMEM],
         out_specs=VMEM,
         compiler_params=PARAMS,
+        cost_estimate=cost(2),
         name="combine",
     )(got.reshape(2 * count, WINDOW))
 
+    back = lax.all_to_all(cut, both, 0, 0, tiled=True)
     parts = pl.pallas_call(
         denoise_kernel,
         out_shape=[jax.ShapeDtypeStruct((3,) + shape, f32)] * 4,
-        in_specs=[SMEM] + [VMEM] * 6,
+        in_specs=[SMEM] + [VMEM] * 4 + [HBM] * 2,
         out_specs=[VMEM] * 4,
-        compiler_params=PARAMS,
+        scratch_shapes=[
+            pltpu.VMEM(up_weight.shape, up_weight.dtype),
+            pltpu.VMEM(down_weight.shape, down_weight.dtype),
+            pltpu.SemaphoreType.DMA((6,)),
+        ],
+        compiler_params=pltpu.CompilerParams(vmem_limit_bytes=54500000),
+        cost_estimate=cost(6),
         name="denoise",
     )(patch_offsets, region, *others, up_weight, down_weight)
     arrived = []
     for step in range(1, agent_count):
         arrived.append(hop(parts[step], "agent", step))
 
-    back = lax.all_to_all(cut, both, 0, 0, tiled=True)
-    nets = parts[0] + arrived[0] + arrived[1] + arrived[2]
-    previous = hop(nets[:2], "tile", 1)
-
-    return pl.pallas_call(
-        functools.partial(finish_kernel, factor),
+    fit, held = pl.pallas_call(
+        functools.partial(spread_kernel, factor),
+        out_shape=[jax.ShapeDtypeStruct(agent_state.shape[1:], f32)] * 2,
+        in_specs=[VMEM] * 4,
+        out_specs=[VMEM] * 2,
+        compiler_params=PARAMS,
+        cost_estimate=cost(4),
+        name="spread",
+    )(flat, rel, near, back.reshape(angles, planes, WINDOW))
+    head, tail = pl.pallas_call(
+        add_kernel,
         out_shape=[
-            jax.ShapeDtypeStruct(agent_state.shape, f32),
-            jax.ShapeDtypeStruct(agent_state.shape[1:], f32),
-        ],
-        in_specs=[SMEM, SMEM] + [VMEM] * 7,
-        out_specs=[VMEM, VMEM],
+            jax.ShapeDtypeStruct((2,) + shape, f32),
+            jax.ShapeDtypeStruct((1,) + shape, f32),
+        ],
+        in_specs=[VMEM] * 4,
+        out_specs=[VMEM] * 2,
         compiler_params=PARAMS,
-        name="finish",
-    )(
-        patch_offsets, agent_weights, agent_state, flat, rel, near,
-        back.reshape(angles, planes, WINDOW), nets, previous,
-    )
+        cost_estimate=cost(1),
+        name="add",
+    )(parts[0], *arrived)
+    previous = hop(head, "tile", 1)
+    state_next = pl.pallas_call(
+        join_kernel,
+        out_shape=jax.ShapeDtypeStruct(agent_state.shape, f32),
+        in_specs=[SMEM, SMEM] + [VMEM] * 5,
+        out_specs=VMEM,
+        compiler_params=PARAMS,
+        cost_estimate=cost(2),
+        name="join",
+    )(patch_offsets, agent_weights, agent_state, held, head, tail, previous)
+    return (state_next, fit)
 
 
 def solution(mesh):

time: 91.6 us -> 80.9 us (0.88)
  local copies, waits for them, and re-layouts: 6.67 us -> 0.67 us
  waiting for transfers between devices: 22.1 us -> 16.9 us
    ppermute x8, waiting for transfers between devices: 14.7 us -> 7.35 us  [hop(): lax.ppermute(value, axis, [(i, (i + step) % count) for i in range(count)])]
    unnamed x22 -> x10, local copies, waits for them, and re-layouts: 6.66 us -> 0.67 us
    all_to_all x1, starting transfers between devices: 12.1 us -> 8.14 us  [step(): back = lax.all_to_all(cut, both, 0, 0, tiled=True)]
    ppermute x8, starting transfers between devices: 18.8 us -> 22.1 us  [hop(): lax.ppermute(value, axis, [(i, (i + step) % count) for i in range(count)])]
    pallas_call x1, Pallas kernels: 7.74 us -> 5.14 us  [step(): pl.pallas_call(denoise_kernel, out_shape=[jax.ShapeDtypeStruct((3,) + sha...]
    pallas_call x2 -> x4, Pallas kernels: 4.03 us -> 6.41 us  [the longest x1 3.17 us: step(): pl.pallas_call(functools.partial(spread_kernel, factor), out_shape=[jax.S...]
    all_to_all x1, waiting for transfers between devices: 7.41 us -> 8.76 us  [step(): back = lax.all_to_all(cut, both, 0, 0, tiled=True)]
    all_to_all x1, starting transfers between devices: 12.9 us -> 14.1 us  [step(): lax.all_to_all(pieces.reshape(count, 2, WINDOW), both, 0, 0, tiled=True)]
  transfers between devices with their start and end apart: 10 -> 10, of which waited for: 5 -> 4; matrix products, arithmetic and copies ran while one was open for 0% -> 0% of each run, Pallas kernels for 14% -> 18%
where the time goes in v4:
time: 80.9 us; the launch traced here: 80.7 us
  starting transfers between devices  44.3 us (55%)
  Pallas kernels  18.1 us (22%)
  waiting for transfers between devices  16.9 us (21%)
    ppermute x8, starting transfers between devices, hop(): lax.ppermute(value, axis, [(i, (i + step) % count) for i in range(count)])  22.1 us
    all_to_all x1, starting transfers between devices, step(): lax.all_to_all(pieces.reshape(count, 2, WINDOW), both, 0, 0, tiled=True)  14.1 us
    all_to_all x1, waiting for transfers between devices, step(): back = lax.all_to_all(cut, both, 0, 0, tiled=True)  8.76 us
    all_to_all x1, starting transfers between devices, step(): back = lax.all_to_all(cut, both, 0, 0, tiled=True)  8.14 us
    ppermute x8, waiting for transfers between devices, hop(): lax.ppermute(value, axis, [(i, (i + step) % count) for i in range(count)])  7.35 us
    pallas_call x1, Pallas kernels, step(): pl.pallas_call(denoise_kernel, out_shape=[jax.ShapeDtypeStruct((3,) + sha...  5.14 us
    pallas_call x1, Pallas kernels, step(): pl.pallas_call(project_kernel, out_shape=[jax.ShapeDtypeStruct((2 * angle...  5.11 us
    pallas_call x1, Pallas kernels, step(): pl.pallas_call(functools.partial(spread_kernel, factor), out_shape=[jax.S...  3.17 us
  transfers between devices with their start and end apart: 10, of which 4 were waited for; matrix products, arithmetic and copies ran while one was open for 0% of the time, Pallas kernels for 18%

profile of v4, /device:TPU:1, one launch (start us, length us, event | category | flops | bytes accessed | tf_op | source)
XLA Modules:
  0.0 80.7 jit_solution(2520104261101003638)
XLA Ops:
  0.6 0.0 copy-start.2
  0.6 0.6 copy-done.2
  1.3 1.7 %pack.1 = (bf16[3,8,16,128]{3,2,1,0:T(8,128)(2,1)S(1)}, bf16[2,8,16,128]{3,2,1,0:T(8,128)(2,1)S(1)}) custom-call(s32[3]{0:T(128)S(1)} %copy-done.2, f32[4,1,16,16,64]{4,3,2,1,0:T(8,128)} %state_ref.1), custom_call_target="tpu_custom_call" | custom-call | flops 2000000000 | bytes 6000000 | tf_op jit(solution)/shard_map/pack/pallas_call | solution.py:354
  3.0 3.3 %collective-permute-start = (bf16[2,8,16,128]{3,2,1,0:T(8,128)(2,1)S(1)}, bf16[2,8,16,128]{3,2,1,0:T(8,128)(2,1)S(1)}, u32[]{:S(2)}, u32[]{:S(2)}) collective-permute-start(bf16[2,8,16,128]{3,2,1,0:T(8,128)(2,1)S(1)} %get-tuple-element.22), channel_id=1, source_target_pairs={{0,252},{4,0},{8,4},{12,8},{16,12},{20,16},{24,20},{28,24},{32,28}... | collective-permute-start | bytes 196616 | tf_op jit(solution)/shard_map/ppermute | solution.py:338
  6.3 1.8 %collective-permute-done.next_ref = bf16[2,8,16,128]{3,2,1,0:T(8,128)(2,1)S(1)} collective-permute-done((bf16[2,8,16,128]{3,2,1,0:T(8,128)(2,1)S(1)}, bf16[2,8,16,128]{3,2,1,0:T(8,128)(2,1)S(1)}, u32[]{:S(2)}, u32[]{:S(2)}) %collective-permute-start) | collective-permute-done | bytes 65568 | tf_op jit(solution)/shard_map/ppermute | solution.py:338
  8.0 0.0 copy-start.1
  8.1 5.6 %collective-permute-start.1 = (bf16[3,8,16,128]{3,2,1,0:T(8,128)(2,1)S(1)}, bf16[3,8,16,128]{3,2,1,0:T(8,128)(2,1)S(1)}, u32[]{:S(2)}, u32[]{:S(2)}) collective-permute-start(bf16[3,8,16,128]{3,2,1,0:T(8,128)(2,1)S(1)} %shift.1.p0), channel_id=1, source_target_pairs={{0,3},{1,0},{2,1},{3,2},{4,7},{5,4},{6,5},{7,6},{8,11},{9,8},{10,9... | collective-permute-start | bytes 294920 | tf_op jit(solution)/shard_map/ppermute | solution.py:338
  13.7 1.0 %collective-permute-start.2 = (bf16[3,8,16,128]{3,2,1,0:T(8,128)(2,1)S(1)}, bf16[3,8,16,128]{3,2,1,0:T(8,128)(2,1)S(1)}, u32[]{:S(2)}, u32[]{:S(2)}) collective-permute-start(bf16[3,8,16,128]{3,2,1,0:T(8,128)(2,1)S(1)} %shift.1.p0), channel_id=1, source_target_pairs={{0,2},{1,3},{2,0},{3,1},{4,6},{5,7},{6,4},{7,5},{8,10},{9,11},{10,... | collective-permute-start | bytes 294920 | tf_op jit(solution)/shard_map/ppermute | solution.py:338
  14.7 2.3 %collective-permute-start.3 = (bf16[3,8,16,128]{3,2,1,0:T(8,128)(2,1)S(1)}, bf16[3,8,16,128]{3,2,1,0:T(8,128)(2,1)S(1)}, u32[]{:S(2)}, u32[]{:S(2)}) collective-permute-start(bf16[3,8,16,128]{3,2,1,0:T(8,128)(2,1)S(1)} %shift.1.p0), channel_id=1, source_target_pairs={{0,1},{1,2},{2,3},{3,0},{4,5},{5,6},{6,7},{7,4},{8,9},{9,10},{10,1... | collective-permute-start | bytes 294920 | tf_op jit(solution)/shard_map/ppermute | solution.py:338
  17.0 0.0 copy-done.1
  17.0 0.0 copy-start.3
  17.0 5.1 %project.1 = (f32[512,128]{1,0:T(8,128)}, f32[16,1024]{1,0:T(8,128)S(1)}, s32[16,1024]{1,0:T(8,128)S(1)}, f32[16,1024]{1,0:T(8,128)S(1)}) custom-call(s32[1]{0:T(128)} %bitcast.group_ref, f32[4,1,16,16,64]{4,3,2,1,0:T(8,128)} %state_ref.1, s32[16,16,64]{2,1,0:T(8,128)} %bin_hbm.1, s32[16,16,64]{2,1,0:T(8,128)} %num_hbm.1, f32[1,16,88]{2,1,0:T(8,128)S(1)} %copy-done.1), custom_call_target="tpu_custom_call" | custom-call | flops 5000000000 | bytes 15000000 | tf_op jit(solution)/shard_map/project/pallas_call | solution.py:373
  22.1 14.1 %all-to-all-start = ((f32[256,2,128]{2,1,0:T(2,128)}), f32[256,2,128]{2,1,0:T(2,128)S(1)}, u32[]{:S(2)}, u32[]{:S(2)}) async-start(f32[256,2,128]{2,1,0:T(2,128)} %bitcast.9), calls=%async_computation | async-start | bytes 524288 | tf_op jit(solution)/shard_map/all_to_all | solution.py:410
  36.1 0.0 collective-permute-done.1.p1
  36.2 0.0 collective-permute-done.2.p2
  36.2 0.0 collective-permute-done.3.p3
  36.2 0.0 copy-done.3
  36.2 5.1 %denoise.1 = (f32[3,8,16,128]{3,2,1,0:T(8,128)S(1)}, f32[3,8,16,128]{3,2,1,0:T(8,128)S(1)}, f32[3,8,16,128]{3,2,1,0:T(8,128)S(1)}, f32[3,8,16,128]{3,2,1,0:T(8,128)S(1)}) custom-call(s32[3]{0:T(128)S(1)} %copy-done.3, bf16[3,8,16,128]{3,2,1,0:T(8,128)(2,1)S(1)} %shift.1.p0, bf16[3,8,16,128]{3,2,1,0:T(8,128)(2,1)S(1)} %collective-permute-done.1.p1, ...), custom_call_target="tpu_custom_call" | custom-call | flops 6000000000 | bytes 18000000 | tf_op jit(solution)/shard_map/denoise/pallas_call | solution.py:422
  41.3 2.7 %collective-permute-start.4 = (f32[3,8,16,128]{3,2,1,0:T(8,128)S(1)}, f32[3,8,16,128]{3,2,1,0:T(8,128)S(1)}, u32[]{:S(2)}, u32[]{:S(2)}) collective-permute-start(f32[3,8,16,128]{3,2,1,0:T(8,128)S(1)} %get-tuple-element.24), channel_id=1, source_target_pairs={{0,1},{1,2},{2,3},{3,0},{4,5},{5,6},{6,7},{7,4},{8,9},{9,10},{10,1... | collective-permute-start | bytes 589832 | tf_op jit(solution)/shard_map/ppermute | solution.py:338
  44.1 4.4 %collective-permute-start.5 = (f32[3,8,16,128]{3,2,1,0:T(8,128)S(1)}, f32[3,8,16,128]{3,2,1,0:T(8,128)S(1)}, u32[]{:S(2)}, u32[]{:S(2)}) collective-permute-start(f32[3,8,16,128]{3,2,1,0:T(8,128)S(1)} %get-tuple-element.25), channel_id=1, source_target_pairs={{0,2},{1,3},{2,0},{3,1},{4,6},{5,7},{6,4},{7,5},{8,10},{9,11},{10,... | collective-permute-start | bytes 589832 | tf_op jit(solution)/shard_map/ppermute | solution.py:338
  48.4 2.8 %collective-permute-start.6 = (f32[3,8,16,128]{3,2,1,0:T(8,128)S(1)}, f32[3,8,16,128]{3,2,1,0:T(8,128)S(1)}, u32[]{:S(2)}, u32[]{:S(2)}) collective-permute-start(f32[3,8,16,128]{3,2,1,0:T(8,128)S(1)} %get-tuple-element.26), channel_id=1, source_target_pairs={{0,3},{1,0},{2,1},{3,2},{4,7},{5,4},{6,5},{7,6},{8,11},{9,8},{10,9... | collective-permute-start | bytes 589832 | tf_op jit(solution)/shard_map/ppermute | solution.py:338
  51.2 0.8 all-to-all-done
  52.0 1.4 %combine.1 = f32[256,128]{1,0:T(8,128)} custom-call(f32[512,128]{1,0:T(8,128)S(1)} %bitcast.7), custom_call_target="tpu_custom_call" | custom-call | flops 2000000000 | bytes 6000000 | tf_op jit(solution)/shard_map/combine/pallas_call | solution.py:411
  53.4 8.1 %all-to-all-start.1 = ((f32[256,1,128]{2,1,0:T(1,128)}), f32[256,1,128]{2,1,0:T(1,128)S(1)}, u32[]{:S(2)}, u32[]{:S(2)}) async-start(f32[256,1,128]{2,1,0:T(1,128)} %bitcast.4), calls=%async_computation.1 | async-start | bytes 262144 | tf_op jit(solution)/shard_map/all_to_all | solution.py:421
  61.5 0.0 collective-permute-done.4.p1
  61.5 0.0 collective-permute-done.5.p2
  61.5 5.6 %collective-permute-done.6.p3 = f32[3,8,16,128]{3,2,1,0:T(8,128)S(1)} collective-permute-done((f32[3,8,16,128]{3,2,1,0:T(8,128)S(1)}, f32[3,8,16,128]{3,2,1,0:T(8,128)S(1)}, u32[]{:S(2)}, u32[]{:S(2)}) %collective-permute-start.6) | collective-permute-done | bytes 196640 | tf_op jit(solution)/shard_map/ppermute | solution.py:338
  67.2 0.1 collective-permute-start.7
  67.2 8.8 %all-to-all-done.1 = f32[256,1,128]{2,1,0:T(1,128)S(1)} async-done(((f32[256,1,128]{2,1,0:T(1,128)}), f32[256,1,128]{2,1,0:T(1,128)S(1)}, u32[]{:S(2)}, u32[]{:S(2)}) %all-to-all-start.1) | async-done | bytes 131104 | tf_op jit(solution)/shard_map/all_to_all | solution.py:421
  76.0 0.0 copy-start
  76.0 0.0 copy-start.4
  76.0 3.2 %spread.1 = (f32[1,16,16,64]{3,2,1,0:T(8,128)}, f32[1,16,16,64]{3,2,1,0:T(8,128)S(1)}) custom-call(f32[16,1024]{1,0:T(8,128)S(1)} %get-tuple-element.16.u_ref, s32[16,1024]{1,0:T(8,128)S(1)} %get-tuple-element.17.rel_ref, f32[16,1024]{1,0:T(8,128)S(1)} %get-tuple-element.18.w_ref, f32[16,16,128]{2,1,0:T(8,128)S(1)} %bitcast.8), custom_call_target="tpu_custom_call" | custom-call | flops 4000000000 | bytes 12000000 | tf_op jit(solution)/shard_map/spread/pallas_call | solution.py:440
  79.2 0.0 collective-permute-done.7.prev_ref
  79.2 0.0 copy-done
  79.2 0.0 copy-done.4
  79.2 1.5 %join.1 = f32[4,1,16,16,64]{4,3,2,1,0:T(8,128)} custom-call(s32[3]{0:T(128)S(1)} %copy-done.3, f32[4]{0:T(128)S(1)} %copy-done.4, f32[4,1,16,16,64]{4,3,2,1,0:T(8,128)S(1)} %copy-done, f32[1,16,16,64]{3,2,1,0:T(8,128)S(1)} %get-tuple-element.20.fit_ref, f32[2,8,16,128]{3,2,1,0:T(8,128)S(1)} %get-tuple-element.27.head_ref, ...), custom_call_target="tpu_custom_call" | custom-call | flops 2000000000 | bytes 6000000 | tf_op jit(solution)/shard_map/join/pallas_call | solution.py:462
  (2 shorter events, 0.1 us)
Async XLA Ops:
  0.6 0.7 copy-start.2
  3.0 5.0 %collective-permute-start = (bf16[2,8,16,128]{3,2,1,0:T(8,128)(2,1)S(1)}, bf16[2,8,16,128]{3,2,1,0:T(8,128)(2,1)S(1)}, u32[]{:S(2)}, u32[]{:S(2)}) collective-permute-start(bf16[2,8,16,128]{3,2,1,0:T(8,128)(2,1)S(1)} %get-tuple-element.22), channel_id=1, source_target_pairs={{0,252},{4,0},{8,4},{12,8},{16,12},{20,16},{24,20},{28,24},{32,28}... | collective-permute-start | bytes 196616 | tf_op jit(solution)/shard_map/ppermute | solution.py:338
  8.0 8.9 %copy-start.1 = (f32[1,16,88]{2,1,0:T(8,128)S(1)}, f32[1,16,88]{2,1,0:T(8,128)}, u32[]{:S(2)}) copy-start(f32[1,16,88]{2,1,0:T(8,128)} %meas_hbm.1) | copy-start | bytes 16900
  8.1 28.1 %collective-permute-start.1 = (bf16[3,8,16,128]{3,2,1,0:T(8,128)(2,1)S(1)}, bf16[3,8,16,128]{3,2,1,0:T(8,128)(2,1)S(1)}, u32[]{:S(2)}, u32[]{:S(2)}) collective-permute-start(bf16[3,8,16,128]{3,2,1,0:T(8,128)(2,1)S(1)} %shift.1.p0), channel_id=1, source_target_pairs={{0,3},{1,0},{2,1},{3,2},{4,7},{5,4},{6,5},{7,6},{8,11},{9,8},{10,9... | collective-permute-start | bytes 294920 | tf_op jit(solution)/shard_map/ppermute | solution.py:338
  13.7 22.5 %collective-permute-start.2 = (bf16[3,8,16,128]{3,2,1,0:T(8,128)(2,1)S(1)}, bf16[3,8,16,128]{3,2,1,0:T(8,128)(2,1)S(1)}, u32[]{:S(2)}, u32[]{:S(2)}) collective-permute-start(bf16[3,8,16,128]{3,2,1,0:T(8,128)(2,1)S(1)} %shift.1.p0), channel_id=1, source_target_pairs={{0,2},{1,3},{2,0},{3,1},{4,6},{5,7},{6,4},{7,5},{8,10},{9,11},{10,... | collective-permute-start | bytes 294920 | tf_op jit(solution)/shard_map/ppermute | solution.py:338
  14.7 21.5 %collective-permute-start.3 = (bf16[3,8,16,128]{3,2,1,0:T(8,128)(2,1)S(1)}, bf16[3,8,16,128]{3,2,1,0:T(8,128)(2,1)S(1)}, u32[]{:S(2)}, u32[]{:S(2)}) collective-permute-start(bf16[3,8,16,128]{3,2,1,0:T(8,128)(2,1)S(1)} %shift.1.p0), channel_id=1, source_target_pairs={{0,1},{1,2},{2,3},{3,0},{4,5},{5,6},{6,7},{7,4},{8,9},{9,10},{10,1... | collective-permute-start | bytes 294920 | tf_op jit(solution)/shard_map/ppermute | solution.py:338
  17.0 19.2 %copy-start.3 = (s32[3]{0:T(128)S(1)}, s32[3]{0:T(128)}, u32[]{:S(2)}) copy-start(s32[3]{0:T(128)} %offset_ref.5) | copy-start | bytes 40
  22.1 29.9 %all-to-all-start = ((f32[256,2,128]{2,1,0:T(2,128)}), f32[256,2,128]{2,1,0:T(2,128)S(1)}, u32[]{:S(2)}, u32[]{:S(2)}) async-start(f32[256,2,128]{2,1,0:T(2,128)} %bitcast.9), calls=%async_computation | async-start | bytes 524288 | tf_op jit(solution)/shard_map/all_to_all | solution.py:410
  41.3 20.2 %collective-permute-start.4 = (f32[3,8,16,128]{3,2,1,0:T(8,128)S(1)}, f32[3,8,16,128]{3,2,1,0:T(8,128)S(1)}, u32[]{:S(2)}, u32[]{:S(2)}) collective-permute-start(f32[3,8,16,128]{3,2,1,0:T(8,128)S(1)} %get-tuple-element.24), channel_id=1, source_target_pairs={{0,1},{1,2},{2,3},{3,0},{4,5},{5,6},{6,7},{7,4},{8,9},{9,10},{10,1... | collective-permute-start | bytes 589832 | tf_op jit(solution)/shard_map/ppermute | solution.py:338
  44.1 17.5 %collective-permute-start.5 = (f32[3,8,16,128]{3,2,1,0:T(8,128)S(1)}, f32[3,8,16,128]{3,2,1,0:T(8,128)S(1)}, u32[]{:S(2)}, u32[]{:S(2)}) collective-permute-start(f32[3,8,16,128]{3,2,1,0:T(8,128)S(1)} %get-tuple-element.25), channel_id=1, source_target_pairs={{0,2},{1,3},{2,0},{3,1},{4,6},{5,7},{6,4},{7,5},{8,10},{9,11},{10,... | collective-permute-start | bytes 589832 | tf_op jit(solution)/shard_map/ppermute | solution.py:338
  48.4 18.7 %collective-permute-start.6 = (f32[3,8,16,128]{3,2,1,0:T(8,128)S(1)}, f32[3,8,16,128]{3,2,1,0:T(8,128)S(1)}, u32[]{:S(2)}, u32[]{:S(2)}) collective-permute-start(f32[3,8,16,128]{3,2,1,0:T(8,128)S(1)} %get-tuple-element.26), channel_id=1, source_target_pairs={{0,3},{1,0},{2,1},{3,2},{4,7},{5,4},{6,5},{7,6},{8,11},{9,8},{10,9... | collective-permute-start | bytes 589832 | tf_op jit(solution)/shard_map/ppermute | solution.py:338
  53.4 22.6 %all-to-all-start.1 = ((f32[256,1,128]{2,1,0:T(1,128)}), f32[256,1,128]{2,1,0:T(1,128)S(1)}, u32[]{:S(2)}, u32[]{:S(2)}) async-start(f32[256,1,128]{2,1,0:T(1,128)} %bitcast.4), calls=%async_computation.1 | async-start | bytes 262144 | tf_op jit(solution)/shard_map/all_to_all | solution.py:421
  67.2 12.0 %collective-permute-start.7 = (f32[2,8,16,128]{3,2,1,0:T(8,128)S(1)}, f32[2,8,16,128]{3,2,1,0:T(8,128)S(1)}, u32[]{:S(2)}, u32[]{:S(2)}) collective-permute-start(f32[2,8,16,128]{3,2,1,0:T(8,128)S(1)} %get-tuple-element.27.head_ref), channel_id=1, source_target_pairs={{0,4},{4,8},{8,12},{12,16},{16,20},{20,24},{24,28},{28,32},{32,36}... | collective-permute-start | bytes 393224 | tf_op jit(solution)/shard_map/ppermute | solution.py:338
  76.0 3.2 %copy-start = (f32[4,1,16,16,64]{4,3,2,1,0:T(8,128)S(1)}, f32[4,1,16,16,64]{4,3,2,1,0:T(8,128)}, u32[]{:S(2)}) copy-start(f32[4,1,16,16,64]{4,3,2,1,0:T(8,128)} %state_ref.1) | copy-start | bytes 786436
  76.0 3.2 %copy-start.4 = (f32[4]{0:T(128)S(1)}, f32[4]{0:T(128)}, u32[]{:S(2)}) copy-start(f32[4]{0:T(128)} %weight_ref.1) | copy-start | bytes 52

commit v5 on v4

--- a/solution.py
+++ b/solution.py
@@ -13,6 +13,9 @@
 SCALE = 724
 WINDOW = 128
 ALIGN = 32
+WIRE = jnp.int16
+STEPS = 32700.0
+GRAIN = 128.0
 
 
 def split_two(value):
@@ -30,20 +33,9 @@
 
 
 def project_kernel(
-    group_ref, state_hbm, bin_hbm, num_hbm, meas_hbm, out_ref, u_ref, rel_ref, w_ref, start_ref,
-    state_ref, bin_ref, num_ref, meas_ref, sems,
+    group_ref, state_ref, bin_ref, num_ref, meas_ref, out_ref, u_ref, rel_ref, w_ref, start_ref
 ):
-    loads = [
-        pltpu.make_async_copy(state_hbm.at[0, 0], state_ref, sems.at[0]),
-        pltpu.make_async_copy(bin_hbm, bin_ref, sems.at[1]),
-        pltpu.make_async_copy(num_hbm, num_ref, sems.at[2]),
-        pltpu.make_async_copy(meas_hbm.at[0], meas_ref, sems.at[3]),
-    ]
-    for load in loads:
-        load.start()
     out_ref[...] = jnp.zeros_like(out_ref)
-    for load in loads:
-        load.wait()
     angles, rows, cols = bin_ref.shape
     planes = state_ref.shape[0]
     for x in range(rows):
@@ -55,9 +47,9 @@
     start = window_starts(low)
     rel_ref[...] = low - start
     start_ref[...] = jnp.broadcast_to(start.astype(jnp.float32), (angles, WINDOW))
-    owned = meas_ref.shape[1]
+    owned = meas_ref.shape[2]
     mine = pl.multiple_of(group_ref[0] * (2 * planes), 2 * planes)
-    out_ref[pl.ds(mine + 1, planes, stride=2), :owned] = meas_ref[...]
+    out_ref[pl.ds(mine + 1, planes, stride=2), :owned] = meas_ref[0]
     lane = lax.broadcasted_iota(jnp.int32, (planes, WINDOW), 1)
 
     def body(a, carry):
@@ -78,7 +70,7 @@
         out_ref[pl.ds(first, planes, stride=2), :] = piece
         return carry
 
-    lax.fori_loop(0, angles, body, 0, unroll=2)
+    lax.fori_loop(0, angles, body, 0, unroll=8)
 
 
 def combine_kernel(factor, owned, got_ref, out_ref):
@@ -132,35 +124,66 @@
     out_ref[...] = cut[:, :WINDOW] + cut[:, WINDOW:]
 
 
-def pack_kernel(offset_ref, state_hbm, keep_ref, send_ref, state_ref, sem):
-    load = pltpu.make_async_copy(state_hbm.at[pl.ds(1, 3), 0], state_ref, sem)
-    load.start()
+def pack_kernel(
+    state_hbm, bin_hbm, num_hbm, head_ref, tail_ref, first_ref, bin_ref, num_ref, state_ref, sems
+):
+    load = pltpu.make_async_copy(state_hbm.at[pl.ds(1, 3), 0], state_ref, sems.at[0])
+    ahead = [
+        pltpu.make_async_copy(state_hbm.at[0, 0], first_ref, sems.at[1]),
+        pltpu.make_async_copy(bin_hbm, bin_ref, sems.at[2]),
+        pltpu.make_async_copy(num_hbm, num_ref, sems.at[3]),
+    ]
+    for copy in [load] + ahead:
+        copy.start()
     load.wait()
-    half, rows, cols = state_ref.shape[1] // 2, state_ref.shape[2], state_ref.shape[3]
-    row = lax.broadcasted_iota(jnp.int32, (half, rows, cols), 1)
+    half, cols = state_ref.shape[1] // 2, state_ref.shape[3]
     for k in range(3):
+        out = head_ref.at[k] if k < 2 else tail_ref.at[0]
         for part in range(2):
             block = state_ref[k, part * half : (part + 1) * half]
-            span = slice(part * cols, (part + 1) * cols)
-            if k == 2:
-                keep_ref[k, :, :, span] = block.astype(keep_ref.dtype)
-                continue
-            o = offset_ref[k]
-            block = pltpu.roll(block, rows - o, 1)
-            own = row < rows - o
-            keep_ref[k, :, :, span] = jnp.where(own, block, 0.0).astype(keep_ref.dtype)
-            send_ref[k, :, :, span] = jnp.where(own, 0.0, block).astype(send_ref.dtype)
-
-
-def shift_kernel(keep_ref, next_ref, out_ref):
-    out_ref[:2] = keep_ref[:2] + next_ref[...]
-    out_ref[2] = keep_ref[2]
-
-
-def add_kernel(p0, p1, p2, p3, head_ref, tail_ref):
-    total = p0[...] + p1[...] + p2[...] + p3[...]
-    head_ref[...] = total[:2]
-    tail_ref[...] = total[2:]
+            out[:, :, part * cols : (part + 1) * cols] = block.astype(out.dtype)
+    for copy in ahead:
+        copy.wait()
+
+
+def shift_kernel(offset_ref, head_ref, tail_ref, next_ref, out_ref):
+    rows = head_ref.shape[2]
+    for k in range(2):
+        o = offset_ref[k]
+        own = pltpu.roll(head_ref[k].astype(jnp.float32), rows - o, 1)
+        more = pltpu.roll(next_ref[k].astype(jnp.float32), rows - o, 1)
+        row = lax.broadcasted_iota(jnp.int32, own.shape, 1)
+        out_ref[k] = jnp.where(row < rows - o, own, more).astype(out_ref.dtype)
+    out_ref[2] = tail_ref[0]
+
+
+def encode(block, out):
+    count = block.shape[0]
+    top = jnp.max(jnp.max(jnp.abs(block), axis=0), axis=0, keepdims=True)
+    level = jnp.ceil(jnp.log2(jnp.maximum(top, 1e-30)) * GRAIN)
+    scale = STEPS * jnp.exp2(level * (-1.0 / GRAIN))
+    out[:count] = jnp.round(block * scale[None]).astype(jnp.int32).astype(out.dtype)
+    level = jnp.broadcast_to(level, block.shape[1:])
+    out[count] = level.astype(jnp.int32).astype(out.dtype)
+
+
+def decode(held):
+    count = held.shape[0] - 1
+    level = held[count].astype(jnp.float32)[:1]
+    scale = (1.0 / STEPS) * jnp.exp2(level * (1.0 / GRAIN))
+    return held[:count].astype(jnp.float32) * scale[None]
+
+
+def halve_kernel(near_ref, got_ref, keep_ref, send_ref):
+    for k in range(3):
+        keep_ref[k] = near_ref[0, k] + decode(got_ref.at[0, k])
+        encode(near_ref[1, k] + decode(got_ref.at[1, k]), send_ref.at[k])
+
+
+def add_kernel(keep_ref, got_ref, head_ref, tail_ref):
+    for k in range(3):
+        out = head_ref.at[k] if k < 2 else tail_ref.at[0]
+        out[...] = keep_ref[k] + decode(got_ref.at[k])
 
 
 def swap_slabs(slabs):
@@ -201,7 +224,7 @@
 
 
 def denoise_kernel(
-    offset_ref, p0, p1, p2, p3, up_hbm, down_hbm, o0, o1, o2, o3, up_ref, down_ref, sems
+    offset_ref, p0, p1, p2, p3, up_hbm, down_hbm, near_ref, far_ref, up_ref, down_ref, sems
 ):
     loads = []
     for k in range(3):
@@ -262,14 +285,18 @@
             a, b = [pltpu.roll(half, o, 1) for half in halves]
             inside = wide >= o
             halves = [jnp.where(inside, a, b), jnp.where(inside, b, a)]
-        for half, first, second in ((halves[0], o0, o1), (halves[1], o2, o3)):
+        for half, near in ((halves[0], True), (halves[1], False)):
             early, late = half[: size // 2], half[size // 2 :]
-            first[k] = jnp.where(left, early, pltpu.roll(late, WINDOW // 2, 1)).reshape(
-                first.shape[1:]
+            blocks = (
+                jnp.where(left, early, pltpu.roll(late, WINDOW // 2, 1)),
+                jnp.where(left, pltpu.roll(early, WINDOW // 2, 1), late),
             )
-            second[k] = jnp.where(left, pltpu.roll(early, WINDOW // 2, 1), late).reshape(
-                second.shape[1:]
-            )
+            for j in range(2):
+                block = blocks[j].reshape(near_ref.shape[2:])
+                if near:
+                    near_ref[j, k] = block
+                else:
+                    encode(block, far_ref.at[j, k])
 
 
 def spread_kernel(factor, u_ref, rel_ref, w_ref, win_ref, fit_ref, copy_ref):
@@ -286,7 +313,7 @@
         w = w_ref[pl.ds(a, 1), :]
         return total + (far + w * (near - far))
 
-    total = lax.fori_loop(0, angles, body, jnp.zeros(u_ref.shape, jnp.float32), unroll=2)
+    total = lax.fori_loop(0, angles, body, jnp.zeros(u_ref.shape, jnp.float32), unroll=8)
     fit = u_ref[...] - factor * total
     rows, cols = fit_ref.shape[2:]
     for x in range(rows):
@@ -351,23 +378,27 @@
     f32 = jnp.float32
 
     shape = (planes // 2, row_count, 2 * col_count)
-    keep, sent = pl.pallas_call(
+    coded = (planes // 2 + 1, row_count, 2 * col_count)
+    head, tail, volume, bins, nums = pl.pallas_call(
         pack_kernel,
         out_shape=[
-            jax.ShapeDtypeStruct((3,) + shape, jnp.bfloat16),
             jax.ShapeDtypeStruct((2,) + shape, jnp.bfloat16),
-        ],
-        in_specs=[SMEM, HBM],
-        out_specs=[VMEM] * 2,
+            jax.ShapeDtypeStruct((1,) + shape, jnp.bfloat16),
+            jax.ShapeDtypeStruct(agent_state.shape[2:], f32),
+            jax.ShapeDtypeStruct(bin_index.shape, jnp.int32),
+            jax.ShapeDtypeStruct(bin_frac.shape, jnp.int32),
+        ],
+        in_specs=[HBM] * 3,
+        out_specs=[VMEM] * 5,
         scratch_shapes=[
             pltpu.VMEM((3,) + agent_state.shape[2:], f32),
-            pltpu.SemaphoreType.DMA(()),
-        ],
-        compiler_params=pltpu.CompilerParams(vmem_limit_bytes=56050000),
+            pltpu.SemaphoreType.DMA((4,)),
+        ],
+        compiler_params=pltpu.CompilerParams(vmem_limit_bytes=56000000),
         cost_estimate=cost(2),
         name="pack",
-    )(patch_offsets, agent_state)
-    following = hop(sent, "tile", -1)
+    )(agent_state, bin_index, bin_frac)
+    following = hop(head, "tile", -1)
 
     group = (lax.axis_index("tile") * agent_count // planes).astype(jnp.int32)
     pieces, flat, rel, near = pl.pallas_call(
@@ -378,30 +409,23 @@
             jax.ShapeDtypeStruct((angles, pixels), jnp.int32),
             jax.ShapeDtypeStruct((angles, pixels), f32),
         ],
-        in_specs=[SMEM] + [HBM] * 4,
+        in_specs=[SMEM] + [VMEM] * 4,
         out_specs=[VMEM] * 4,
-        scratch_shapes=[
-            pltpu.VMEM((angles, WINDOW), f32),
-            pltpu.VMEM(agent_state.shape[2:], f32),
-            pltpu.VMEM(bin_index.shape, jnp.int32),
-            pltpu.VMEM(bin_frac.shape, jnp.int32),
-            pltpu.VMEM(measured.shape[1:], f32),
-            pltpu.SemaphoreType.DMA((4,)),
-        ],
-        compiler_params=pltpu.CompilerParams(vmem_limit_bytes=56250000),
+        scratch_shapes=[pltpu.VMEM((angles, WINDOW), f32)],
+        compiler_params=PARAMS,
         cost_estimate=cost(5),
         name="project",
-    )(group.reshape(1), agent_state, bin_index, bin_frac, measured)
+    )(group.reshape(1), volume, bins, nums, measured)
 
     region = pl.pallas_call(
         shift_kernel,
         out_shape=jax.ShapeDtypeStruct((3,) + shape, jnp.bfloat16),
-        in_specs=[VMEM, VMEM],
+        in_specs=[SMEM, VMEM, VMEM, VMEM],
         out_specs=VMEM,
         compiler_params=PARAMS,
         cost_estimate=cost(1),
         name="shift",
-    )(keep, following)
+    )(patch_offsets, head, tail, following)
     others = []
     for step in range(1, agent_count):
         others.append(hop(region, "agent", -step))
@@ -419,11 +443,14 @@
     )(got.reshape(2 * count, WINDOW))
 
     back = lax.all_to_all(cut, both, 0, 0, tiled=True)
-    parts = pl.pallas_call(
+    own, far = pl.pallas_call(
         denoise_kernel,
-        out_shape=[jax.ShapeDtypeStruct((3,) + shape, f32)] * 4,
+        out_shape=[
+            jax.ShapeDtypeStruct((2, 3) + shape, f32),
+            jax.ShapeDtypeStruct((2, 3) + coded, WIRE),
+        ],
         in_specs=[SMEM] + [VMEM] * 4 + [HBM] * 2,
-        out_specs=[VMEM] * 4,
+        out_specs=[VMEM] * 2,
         scratch_shapes=[
             pltpu.VMEM(up_weight.shape, up_weight.dtype),
             pltpu.VMEM(down_weight.shape, down_weight.dtype),
@@ -433,9 +460,20 @@
         cost_estimate=cost(6),
         name="denoise",
     )(patch_offsets, region, *others, up_weight, down_weight)
-    arrived = []
-    for step in range(1, agent_count):
-        arrived.append(hop(parts[step], "agent", step))
+    opposite = hop(far, "agent", 2)
+    kept, passed = pl.pallas_call(
+        halve_kernel,
+        out_shape=[
+            jax.ShapeDtypeStruct((3,) + shape, f32),
+            jax.ShapeDtypeStruct((3,) + coded, WIRE),
+        ],
+        in_specs=[VMEM] * 2,
+        out_specs=[VMEM] * 2,
+        compiler_params=PARAMS,
+        cost_estimate=cost(1),
+        name="halve",
+    )(own, opposite)
+    beside = hop(passed, "agent", 1)
 
     fit, held = pl.pallas_call(
         functools.partial(spread_kernel, factor),
@@ -452,12 +490,12 @@
             jax.ShapeDtypeStruct((2,) + shape, f32),
             jax.ShapeDtypeStruct((1,) + shape, f32),
         ],
-        in_specs=[VMEM] * 4,
+        in_specs=[VMEM] * 2,
         out_specs=[VMEM] * 2,
         compiler_params=PARAMS,
         cost_estimate=cost(1),
         name="add",
-    )(parts[0], *arrived)
+    )(kept, beside)
     previous = hop(head, "tile", 1)
     state_next = pl.pallas_call(
         join_kernel,

time: 80.9 us -> 76.5 us (0.946)
  the two profiles are of different devices: /device:TPU:1 before, /device:TPU:0 now
where the time goes in v5:
time: 76.5 us; the launch traced here: 76.3 us
  starting transfers between devices  39.8 us (52%)
  waiting for transfers between devices  20.9 us (27%)
  Pallas kernels  14.8 us (19%)
    ppermute x7, starting transfers between devices, hop(): lax.ppermute(value, axis, [(i, (i + step) % count) for i in range(count)])  23.2 us
    ppermute x7, waiting for transfers between devices, hop(): lax.ppermute(value, axis, [(i, (i + step) % count) for i in range(count)])  13.7 us
    all_to_all x1, starting transfers between devices, step(): lax.all_to_all(pieces.reshape(count, 2, WINDOW), both, 0, 0, tiled=True)  9.31 us
    all_to_all x1, starting transfers between devices, step(): back = lax.all_to_all(cut, both, 0, 0, tiled=True)  7.29 us
    pallas_call x1, Pallas kernels, step(): pl.pallas_call(denoise_kernel, out_shape=[jax.ShapeDtypeStruct((2, 3) + s...  5.15 us
    all_to_all x1, waiting for transfers between devices, step(): lax.all_to_all(pieces.reshape(count, 2, WINDOW), both, 0, 0, tiled=True)  4.21 us
    all_to_all x1, waiting for transfers between devices, step(): back = lax.all_to_all(cut, both, 0, 0, tiled=True)  3 us
    pallas_call x1, Pallas kernels, step(): pl.pallas_call(project_kernel, out_shape=[jax.ShapeDtypeStruct((2 * angle...  2.8 us
  transfers between devices with their start and end apart: 9, of which 5 were waited for; matrix products, arithmetic and copies ran while one was open for 0% of the time, Pallas kernels for 15%

profile of v5, /device:TPU:0, one launch (start us, length us, event | category | flops | bytes accessed | tf_op | source)
XLA Modules:
  0.0 76.3 jit_solution(9818892544874315022)
XLA Ops:
  0.6 0.0 copy-start.2
  0.6 1.2 %pack.1 = (bf16[2,8,16,128]{3,2,1,0:T(8,128)(2,1)S(1)}, bf16[1,8,16,128]{3,2,1,0:T(8,128)(2,1)S(1)}, f32[16,16,64]{2,1,0:T(8,128)S(1)}, s32[16,16,64]{2,1,0:T(8,128)S(1)}, s32[16,16,64]{2,1,0:T(8,128)S(1)}) custom-call(f32[4,1,16,16,64]{4,3,2,1,0:T(8,128)} %state_ref.1, s32[16,16,64]{2,1,0:T(8,128)} %bin_hbm.1, s32[16,16,64]{2,1,0:T(8,128)} %num_hbm.1), custom_call_target="tpu_custom_call" | custom-call | flops 2000000000 | bytes 6000000 | tf_op jit(solution)/shard_map/pack/pallas_call | solution.py:382
  1.8 4.4 %collective-permute-start = (bf16[2,8,16,128]{3,2,1,0:T(8,128)(2,1)S(1)}, bf16[2,8,16,128]{3,2,1,0:T(8,128)(2,1)S(1)}, u32[]{:S(2)}, u32[]{:S(2)}) collective-permute-start(bf16[2,8,16,128]{3,2,1,0:T(8,128)(2,1)S(1)} %get-tuple-element.27.head_ref), channel_id=1, source_target_pairs={{0,252},{4,0},{8,4},{12,8},{16,12},{20,16},{24,20},{28,24},{32,28}... | collective-permute-start | bytes 196616 | tf_op jit(solution)/shard_map/ppermute | solution.py:365
  6.2 1.9 %collective-permute-done.next_ref = bf16[2,8,16,128]{3,2,1,0:T(8,128)(2,1)S(1)} collective-permute-done((bf16[2,8,16,128]{3,2,1,0:T(8,128)(2,1)S(1)}, bf16[2,8,16,128]{3,2,1,0:T(8,128)(2,1)S(1)}, u32[]{:S(2)}, u32[]{:S(2)}) %collective-permute-start) | collective-permute-done | bytes 65568 | tf_op jit(solution)/shard_map/ppermute | solution.py:365
  8.1 0.0 copy-done.2
  8.1 0.0 copy-start.1
  8.1 0.6 shift.1.p0
  8.7 3.4 %collective-permute-start.3 = (bf16[3,8,16,128]{3,2,1,0:T(8,128)(2,1)S(1)}, bf16[3,8,16,128]{3,2,1,0:T(8,128)(2,1)S(1)}, u32[]{:S(2)}, u32[]{:S(2)}) collective-permute-start(bf16[3,8,16,128]{3,2,1,0:T(8,128)(2,1)S(1)} %shift.1.p0), channel_id=1, source_target_pairs={{0,1},{1,2},{2,3},{3,0},{4,5},{5,6},{6,7},{7,4},{8,9},{9,10},{10,1... | collective-permute-start | bytes 294920 | tf_op jit(solution)/shard_map/ppermute | solution.py:365
  12.1 5.2 %collective-permute-start.2 = (bf16[3,8,16,128]{3,2,1,0:T(8,128)(2,1)S(1)}, bf16[3,8,16,128]{3,2,1,0:T(8,128)(2,1)S(1)}, u32[]{:S(2)}, u32[]{:S(2)}) collective-permute-start(bf16[3,8,16,128]{3,2,1,0:T(8,128)(2,1)S(1)} %shift.1.p0), channel_id=1, source_target_pairs={{0,2},{1,3},{2,0},{3,1},{4,6},{5,7},{6,4},{7,5},{8,10},{9,11},{10,... | collective-permute-start | bytes 294920 | tf_op jit(solution)/shard_map/ppermute | solution.py:365
  17.3 4.0 %collective-permute-start.1 = (bf16[3,8,16,128]{3,2,1,0:T(8,128)(2,1)S(1)}, bf16[3,8,16,128]{3,2,1,0:T(8,128)(2,1)S(1)}, u32[]{:S(2)}, u32[]{:S(2)}) collective-permute-start(bf16[3,8,16,128]{3,2,1,0:T(8,128)(2,1)S(1)} %shift.1.p0), channel_id=1, source_target_pairs={{0,3},{1,0},{2,1},{3,2},{4,7},{5,4},{6,5},{7,6},{8,11},{9,8},{10,9... | collective-permute-start | bytes 294920 | tf_op jit(solution)/shard_map/ppermute | solution.py:365
  21.4 0.0 copy-done.1
  21.4 2.8 %project.1 = (f32[512,128]{1,0:T(8,128)}, f32[16,1024]{1,0:T(8,128)S(1)}, s32[16,1024]{1,0:T(8,128)S(1)}, f32[16,1024]{1,0:T(8,128)S(1)}) custom-call(s32[1]{0:T(128)} %bitcast.group_ref, f32[16,16,64]{2,1,0:T(8,128)S(1)} %get-tuple-element.19.state_ref, s32[16,16,64]{2,1,0:T(8,128)S(1)} %get-tuple-element.20.bin_ref, ...), custom_call_target="tpu_custom_call" | custom-call | flops 5000000000 | bytes 15000000 | tf_op jit(solution)/shard_map/project/pallas_call | solution.py:404
  24.2 9.3 %all-to-all-start = ((f32[256,2,128]{2,1,0:T(2,128)}), f32[256,2,128]{2,1,0:T(2,128)S(1)}, u32[]{:S(2)}, u32[]{:S(2)}) async-start(f32[256,2,128]{2,1,0:T(2,128)} %bitcast.1), calls=%async_computation | async-start | bytes 524288 | tf_op jit(solution)/shard_map/all_to_all | solution.py:434
  33.5 0.0 collective-permute-done.3.p3
  33.5 0.0 collective-permute-done.2.p2
  33.5 0.0 collective-permute-done.1.p1
  33.5 5.1 %denoise.1 = (f32[2,3,8,16,128]{4,3,2,1,0:T(8,128)S(1)}, s16[2,3,9,16,128]{4,3,2,1,0:T(8,128)(2,1)S(1)}) custom-call(s32[3]{0:T(128)S(1)} %copy-done.2, bf16[3,8,16,128]{3,2,1,0:T(8,128)(2,1)S(1)} %shift.1.p0, bf16[3,8,16,128]{3,2,1,0:T(8,128)(2,1)S(1)} %collective-permute-done.1.p1, bf16[3,8,16,128]{3,2,1,0:T(8,128)(2,1)S(1)} %collective-permute-done.2.p2, ...), custom_call_target="tpu_custom_call" | custom-call | flops 6000000000 | bytes 18000000 | tf_op jit(solution)/shard_map/denoise/pallas_call | solution.py:446
  38.7 4.8 %collective-permute-start.4 = (s16[2,3,9,16,128]{4,3,2,1,0:T(8,128)(2,1)S(1)}, s16[2,3,9,16,128]{4,3,2,1,0:T(8,128)(2,1)S(1)}, u32[]{:S(2)}, u32[]{:S(2)}) collective-permute-start(s16[2,3,9,16,128]{4,3,2,1,0:T(8,128)(2,1)S(1)} %get-tuple-element.30), channel_id=1, source_target_pairs={{0,2},{1,3},{2,0},{3,1},{4,6},{5,7},{6,4},{7,5},{8,10},{9,11},{10,... | collective-permute-start | bytes 663560 | tf_op jit(solution)/shard_map/ppermute | solution.py:365
  43.5 4.2 %all-to-all-done = f32[256,2,128]{2,1,0:T(2,128)S(1)} async-done(((f32[256,2,128]{2,1,0:T(2,128)}), f32[256,2,128]{2,1,0:T(2,128)S(1)}, u32[]{:S(2)}, u32[]{:S(2)}) %all-to-all-start) | async-done | bytes 262176 | tf_op jit(solution)/shard_map/all_to_all | solution.py:434
  47.7 1.4 %combine.1 = f32[256,128]{1,0:T(8,128)} custom-call(f32[512,128]{1,0:T(8,128)S(1)} %bitcast.7), custom_call_target="tpu_custom_call" | custom-call | flops 2000000000 | bytes 6000000 | tf_op jit(solution)/shard_map/combine/pallas_call | solution.py:435
  49.1 7.3 %all-to-all-start.1 = ((f32[256,1,128]{2,1,0:T(1,128)}), f32[256,1,128]{2,1,0:T(1,128)S(1)}, u32[]{:S(2)}, u32[]{:S(2)}) async-start(f32[256,1,128]{2,1,0:T(1,128)} %bitcast.4), calls=%async_computation.1 | async-start | bytes 262144 | tf_op jit(solution)/shard_map/all_to_all | solution.py:445
  56.4 0.0 collective-permute-done.4.got_ref
  56.4 0.1 halve.1
  56.5 1.2 %collective-permute-start.5 = (s16[3,9,16,128]{3,2,1,0:T(8,128)(2,1)S(1)}, s16[3,9,16,128]{3,2,1,0:T(8,128)(2,1)S(1)}, u32[]{:S(2)}, u32[]{:S(2)}) collective-permute-start(s16[3,9,16,128]{3,2,1,0:T(8,128)(2,1)S(1)} %get-tuple-element.32), channel_id=1, source_target_pairs={{0,1},{1,2},{2,3},{3,0},{4,5},{5,6},{6,7},{7,4},{8,9},{9,10},{10,1... | collective-permute-start | bytes 331784 | tf_op jit(solution)/shard_map/ppermute | solution.py:365
  57.8 7.1 %collective-permute-done.5.got_ref = s16[3,9,16,128]{3,2,1,0:T(8,128)(2,1)S(1)} collective-permute-done((s16[3,9,16,128]{3,2,1,0:T(8,128)(2,1)S(1)}, s16[3,9,16,128]{3,2,1,0:T(8,128)(2,1)S(1)}, u32[]{:S(2)}, u32[]{:S(2)}) %collective-permute-start.5) | collective-permute-done | bytes 110624 | tf_op jit(solution)/shard_map/ppermute | solution.py:365
  64.9 0.1 collective-permute-start.6
  65.0 3.0 %all-to-all-done.1 = f32[256,1,128]{2,1,0:T(1,128)S(1)} async-done(((f32[256,1,128]{2,1,0:T(1,128)}), f32[256,1,128]{2,1,0:T(1,128)S(1)}, u32[]{:S(2)}, u32[]{:S(2)}) %all-to-all-start.1) | async-done | bytes 131104 | tf_op jit(solution)/shard_map/all_to_all | solution.py:445
  68.0 0.0 copy-start
  68.0 0.0 copy-start.3
  68.0 2.1 %spread.1 = (f32[1,16,16,64]{3,2,1,0:T(8,128)}, f32[1,16,16,64]{3,2,1,0:T(8,128)S(1)}) custom-call(f32[16,1024]{1,0:T(8,128)S(1)} %get-tuple-element.22.u_ref, s32[16,1024]{1,0:T(8,128)S(1)} %get-tuple-element.23.rel_ref, f32[16,1024]{1,0:T(8,128)S(1)} %get-tuple-element.24.w_ref, f32[16,16,128]{2,1,0:T(8,128)S(1)} %bitcast.8), custom_call_target="tpu_custom_call" | custom-call | flops 4000000000 | bytes 12000000 | tf_op jit(solution)/shard_map/spread/pallas_call | solution.py:478
  70.0 4.7 %collective-permute-done.6.prev_ref = f32[2,8,16,128]{3,2,1,0:T(8,128)S(1)} collective-permute-done((f32[2,8,16,128]{3,2,1,0:T(8,128)S(1)}, f32[2,8,16,128]{3,2,1,0:T(8,128)S(1)}, u32[]{:S(2)}, u32[]{:S(2)}) %collective-permute-start.6) | collective-permute-done | bytes 131104 | tf_op jit(solution)/shard_map/ppermute | solution.py:365
  74.8 0.0 copy-done
  74.8 0.0 copy-done.3
  74.8 1.5 %join.1 = f32[4,1,16,16,64]{4,3,2,1,0:T(8,128)} custom-call(s32[3]{0:T(128)S(1)} %copy-done.2, f32[4]{0:T(128)S(1)} %copy-done.3, f32[4,1,16,16,64]{4,3,2,1,0:T(8,128)S(1)} %copy-done, f32[1,16,16,64]{3,2,1,0:T(8,128)S(1)} %get-tuple-element.26.fit_ref, f32[2,8,16,128]{3,2,1,0:T(8,128)S(1)} %get-tuple-element.33.head_ref, ...), custom_call_target="tpu_custom_call" | custom-call | flops 2000000000 | bytes 6000000 | tf_op jit(solution)/shard_map/join/pallas_call | solution.py:500
  (1 shorter events, 0.0 us)
Async XLA Ops:
  0.6 7.5 %copy-start.2 = (s32[3]{0:T(128)S(1)}, s32[3]{0:T(128)}, u32[]{:S(2)}) copy-start(s32[3]{0:T(128)} %offset_ref.5) | copy-start | bytes 40
  1.8 6.3 %collective-permute-start = (bf16[2,8,16,128]{3,2,1,0:T(8,128)(2,1)S(1)}, bf16[2,8,16,128]{3,2,1,0:T(8,128)(2,1)S(1)}, u32[]{:S(2)}, u32[]{:S(2)}) collective-permute-start(bf16[2,8,16,128]{3,2,1,0:T(8,128)(2,1)S(1)} %get-tuple-element.27.head_ref), channel_id=1, source_target_pairs={{0,252},{4,0},{8,4},{12,8},{16,12},{20,16},{24,20},{28,24},{32,28}... | collective-permute-start | bytes 196616 | tf_op jit(solution)/shard_map/ppermute | solution.py:365
  8.1 13.3 %copy-start.1 = (f32[1,16,88]{2,1,0:T(8,128)S(1)}, f32[1,16,88]{2,1,0:T(8,128)}, u32[]{:S(2)}) copy-start(f32[1,16,88]{2,1,0:T(8,128)} %meas_ref.1) | copy-start | bytes 16900
  8.7 24.8 %collective-permute-start.3 = (bf16[3,8,16,128]{3,2,1,0:T(8,128)(2,1)S(1)}, bf16[3,8,16,128]{3,2,1,0:T(8,128)(2,1)S(1)}, u32[]{:S(2)}, u32[]{:S(2)}) collective-permute-start(bf16[3,8,16,128]{3,2,1,0:T(8,128)(2,1)S(1)} %shift.1.p0), channel_id=1, source_target_pairs={{0,1},{1,2},{2,3},{3,0},{4,5},{5,6},{6,7},{7,4},{8,9},{9,10},{10,1... | collective-permute-start | bytes 294920 | tf_op jit(solution)/shard_map/ppermute | solution.py:365
  12.1 21.4 %collective-permute-start.2 = (bf16[3,8,16,128]{3,2,1,0:T(8,128)(2,1)S(1)}, bf16[3,8,16,128]{3,2,1,0:T(8,128)(2,1)S(1)}, u32[]{:S(2)}, u32[]{:S(2)}) collective-permute-start(bf16[3,8,16,128]{3,2,1,0:T(8,128)(2,1)S(1)} %shift.1.p0), channel_id=1, source_target_pairs={{0,2},{1,3},{2,0},{3,1},{4,6},{5,7},{6,4},{7,5},{8,10},{9,11},{10,... | collective-permute-start | bytes 294920 | tf_op jit(solution)/shard_map/ppermute | solution.py:365
  17.3 16.2 %collective-permute-start.1 = (bf16[3,8,16,128]{3,2,1,0:T(8,128)(2,1)S(1)}, bf16[3,8,16,128]{3,2,1,0:T(8,128)(2,1)S(1)}, u32[]{:S(2)}, u32[]{:S(2)}) collective-permute-start(bf16[3,8,16,128]{3,2,1,0:T(8,128)(2,1)S(1)} %shift.1.p0), channel_id=1, source_target_pairs={{0,3},{1,0},{2,1},{3,2},{4,7},{5,4},{6,5},{7,6},{8,11},{9,8},{10,9... | collective-permute-start | bytes 294920 | tf_op jit(solution)/shard_map/ppermute | solution.py:365
  24.2 23.5 %all-to-all-start = ((f32[256,2,128]{2,1,0:T(2,128)}), f32[256,2,128]{2,1,0:T(2,128)S(1)}, u32[]{:S(2)}, u32[]{:S(2)}) async-start(f32[256,2,128]{2,1,0:T(2,128)} %bitcast.1), calls=%async_computation | async-start | bytes 524288 | tf_op jit(solution)/shard_map/all_to_all | solution.py:434
  38.7 17.7 %collective-permute-start.4 = (s16[2,3,9,16,128]{4,3,2,1,0:T(8,128)(2,1)S(1)}, s16[2,3,9,16,128]{4,3,2,1,0:T(8,128)(2,1)S(1)}, u32[]{:S(2)}, u32[]{:S(2)}) collective-permute-start(s16[2,3,9,16,128]{4,3,2,1,0:T(8,128)(2,1)S(1)} %get-tuple-element.30), channel_id=1, source_target_pairs={{0,2},{1,3},{2,0},{3,1},{4,6},{5,7},{6,4},{7,5},{8,10},{9,11},{10,... | collective-permute-start | bytes 663560 | tf_op jit(solution)/shard_map/ppermute | solution.py:365
  49.1 18.9 %all-to-all-start.1 = ((f32[256,1,128]{2,1,0:T(1,128)}), f32[256,1,128]{2,1,0:T(1,128)S(1)}, u32[]{:S(2)}, u32[]{:S(2)}) async-start(f32[256,1,128]{2,1,0:T(1,128)} %bitcast.4), calls=%async_computation.1 | async-start | bytes 262144 | tf_op jit(solution)/shard_map/all_to_all | solution.py:445
  56.5 8.3 %collective-permute-start.5 = (s16[3,9,16,128]{3,2,1,0:T(8,128)(2,1)S(1)}, s16[3,9,16,128]{3,2,1,0:T(8,128)(2,1)S(1)}, u32[]{:S(2)}, u32[]{:S(2)}) collective-permute-start(s16[3,9,16,128]{3,2,1,0:T(8,128)(2,1)S(1)} %get-tuple-element.32), channel_id=1, source_target_pairs={{0,1},{1,2},{2,3},{3,0},{4,5},{5,6},{6,7},{7,4},{8,9},{9,10},{10,1... | collective-permute-start | bytes 331784 | tf_op jit(solution)/shard_map/ppermute | solution.py:365
  64.9 9.9 %collective-permute-start.6 = (f32[2,8,16,128]{3,2,1,0:T(8,128)S(1)}, f32[2,8,16,128]{3,2,1,0:T(8,128)S(1)}, u32[]{:S(2)}, u32[]{:S(2)}) collective-permute-start(f32[2,8,16,128]{3,2,1,0:T(8,128)S(1)} %get-tuple-element.33.head_ref), channel_id=1, source_target_pairs={{0,4},{4,8},{8,12},{12,16},{16,20},{20,24},{24,28},{28,32},{32,36}... | collective-permute-start | bytes 393224 | tf_op jit(solution)/shard_map/ppermute | solution.py:365
  68.0 6.8 %copy-start = (f32[4,1,16,16,64]{4,3,2,1,0:T(8,128)S(1)}, f32[4,1,16,16,64]{4,3,2,1,0:T(8,128)}, u32[]{:S(2)}) copy-start(f32[4,1,16,16,64]{4,3,2,1,0:T(8,128)} %state_ref.1) | copy-start | bytes 786436
  68.0 6.8 %copy-start.3 = (f32[4]{0:T(128)S(1)}, f32[4]{0:T(128)}, u32[]{:S(2)}) copy-start(f32[4]{0:T(128)} %weight_ref.1) | copy-start | bytes 52

commit v6 on v5

--- a/solution.py
+++ b/solution.py
@@ -70,7 +70,7 @@
         out_ref[pl.ds(first, planes, stride=2), :] = piece
         return carry
 
-    lax.fori_loop(0, angles, body, 0, unroll=8)
+    lax.fori_loop(0, angles, body, 0, unroll=16)
 
 
 def combine_kernel(factor, owned, got_ref, out_ref):
@@ -174,16 +174,12 @@
     return held[:count].astype(jnp.float32) * scale[None]
 
 
-def halve_kernel(near_ref, got_ref, keep_ref, send_ref):
-    for k in range(3):
-        keep_ref[k] = near_ref[0, k] + decode(got_ref.at[0, k])
-        encode(near_ref[1, k] + decode(got_ref.at[1, k]), send_ref.at[k])
-
-
-def add_kernel(keep_ref, got_ref, head_ref, tail_ref):
+def halve_kernel(near_ref, got_ref, head_ref, tail_ref, send_ref, ahead_ref):
     for k in range(3):
         out = head_ref.at[k] if k < 2 else tail_ref.at[0]
-        out[...] = keep_ref[k] + decode(got_ref.at[k])
+        out[...] = near_ref[0, k] + decode(got_ref.at[0, k])
+        encode(near_ref[1, k] + decode(got_ref.at[1, k]), send_ref.at[k])
+    ahead_ref[...] = send_ref[:2]
 
 
 def swap_slabs(slabs):
@@ -313,7 +309,7 @@
         w = w_ref[pl.ds(a, 1), :]
         return total + (far + w * (near - far))
 
-    total = lax.fori_loop(0, angles, body, jnp.zeros(u_ref.shape, jnp.float32), unroll=8)
+    total = lax.fori_loop(0, angles, body, jnp.zeros(u_ref.shape, jnp.float32), unroll=16)
     fit = u_ref[...] - factor * total
     rows, cols = fit_ref.shape[2:]
     for x in range(rows):
@@ -322,7 +318,8 @@
 
 
 def join_kernel(
-    offset_ref, weight_ref, state_ref, fit_ref, head_ref, tail_ref, prev_ref, next_ref
+    offset_ref, weight_ref, state_ref, fit_ref, head_ref, tail_ref, beside_ref, prev_ref, side_ref,
+    next_ref,
 ):
     planes, _, cols = fit_ref.shape[1:]
     raw = [jnp.full((1, cols), weight_ref[i], jnp.float32) for i in range(4)]
@@ -332,10 +329,12 @@
     nets = []
     for k in range(3):
         if k == 2:
-            net = tail_ref[0]
+            net = tail_ref[0] + decode(beside_ref.at[k])
         else:
-            net, o = head_ref[k], offset_ref[k]
-            net = jnp.where(row >= o, pltpu.roll(net, o, 1), pltpu.roll(prev_ref[k], o, 1))
+            o = offset_ref[k]
+            net = head_ref[k] + decode(beside_ref.at[k])
+            before = prev_ref[k] + decode(side_ref.at[k])
+            net = jnp.where(row >= o, pltpu.roll(net, o, 1), pltpu.roll(before, o, 1))
         nets.append((net[:, :, :cols], pltpu.roll(net, WINDOW - cols, 2)[:, :, :cols]))
     count = planes // 2
     for part in range(2):
@@ -461,19 +460,28 @@
         name="denoise",
     )(patch_offsets, region, *others, up_weight, down_weight)
     opposite = hop(far, "agent", 2)
-    kept, passed = pl.pallas_call(
+    head, tail, passed, ahead = pl.pallas_call(
         halve_kernel,
         out_shape=[
-            jax.ShapeDtypeStruct((3,) + shape, f32),
+            jax.ShapeDtypeStruct((2,) + shape, f32),
+            jax.ShapeDtypeStruct((1,) + shape, f32),
             jax.ShapeDtypeStruct((3,) + coded, WIRE),
+            jax.ShapeDtypeStruct((2,) + coded, WIRE),
         ],
         in_specs=[VMEM] * 2,
-        out_specs=[VMEM] * 2,
+        out_specs=[VMEM] * 4,
         compiler_params=PARAMS,
         cost_estimate=cost(1),
         name="halve",
     )(own, opposite)
     beside = hop(passed, "agent", 1)
+    pairs = [
+        (t * agent_count + g, (t + 1) % tile_count * agent_count + (g + 1) % agent_count)
+        for t in range(tile_count)
+        for g in range(agent_count)
+    ]
+    side = lax.ppermute(ahead, both, pairs)
+    previous = hop(head, "tile", 1)
 
     fit, held = pl.pallas_call(
         functools.partial(spread_kernel, factor),
@@ -484,28 +492,15 @@
         cost_estimate=cost(4),
         name="spread",
     )(flat, rel, near, back.reshape(angles, planes, WINDOW))
-    head, tail = pl.pallas_call(
-        add_kernel,
-        out_shape=[
-            jax.ShapeDtypeStruct((2,) + shape, f32),
-            jax.ShapeDtypeStruct((1,) + shape, f32),
-        ],
-        in_specs=[VMEM] * 2,
-        out_specs=[VMEM] * 2,
-        compiler_params=PARAMS,
-        cost_estimate=cost(1),
-        name="add",
-    )(kept, beside)
-    previous = hop(head, "tile", 1)
     state_next = pl.pallas_call(
         join_kernel,
         out_shape=jax.ShapeDtypeStruct(agent_state.shape, f32),
-        in_specs=[SMEM, SMEM] + [VMEM] * 5,
+        in_specs=[SMEM, SMEM] + [VMEM] * 7,
         out_specs=VMEM,
         compiler_params=PARAMS,
         cost_estimate=cost(2),
         name="join",
-    )(patch_offsets, agent_weights, agent_state, held, head, tail, previous)
+    )(patch_offsets, agent_weights, agent_state, held, head, tail, beside, previous, side)
     return (state_next, fit)
 
 

time: 76.5 us -> 73.7 us (0.963)
  the two profiles are of different devices: /device:TPU:0 before, /device:TPU:1 now
where the time goes in v6:
time: 73.7 us; the launch traced here: 73.5 us
  starting transfers between devices  47.4 us (64%)
  Pallas kernels  14.4 us (20%)
  waiting for transfers between devices  11 us (15%)
    ppermute x7, starting transfers between devices, hop(): lax.ppermute(value, axis, [(i, (i + step) % count) for i in range(count)])  23.2 us
    all_to_all x1, starting transfers between devices, step(): lax.all_to_all(pieces.reshape(count, 2, WINDOW), both, 0, 0, tiled=True)  14.2 us
    all_to_all x1, starting transfers between devices, step(): back = lax.all_to_all(cut, both, 0, 0, tiled=True)  5.55 us
    pallas_call x1, Pallas kernels, step(): pl.pallas_call(denoise_kernel, out_shape=[jax.ShapeDtypeStruct((2, 3) + s...  5.14 us
    all_to_all x1, waiting for transfers between devices, step(): back = lax.all_to_all(cut, both, 0, 0, tiled=True)  4.83 us
    ppermute x1, starting transfers between devices, step(): side = lax.ppermute(ahead, both, pairs)  4.49 us
    all_to_all x1, waiting for transfers between devices, step(): lax.all_to_all(pieces.reshape(count, 2, WINDOW), both, 0, 0, tiled=True)  4.34 us
    pallas_call x1, Pallas kernels, step(): pl.pallas_call(project_kernel, out_shape=[jax.ShapeDtypeStruct((2 * angle...  2.6 us
  transfers between devices with their start and end apart: 10, of which 3 were waited for; matrix products, arithmetic and copies ran while one was open for 0% of the time, Pallas kernels for 15%

profile of v6, /device:TPU:1, one launch (start us, length us, event | category | flops | bytes accessed | tf_op | source)
XLA Modules:
  0.0 73.5 jit_solution(14129102496377436612)
XLA Ops:
  0.6 0.0 copy-start.2
  0.6 1.2 %pack.1 = (bf16[2,8,16,128]{3,2,1,0:T(8,128)(2,1)S(1)}, bf16[1,8,16,128]{3,2,1,0:T(8,128)(2,1)S(1)}, f32[16,16,64]{2,1,0:T(8,128)S(1)}, s32[16,16,64]{2,1,0:T(8,128)S(1)}, s32[16,16,64]{2,1,0:T(8,128)S(1)}) custom-call(f32[4,1,16,16,64]{4,3,2,1,0:T(8,128)} %state_ref.1, s32[16,16,64]{2,1,0:T(8,128)} %bin_hbm.1, s32[16,16,64]{2,1,0:T(8,128)} %num_hbm.1), custom_call_target="tpu_custom_call" | custom-call | flops 2000000000 | bytes 6000000 | tf_op jit(solution)/shard_map/pack/pallas_call | solution.py:381
  1.8 3.3 %collective-permute-start = (bf16[2,8,16,128]{3,2,1,0:T(8,128)(2,1)S(1)}, bf16[2,8,16,128]{3,2,1,0:T(8,128)(2,1)S(1)}, u32[]{:S(2)}, u32[]{:S(2)}) collective-permute-start(bf16[2,8,16,128]{3,2,1,0:T(8,128)(2,1)S(1)} %get-tuple-element.27.head_ref), channel_id=1, source_target_pairs={{0,252},{4,0},{8,4},{12,8},{16,12},{20,16},{24,20},{28,24},{32,28}... | collective-permute-start | bytes 196616 | tf_op jit(solution)/shard_map/ppermute | solution.py:364
  5.1 1.8 %collective-permute-done.next_ref = bf16[2,8,16,128]{3,2,1,0:T(8,128)(2,1)S(1)} collective-permute-done((bf16[2,8,16,128]{3,2,1,0:T(8,128)(2,1)S(1)}, bf16[2,8,16,128]{3,2,1,0:T(8,128)(2,1)S(1)}, u32[]{:S(2)}, u32[]{:S(2)}) %collective-permute-start) | collective-permute-done | bytes 65568 | tf_op jit(solution)/shard_map/ppermute | solution.py:364
  6.9 0.0 copy-done.2
  6.9 0.0 copy-start.1
  6.9 0.6 shift.1.p0
  7.5 3.1 %collective-permute-start.3 = (bf16[3,8,16,128]{3,2,1,0:T(8,128)(2,1)S(1)}, bf16[3,8,16,128]{3,2,1,0:T(8,128)(2,1)S(1)}, u32[]{:S(2)}, u32[]{:S(2)}) collective-permute-start(bf16[3,8,16,128]{3,2,1,0:T(8,128)(2,1)S(1)} %shift.1.p0), channel_id=1, source_target_pairs={{0,1},{1,2},{2,3},{3,0},{4,5},{5,6},{6,7},{7,4},{8,9},{9,10},{10,1... | collective-permute-start | bytes 294920 | tf_op jit(solution)/shard_map/ppermute | solution.py:364
  10.5 4.7 %collective-permute-start.2 = (bf16[3,8,16,128]{3,2,1,0:T(8,128)(2,1)S(1)}, bf16[3,8,16,128]{3,2,1,0:T(8,128)(2,1)S(1)}, u32[]{:S(2)}, u32[]{:S(2)}) collective-permute-start(bf16[3,8,16,128]{3,2,1,0:T(8,128)(2,1)S(1)} %shift.1.p0), channel_id=1, source_target_pairs={{0,2},{1,3},{2,0},{3,1},{4,6},{5,7},{6,4},{7,5},{8,10},{9,11},{10,... | collective-permute-start | bytes 294920 | tf_op jit(solution)/shard_map/ppermute | solution.py:364
  15.2 2.4 %collective-permute-start.1 = (bf16[3,8,16,128]{3,2,1,0:T(8,128)(2,1)S(1)}, bf16[3,8,16,128]{3,2,1,0:T(8,128)(2,1)S(1)}, u32[]{:S(2)}, u32[]{:S(2)}) collective-permute-start(bf16[3,8,16,128]{3,2,1,0:T(8,128)(2,1)S(1)} %shift.1.p0), channel_id=1, source_target_pairs={{0,3},{1,0},{2,1},{3,2},{4,7},{5,4},{6,5},{7,6},{8,11},{9,8},{10,9... | collective-permute-start | bytes 294920 | tf_op jit(solution)/shard_map/ppermute | solution.py:364
  17.6 0.0 copy-done.1
  17.6 2.6 %project.1 = (f32[512,128]{1,0:T(8,128)}, f32[16,1024]{1,0:T(8,128)S(1)}, s32[16,1024]{1,0:T(8,128)S(1)}, f32[16,1024]{1,0:T(8,128)S(1)}) custom-call(s32[1]{0:T(128)} %bitcast.group_ref, f32[16,16,64]{2,1,0:T(8,128)S(1)} %get-tuple-element.19.state_ref, s32[16,16,64]{2,1,0:T(8,128)S(1)} %get-tuple-element.20.bin_ref, ...), custom_call_target="tpu_custom_call" | custom-call | flops 5000000000 | bytes 15000000 | tf_op jit(solution)/shard_map/project/pallas_call | solution.py:403
  20.2 14.2 %all-to-all-start = ((f32[256,2,128]{2,1,0:T(2,128)}), f32[256,2,128]{2,1,0:T(2,128)S(1)}, u32[]{:S(2)}, u32[]{:S(2)}) async-start(f32[256,2,128]{2,1,0:T(2,128)} %bitcast.1), calls=%async_computation | async-start | bytes 524288 | tf_op jit(solution)/shard_map/all_to_all | solution.py:433
  34.3 0.0 collective-permute-done.3.p3
  34.4 0.0 collective-permute-done.2.p2
  34.4 0.0 collective-permute-done.1.p1
  34.4 5.1 %denoise.1 = (f32[2,3,8,16,128]{4,3,2,1,0:T(8,128)S(1)}, s16[2,3,9,16,128]{4,3,2,1,0:T(8,128)(2,1)S(1)}) custom-call(s32[3]{0:T(128)S(1)} %copy-done.2, bf16[3,8,16,128]{3,2,1,0:T(8,128)(2,1)S(1)} %shift.1.p0, bf16[3,8,16,128]{3,2,1,0:T(8,128)(2,1)S(1)} %collective-permute-done.1.p1, bf16[3,8,16,128]{3,2,1,0:T(8,128)(2,1)S(1)} %collective-permute-done.2.p2, ...), custom_call_target="tpu_custom_call" | custom-call | flops 6000000000 | bytes 18000000 | tf_op jit(solution)/shard_map/denoise/pallas_call | solution.py:445
  39.5 6.3 %collective-permute-start.4 = (s16[2,3,9,16,128]{4,3,2,1,0:T(8,128)(2,1)S(1)}, s16[2,3,9,16,128]{4,3,2,1,0:T(8,128)(2,1)S(1)}, u32[]{:S(2)}, u32[]{:S(2)}) collective-permute-start(s16[2,3,9,16,128]{4,3,2,1,0:T(8,128)(2,1)S(1)} %get-tuple-element.30), channel_id=1, source_target_pairs={{0,2},{1,3},{2,0},{3,1},{4,6},{5,7},{6,4},{7,5},{8,10},{9,11},{10,... | collective-permute-start | bytes 663560 | tf_op jit(solution)/shard_map/ppermute | solution.py:364
  45.8 4.3 %all-to-all-done = f32[256,2,128]{2,1,0:T(2,128)S(1)} async-done(((f32[256,2,128]{2,1,0:T(2,128)}), f32[256,2,128]{2,1,0:T(2,128)S(1)}, u32[]{:S(2)}, u32[]{:S(2)}) %all-to-all-start) | async-done | bytes 262176 | tf_op jit(solution)/shard_map/all_to_all | solution.py:433
  50.1 1.4 %combine.1 = f32[256,128]{1,0:T(8,128)} custom-call(f32[512,128]{1,0:T(8,128)S(1)} %bitcast.7), custom_call_target="tpu_custom_call" | custom-call | flops 2000000000 | bytes 6000000 | tf_op jit(solution)/shard_map/combine/pallas_call | solution.py:434
  51.6 5.6 %all-to-all-start.1 = ((f32[256,1,128]{2,1,0:T(1,128)}), f32[256,1,128]{2,1,0:T(1,128)S(1)}, u32[]{:S(2)}, u32[]{:S(2)}) async-start(f32[256,1,128]{2,1,0:T(1,128)} %bitcast.4), calls=%async_computation.1 | async-start | bytes 262144 | tf_op jit(solution)/shard_map/all_to_all | solution.py:444
  57.1 0.0 collective-permute-done.4.got_ref
  57.1 0.1 halve.1
  57.3 4.5 %collective-permute-start.7 = (s16[2,9,16,128]{3,2,1,0:T(8,128)(2,1)S(1)}, s16[2,9,16,128]{3,2,1,0:T(8,128)(2,1)S(1)}, u32[]{:S(2)}, u32[]{:S(2)}) collective-permute-start(s16[2,9,16,128]{3,2,1,0:T(8,128)(2,1)S(1)} %get-tuple-element.34), channel_id=1, source_target_pairs={{0,5},{1,6},{2,7},{3,4},{4,9},{5,10},{6,11},{7,8},{8,13},{9,14},{1... | collective-permute-start | bytes 221192 | tf_op jit(solution)/shard_map/ppermute | solution.py:483
  61.7 2.9 %collective-permute-start.5 = (s16[3,9,16,128]{3,2,1,0:T(8,128)(2,1)S(1)}, s16[3,9,16,128]{3,2,1,0:T(8,128)(2,1)S(1)}, u32[]{:S(2)}, u32[]{:S(2)}) collective-permute-start(s16[3,9,16,128]{3,2,1,0:T(8,128)(2,1)S(1)} %get-tuple-element.33), channel_id=1, source_target_pairs={{0,1},{1,2},{2,3},{3,0},{4,5},{5,6},{6,7},{7,4},{8,9},{9,10},{10,1... | collective-permute-start | bytes 331784 | tf_op jit(solution)/shard_map/ppermute | solution.py:364
  64.7 0.6 collective-permute-start.6
  65.2 4.8 %all-to-all-done.1 = f32[256,1,128]{2,1,0:T(1,128)S(1)} async-done(((f32[256,1,128]{2,1,0:T(1,128)}), f32[256,1,128]{2,1,0:T(1,128)S(1)}, u32[]{:S(2)}, u32[]{:S(2)}) %all-to-all-start.1) | async-done | bytes 131104 | tf_op jit(solution)/shard_map/all_to_all | solution.py:444
  70.1 0.0 copy-start
  70.1 0.0 copy-start.3
  70.1 1.8 %spread.1 = (f32[1,16,16,64]{3,2,1,0:T(8,128)}, f32[1,16,16,64]{3,2,1,0:T(8,128)S(1)}) custom-call(f32[16,1024]{1,0:T(8,128)S(1)} %get-tuple-element.22.u_ref, s32[16,1024]{1,0:T(8,128)S(1)} %get-tuple-element.23.rel_ref, f32[16,1024]{1,0:T(8,128)S(1)} %get-tuple-element.24.w_ref, f32[16,16,128]{2,1,0:T(8,128)S(1)} %bitcast.8), custom_call_target="tpu_custom_call" | custom-call | flops 4000000000 | bytes 12000000 | tf_op jit(solution)/shard_map/spread/pallas_call | solution.py:486
  71.9 0.0 collective-permute-done.7.side_ref
  71.9 0.0 collective-permute-done.5.beside_ref
  71.9 0.0 collective-permute-done.6.prev_ref
  72.0 0.0 copy-done
  72.0 0.0 copy-done.3
  72.0 1.6 %join.1 = f32[4,1,16,16,64]{4,3,2,1,0:T(8,128)} custom-call(s32[3]{0:T(128)S(1)} %copy-done.2, f32[4]{0:T(128)S(1)} %copy-done.3, f32[4,1,16,16,64]{4,3,2,1,0:T(8,128)S(1)} %copy-done, f32[1,16,16,64]{3,2,1,0:T(8,128)S(1)} %get-tuple-element.26.fit_ref, f32[2,8,16,128]{3,2,1,0:T(8,128)S(1)} %get-tuple-element.31.head_ref, ...), custom_call_target="tpu_custom_call" | custom-call | flops 2000000000 | bytes 6000000 | tf_op jit(solution)/shard_map/join/pallas_call | solution.py:495
Async XLA Ops:
  0.6 6.2 %copy-start.2 = (s32[3]{0:T(128)S(1)}, s32[3]{0:T(128)}, u32[]{:S(2)}) copy-start(s32[3]{0:T(128)} %offset_ref.5) | copy-start | bytes 40
  1.8 5.0 %collective-permute-start = (bf16[2,8,16,128]{3,2,1,0:T(8,128)(2,1)S(1)}, bf16[2,8,16,128]{3,2,1,0:T(8,128)(2,1)S(1)}, u32[]{:S(2)}, u32[]{:S(2)}) collective-permute-start(bf16[2,8,16,128]{3,2,1,0:T(8,128)(2,1)S(1)} %get-tuple-element.27.head_ref), channel_id=1, source_target_pairs={{0,252},{4,0},{8,4},{12,8},{16,12},{20,16},{24,20},{28,24},{32,28}... | collective-permute-start | bytes 196616 | tf_op jit(solution)/shard_map/ppermute | solution.py:364
  6.9 10.7 %copy-start.1 = (f32[1,16,88]{2,1,0:T(8,128)S(1)}, f32[1,16,88]{2,1,0:T(8,128)}, u32[]{:S(2)}) copy-start(f32[1,16,88]{2,1,0:T(8,128)} %meas_ref.1) | copy-start | bytes 16900
  7.5 26.9 %collective-permute-start.3 = (bf16[3,8,16,128]{3,2,1,0:T(8,128)(2,1)S(1)}, bf16[3,8,16,128]{3,2,1,0:T(8,128)(2,1)S(1)}, u32[]{:S(2)}, u32[]{:S(2)}) collective-permute-start(bf16[3,8,16,128]{3,2,1,0:T(8,128)(2,1)S(1)} %shift.1.p0), channel_id=1, source_target_pairs={{0,1},{1,2},{2,3},{3,0},{4,5},{5,6},{6,7},{7,4},{8,9},{9,10},{10,1... | collective-permute-start | bytes 294920 | tf_op jit(solution)/shard_map/ppermute | solution.py:364
  10.5 23.8 %collective-permute-start.2 = (bf16[3,8,16,128]{3,2,1,0:T(8,128)(2,1)S(1)}, bf16[3,8,16,128]{3,2,1,0:T(8,128)(2,1)S(1)}, u32[]{:S(2)}, u32[]{:S(2)}) collective-permute-start(bf16[3,8,16,128]{3,2,1,0:T(8,128)(2,1)S(1)} %shift.1.p0), channel_id=1, source_target_pairs={{0,2},{1,3},{2,0},{3,1},{4,6},{5,7},{6,4},{7,5},{8,10},{9,11},{10,... | collective-permute-start | bytes 294920 | tf_op jit(solution)/shard_map/ppermute | solution.py:364
  15.2 19.2 %collective-permute-start.1 = (bf16[3,8,16,128]{3,2,1,0:T(8,128)(2,1)S(1)}, bf16[3,8,16,128]{3,2,1,0:T(8,128)(2,1)S(1)}, u32[]{:S(2)}, u32[]{:S(2)}) collective-permute-start(bf16[3,8,16,128]{3,2,1,0:T(8,128)(2,1)S(1)} %shift.1.p0), channel_id=1, source_target_pairs={{0,3},{1,0},{2,1},{3,2},{4,7},{5,4},{6,5},{7,6},{8,11},{9,8},{10,9... | collective-permute-start | bytes 294920 | tf_op jit(solution)/shard_map/ppermute | solution.py:364
  20.2 30.0 %all-to-all-start = ((f32[256,2,128]{2,1,0:T(2,128)}), f32[256,2,128]{2,1,0:T(2,128)S(1)}, u32[]{:S(2)}, u32[]{:S(2)}) async-start(f32[256,2,128]{2,1,0:T(2,128)} %bitcast.1), calls=%async_computation | async-start | bytes 524288 | tf_op jit(solution)/shard_map/all_to_all | solution.py:433
  39.5 17.6 %collective-permute-start.4 = (s16[2,3,9,16,128]{4,3,2,1,0:T(8,128)(2,1)S(1)}, s16[2,3,9,16,128]{4,3,2,1,0:T(8,128)(2,1)S(1)}, u32[]{:S(2)}, u32[]{:S(2)}) collective-permute-start(s16[2,3,9,16,128]{4,3,2,1,0:T(8,128)(2,1)S(1)} %get-tuple-element.30), channel_id=1, source_target_pairs={{0,2},{1,3},{2,0},{3,1},{4,6},{5,7},{6,4},{7,5},{8,10},{9,11},{10,... | collective-permute-start | bytes 663560 | tf_op jit(solution)/shard_map/ppermute | solution.py:364
  51.6 18.5 %all-to-all-start.1 = ((f32[256,1,128]{2,1,0:T(1,128)}), f32[256,1,128]{2,1,0:T(1,128)S(1)}, u32[]{:S(2)}, u32[]{:S(2)}) async-start(f32[256,1,128]{2,1,0:T(1,128)} %bitcast.4), calls=%async_computation.1 | async-start | bytes 262144 | tf_op jit(solution)/shard_map/all_to_all | solution.py:444
  57.3 14.7 %collective-permute-start.7 = (s16[2,9,16,128]{3,2,1,0:T(8,128)(2,1)S(1)}, s16[2,9,16,128]{3,2,1,0:T(8,128)(2,1)S(1)}, u32[]{:S(2)}, u32[]{:S(2)}) collective-permute-start(s16[2,9,16,128]{3,2,1,0:T(8,128)(2,1)S(1)} %get-tuple-element.34), channel_id=1, source_target_pairs={{0,5},{1,6},{2,7},{3,4},{4,9},{5,10},{6,11},{7,8},{8,13},{9,14},{1... | collective-permute-start | bytes 221192 | tf_op jit(solution)/shard_map/ppermute | solution.py:483
  61.7 10.2 %collective-permute-start.5 = (s16[3,9,16,128]{3,2,1,0:T(8,128)(2,1)S(1)}, s16[3,9,16,128]{3,2,1,0:T(8,128)(2,1)S(1)}, u32[]{:S(2)}, u32[]{:S(2)}) collective-permute-start(s16[3,9,16,128]{3,2,1,0:T(8,128)(2,1)S(1)} %get-tuple-element.33), channel_id=1, source_target_pairs={{0,1},{1,2},{2,3},{3,0},{4,5},{5,6},{6,7},{7,4},{8,9},{9,10},{10,1... | collective-permute-start | bytes 331784 | tf_op jit(solution)/shard_map/ppermute | solution.py:364
  64.7 7.3 %collective-permute-start.6 = (f32[2,8,16,128]{3,2,1,0:T(8,128)S(1)}, f32[2,8,16,128]{3,2,1,0:T(8,128)S(1)}, u32[]{:S(2)}, u32[]{:S(2)}) collective-permute-start(f32[2,8,16,128]{3,2,1,0:T(8,128)S(1)} %get-tuple-element.31.head_ref), channel_id=1, source_target_pairs={{0,4},{4,8},{8,12},{12,16},{16,20},{20,24},{24,28},{28,32},{32,36}... | collective-permute-start | bytes 393224 | tf_op jit(solution)/shard_map/ppermute | solution.py:364
  70.1 1.9 %copy-start = (f32[4,1,16,16,64]{4,3,2,1,0:T(8,128)S(1)}, f32[4,1,16,16,64]{4,3,2,1,0:T(8,128)}, u32[]{:S(2)}) copy-start(f32[4,1,16,16,64]{4,3,2,1,0:T(8,128)} %state_ref.1) | copy-start | bytes 786436
  70.1 1.9 %copy-start.3 = (f32[4]{0:T(128)S(1)}, f32[4]{0:T(128)}, u32[]{:S(2)}) copy-start(f32[4]{0:T(128)} %weight_ref.1) | copy-start | bytes 52

commit v7 on v6

--- a/solution.py
+++ b/solution.py
@@ -162,16 +162,19 @@
     top = jnp.max(jnp.max(jnp.abs(block), axis=0), axis=0, keepdims=True)
     level = jnp.ceil(jnp.log2(jnp.maximum(top, 1e-30)) * GRAIN)
     scale = STEPS * jnp.exp2(level * (-1.0 / GRAIN))
-    out[:count] = jnp.round(block * scale[None]).astype(jnp.int32).astype(out.dtype)
-    level = jnp.broadcast_to(level, block.shape[1:])
-    out[count] = level.astype(jnp.int32).astype(out.dtype)
+    rows = count * block.shape[1]
+    steps = jnp.round(block * scale[None]).reshape(rows, block.shape[2])
+    out[:rows] = steps.astype(jnp.int32).astype(out.dtype)
+    level = jnp.broadcast_to(level, (8, block.shape[2]))
+    out[rows:] = level.astype(jnp.int32).astype(out.dtype)
 
 
 def decode(held):
-    count = held.shape[0] - 1
-    level = held[count].astype(jnp.float32)[:1]
+    rows = held.shape[0] - 8
+    level = held[rows:].astype(jnp.float32)[:1]
     scale = (1.0 / STEPS) * jnp.exp2(level * (1.0 / GRAIN))
-    return held[:count].astype(jnp.float32) * scale[None]
+    steps = held[:rows].astype(jnp.float32) * scale
+    return steps.reshape(rows // PATCH, PATCH, steps.shape[1])
 
 
 def halve_kernel(near_ref, got_ref, head_ref, tail_ref, send_ref, ahead_ref):
@@ -377,7 +380,7 @@
     f32 = jnp.float32
 
     shape = (planes // 2, row_count, 2 * col_count)
-    coded = (planes // 2 + 1, row_count, 2 * col_count)
+    coded = (planes // 2 * row_count + 8, 2 * col_count)
     head, tail, volume, bins, nums = pl.pallas_call(
         pack_kernel,
         out_shape=[

time: 73.7 us -> 73.7 us (level)
  no operation moved by 1% of the time
where the time goes in v7:
time: 73.7 us; the launch traced here: 73.5 us
  starting transfers between devices  47.4 us (64%)
  Pallas kernels  14.5 us (20%)
  waiting for transfers between devices  11 us (15%)
  between operations  0.74 us (1%)
    ppermute x7, starting transfers between devices, hop(): lax.ppermute(value, axis, [(i, (i + step) % count) for i in range(count)])  23.2 us
    all_to_all x1, starting transfers between devices, step(): lax.all_to_all(pieces.reshape(count, 2, WINDOW), both, 0, 0, tiled=True)  14.2 us
    all_to_all x1, starting transfers between devices, step(): back = lax.all_to_all(cut, both, 0, 0, tiled=True)  5.55 us
    pallas_call x1, Pallas kernels, step(): pl.pallas_call(denoise_kernel, out_shape=[jax.ShapeDtypeStruct((2, 3) + s...  5.15 us
    all_to_all x1, waiting for transfers between devices, step(): back = lax.all_to_all(cut, both, 0, 0, tiled=True)  4.83 us
    ppermute x1, starting transfers between devices, step(): side = lax.ppermute(ahead, both, pairs)  4.49 us
    all_to_all x1, waiting for transfers between devices, step(): lax.all_to_all(pieces.reshape(count, 2, WINDOW), both, 0, 0, tiled=True)  4.34 us
    pallas_call x1, Pallas kernels, step(): pl.pallas_call(project_kernel, out_shape=[jax.ShapeDtypeStruct((2 * angle...  2.61 us
  transfers between devices with their start and end apart: 10, of which 3 were waited for; matrix products, arithmetic and copies ran while one was open for 0% of the time, Pallas kernels for 15%

profile of v7, /device:TPU:1, one launch (start us, length us, event | category | flops | bytes accessed | tf_op | source)
XLA Modules:
  0.0 73.5 jit_solution(12857781834586622325)
XLA Ops:
  0.6 0.0 copy-start.2
  0.6 1.2 %pack.1 = (bf16[2,8,16,128]{3,2,1,0:T(8,128)(2,1)S(1)}, bf16[1,8,16,128]{3,2,1,0:T(8,128)(2,1)S(1)}, f32[16,16,64]{2,1,0:T(8,128)S(1)}, s32[16,16,64]{2,1,0:T(8,128)S(1)}, s32[16,16,64]{2,1,0:T(8,128)S(1)}) custom-call(f32[4,1,16,16,64]{4,3,2,1,0:T(8,128)} %state_ref.1, s32[16,16,64]{2,1,0:T(8,128)} %bin_hbm.1, s32[16,16,64]{2,1,0:T(8,128)} %num_hbm.1), custom_call_target="tpu_custom_call" | custom-call | flops 2000000000 | bytes 6000000 | tf_op jit(solution)/shard_map/pack/pallas_call | solution.py:384
  1.8 3.3 %collective-permute-start = (bf16[2,8,16,128]{3,2,1,0:T(8,128)(2,1)S(1)}, bf16[2,8,16,128]{3,2,1,0:T(8,128)(2,1)S(1)}, u32[]{:S(2)}, u32[]{:S(2)}) collective-permute-start(bf16[2,8,16,128]{3,2,1,0:T(8,128)(2,1)S(1)} %get-tuple-element.27.head_ref), channel_id=1, source_target_pairs={{0,252},{4,0},{8,4},{12,8},{16,12},{20,16},{24,20},{28,24},{32,28}... | collective-permute-start | bytes 196616 | tf_op jit(solution)/shard_map/ppermute | solution.py:367
  5.1 1.8 %collective-permute-done.next_ref = bf16[2,8,16,128]{3,2,1,0:T(8,128)(2,1)S(1)} collective-permute-done((bf16[2,8,16,128]{3,2,1,0:T(8,128)(2,1)S(1)}, bf16[2,8,16,128]{3,2,1,0:T(8,128)(2,1)S(1)}, u32[]{:S(2)}, u32[]{:S(2)}) %collective-permute-start) | collective-permute-done | bytes 65568 | tf_op jit(solution)/shard_map/ppermute | solution.py:367
  6.9 0.0 copy-done.2
  6.9 0.0 copy-start.1
  6.9 0.6 shift.1.p0
  7.5 3.1 %collective-permute-start.3 = (bf16[3,8,16,128]{3,2,1,0:T(8,128)(2,1)S(1)}, bf16[3,8,16,128]{3,2,1,0:T(8,128)(2,1)S(1)}, u32[]{:S(2)}, u32[]{:S(2)}) collective-permute-start(bf16[3,8,16,128]{3,2,1,0:T(8,128)(2,1)S(1)} %shift.1.p0), channel_id=1, source_target_pairs={{0,1},{1,2},{2,3},{3,0},{4,5},{5,6},{6,7},{7,4},{8,9},{9,10},{10,1... | collective-permute-start | bytes 294920 | tf_op jit(solution)/shard_map/ppermute | solution.py:367
  10.5 4.7 %collective-permute-start.2 = (bf16[3,8,16,128]{3,2,1,0:T(8,128)(2,1)S(1)}, bf16[3,8,16,128]{3,2,1,0:T(8,128)(2,1)S(1)}, u32[]{:S(2)}, u32[]{:S(2)}) collective-permute-start(bf16[3,8,16,128]{3,2,1,0:T(8,128)(2,1)S(1)} %shift.1.p0), channel_id=1, source_target_pairs={{0,2},{1,3},{2,0},{3,1},{4,6},{5,7},{6,4},{7,5},{8,10},{9,11},{10,... | collective-permute-start | bytes 294920 | tf_op jit(solution)/shard_map/ppermute | solution.py:367
  15.2 2.4 %collective-permute-start.1 = (bf16[3,8,16,128]{3,2,1,0:T(8,128)(2,1)S(1)}, bf16[3,8,16,128]{3,2,1,0:T(8,128)(2,1)S(1)}, u32[]{:S(2)}, u32[]{:S(2)}) collective-permute-start(bf16[3,8,16,128]{3,2,1,0:T(8,128)(2,1)S(1)} %shift.1.p0), channel_id=1, source_target_pairs={{0,3},{1,0},{2,1},{3,2},{4,7},{5,4},{6,5},{7,6},{8,11},{9,8},{10,9... | collective-permute-start | bytes 294920 | tf_op jit(solution)/shard_map/ppermute | solution.py:367
  17.6 0.0 copy-done.1
  17.6 2.6 %project.1 = (f32[512,128]{1,0:T(8,128)}, f32[16,1024]{1,0:T(8,128)S(1)}, s32[16,1024]{1,0:T(8,128)S(1)}, f32[16,1024]{1,0:T(8,128)S(1)}) custom-call(s32[1]{0:T(128)} %bitcast.group_ref, f32[16,16,64]{2,1,0:T(8,128)S(1)} %get-tuple-element.19.state_ref, s32[16,16,64]{2,1,0:T(8,128)S(1)} %get-tuple-element.20.bin_ref, ...), custom_call_target="tpu_custom_call" | custom-call | flops 5000000000 | bytes 15000000 | tf_op jit(solution)/shard_map/project/pallas_call | solution.py:406
  20.2 14.2 %all-to-all-start = ((f32[256,2,128]{2,1,0:T(2,128)}), f32[256,2,128]{2,1,0:T(2,128)S(1)}, u32[]{:S(2)}, u32[]{:S(2)}) async-start(f32[256,2,128]{2,1,0:T(2,128)} %bitcast.1), calls=%async_computation | async-start | bytes 524288 | tf_op jit(solution)/shard_map/all_to_all | solution.py:436
  34.3 0.0 collective-permute-done.3.p3
  34.3 0.0 collective-permute-done.2.p2
  34.4 0.0 collective-permute-done.1.p1
  34.4 5.1 %denoise.1 = (f32[2,3,8,16,128]{4,3,2,1,0:T(8,128)S(1)}, s16[2,3,136,128]{3,2,1,0:T(8,128)(2,1)S(1)}) custom-call(s32[3]{0:T(128)S(1)} %copy-done.2, bf16[3,8,16,128]{3,2,1,0:T(8,128)(2,1)S(1)} %shift.1.p0, bf16[3,8,16,128]{3,2,1,0:T(8,128)(2,1)S(1)} %collective-permute-done.1.p1, bf16[3,8,16,128]{3,2,1,0:T(8,128)(2,1)S(1)} %collective-permute-done.2.p2, ...), custom_call_target="tpu_custom_call" | custom-call | flops 6000000000 | bytes 18000000 | tf_op jit(solution)/shard_map/denoise/pallas_call | solution.py:448
  39.5 6.3 %collective-permute-start.4 = (s16[2,3,136,128]{3,2,1,0:T(8,128)(2,1)S(1)}, s16[2,3,136,128]{3,2,1,0:T(8,128)(2,1)S(1)}, u32[]{:S(2)}, u32[]{:S(2)}) collective-permute-start(s16[2,3,136,128]{3,2,1,0:T(8,128)(2,1)S(1)} %get-tuple-element.30), channel_id=1, source_target_pairs={{0,2},{1,3},{2,0},{3,1},{4,6},{5,7},{6,4},{7,5},{8,10},{9,11},{10,... | collective-permute-start | bytes 626696 | tf_op jit(solution)/shard_map/ppermute | solution.py:367
  45.8 4.3 %all-to-all-done = f32[256,2,128]{2,1,0:T(2,128)S(1)} async-done(((f32[256,2,128]{2,1,0:T(2,128)}), f32[256,2,128]{2,1,0:T(2,128)S(1)}, u32[]{:S(2)}, u32[]{:S(2)}) %all-to-all-start) | async-done | bytes 262176 | tf_op jit(solution)/shard_map/all_to_all | solution.py:436
  50.1 1.4 %combine.1 = f32[256,128]{1,0:T(8,128)} custom-call(f32[512,128]{1,0:T(8,128)S(1)} %bitcast.7), custom_call_target="tpu_custom_call" | custom-call | flops 2000000000 | bytes 6000000 | tf_op jit(solution)/shard_map/combine/pallas_call | solution.py:437
  51.6 5.6 %all-to-all-start.1 = ((f32[256,1,128]{2,1,0:T(1,128)}), f32[256,1,128]{2,1,0:T(1,128)S(1)}, u32[]{:S(2)}, u32[]{:S(2)}) async-start(f32[256,1,128]{2,1,0:T(1,128)} %bitcast.4), calls=%async_computation.1 | async-start | bytes 262144 | tf_op jit(solution)/shard_map/all_to_all | solution.py:447
  57.1 0.0 collective-permute-done.4.got_ref
  57.1 0.1 halve.1
  57.2 4.5 %collective-permute-start.7 = (s16[2,136,128]{2,1,0:T(8,128)(2,1)S(1)}, s16[2,136,128]{2,1,0:T(8,128)(2,1)S(1)}, u32[]{:S(2)}, u32[]{:S(2)}) collective-permute-start(s16[2,136,128]{2,1,0:T(8,128)(2,1)S(1)} %get-tuple-element.34), channel_id=1, source_target_pairs={{0,5},{1,6},{2,7},{3,4},{4,9},{5,10},{6,11},{7,8},{8,13},{9,14},{1... | collective-permute-start | bytes 208904 | tf_op jit(solution)/shard_map/ppermute | solution.py:486
  61.7 2.9 %collective-permute-start.5 = (s16[3,136,128]{2,1,0:T(8,128)(2,1)S(1)}, s16[3,136,128]{2,1,0:T(8,128)(2,1)S(1)}, u32[]{:S(2)}, u32[]{:S(2)}) collective-permute-start(s16[3,136,128]{2,1,0:T(8,128)(2,1)S(1)} %get-tuple-element.33), channel_id=1, source_target_pairs={{0,1},{1,2},{2,3},{3,0},{4,5},{5,6},{6,7},{7,4},{8,9},{9,10},{10,1... | collective-permute-start | bytes 313352 | tf_op jit(solution)/shard_map/ppermute | solution.py:367
  64.7 0.6 collective-permute-start.6
  65.2 4.8 %all-to-all-done.1 = f32[256,1,128]{2,1,0:T(1,128)S(1)} async-done(((f32[256,1,128]{2,1,0:T(1,128)}), f32[256,1,128]{2,1,0:T(1,128)S(1)}, u32[]{:S(2)}, u32[]{:S(2)}) %all-to-all-start.1) | async-done | bytes 131104 | tf_op jit(solution)/shard_map/all_to_all | solution.py:447
  70.1 0.0 copy-start
  70.1 0.0 copy-start.3
  70.1 1.8 %spread.1 = (f32[1,16,16,64]{3,2,1,0:T(8,128)}, f32[1,16,16,64]{3,2,1,0:T(8,128)S(1)}) custom-call(f32[16,1024]{1,0:T(8,128)S(1)} %get-tuple-element.22.u_ref, s32[16,1024]{1,0:T(8,128)S(1)} %get-tuple-element.23.rel_ref, f32[16,1024]{1,0:T(8,128)S(1)} %get-tuple-element.24.w_ref, f32[16,16,128]{2,1,0:T(8,128)S(1)} %bitcast.8), custom_call_target="tpu_custom_call" | custom-call | flops 4000000000 | bytes 12000000 | tf_op jit(solution)/shard_map/spread/pallas_call | solution.py:489
  71.9 0.0 collective-permute-done.7.side_ref
  71.9 0.0 collective-permute-done.5.beside_ref
  71.9 0.0 collective-permute-done.6.prev_ref
  71.9 0.0 copy-done
  71.9 0.0 copy-done.3
  72.0 1.6 %join.1 = f32[4,1,16,16,64]{4,3,2,1,0:T(8,128)} custom-call(s32[3]{0:T(128)S(1)} %copy-done.2, f32[4]{0:T(128)S(1)} %copy-done.3, f32[4,1,16,16,64]{4,3,2,1,0:T(8,128)S(1)} %copy-done, f32[1,16,16,64]{3,2,1,0:T(8,128)S(1)} %get-tuple-element.26.fit_ref, f32[2,8,16,128]{3,2,1,0:T(8,128)S(1)} %get-tuple-element.31.head_ref, ...), custom_call_target="tpu_custom_call" | custom-call | flops 2000000000 | bytes 6000000 | tf_op jit(solution)/shard_map/join/pallas_call | solution.py:498
Async XLA Ops:
  0.6 6.2 %copy-start.2 = (s32[3]{0:T(128)S(1)}, s32[3]{0:T(128)}, u32[]{:S(2)}) copy-start(s32[3]{0:T(128)} %offset_ref.5) | copy-start | bytes 40
  1.8 5.0 %collective-permute-start = (bf16[2,8,16,128]{3,2,1,0:T(8,128)(2,1)S(1)}, bf16[2,8,16,128]{3,2,1,0:T(8,128)(2,1)S(1)}, u32[]{:S(2)}, u32[]{:S(2)}) collective-permute-start(bf16[2,8,16,128]{3,2,1,0:T(8,128)(2,1)S(1)} %get-tuple-element.27.head_ref), channel_id=1, source_target_pairs={{0,252},{4,0},{8,4},{12,8},{16,12},{20,16},{24,20},{28,24},{32,28}... | collective-permute-start | bytes 196616 | tf_op jit(solution)/shard_map/ppermute | solution.py:367
  6.9 10.7 %copy-start.1 = (f32[1,16,88]{2,1,0:T(8,128)S(1)}, f32[1,16,88]{2,1,0:T(8,128)}, u32[]{:S(2)}) copy-start(f32[1,16,88]{2,1,0:T(8,128)} %meas_ref.1) | copy-start | bytes 16900
  7.5 26.9 %collective-permute-start.3 = (bf16[3,8,16,128]{3,2,1,0:T(8,128)(2,1)S(1)}, bf16[3,8,16,128]{3,2,1,0:T(8,128)(2,1)S(1)}, u32[]{:S(2)}, u32[]{:S(2)}) collective-permute-start(bf16[3,8,16,128]{3,2,1,0:T(8,128)(2,1)S(1)} %shift.1.p0), channel_id=1, source_target_pairs={{0,1},{1,2},{2,3},{3,0},{4,5},{5,6},{6,7},{7,4},{8,9},{9,10},{10,1... | collective-permute-start | bytes 294920 | tf_op jit(solution)/shard_map/ppermute | solution.py:367
  10.5 23.8 %collective-permute-start.2 = (bf16[3,8,16,128]{3,2,1,0:T(8,128)(2,1)S(1)}, bf16[3,8,16,128]{3,2,1,0:T(8,128)(2,1)S(1)}, u32[]{:S(2)}, u32[]{:S(2)}) collective-permute-start(bf16[3,8,16,128]{3,2,1,0:T(8,128)(2,1)S(1)} %shift.1.p0), channel_id=1, source_target_pairs={{0,2},{1,3},{2,0},{3,1},{4,6},{5,7},{6,4},{7,5},{8,10},{9,11},{10,... | collective-permute-start | bytes 294920 | tf_op jit(solution)/shard_map/ppermute | solution.py:367
  15.2 19.2 %collective-permute-start.1 = (bf16[3,8,16,128]{3,2,1,0:T(8,128)(2,1)S(1)}, bf16[3,8,16,128]{3,2,1,0:T(8,128)(2,1)S(1)}, u32[]{:S(2)}, u32[]{:S(2)}) collective-permute-start(bf16[3,8,16,128]{3,2,1,0:T(8,128)(2,1)S(1)} %shift.1.p0), channel_id=1, source_target_pairs={{0,3},{1,0},{2,1},{3,2},{4,7},{5,4},{6,5},{7,6},{8,11},{9,8},{10,9... | collective-permute-start | bytes 294920 | tf_op jit(solution)/shard_map/ppermute | solution.py:367
  20.2 30.0 %all-to-all-start = ((f32[256,2,128]{2,1,0:T(2,128)}), f32[256,2,128]{2,1,0:T(2,128)S(1)}, u32[]{:S(2)}, u32[]{:S(2)}) async-start(f32[256,2,128]{2,1,0:T(2,128)} %bitcast.1), calls=%async_computation | async-start | bytes 524288 | tf_op jit(solution)/shard_map/all_to_all | solution.py:436
  39.5 17.6 %collective-permute-start.4 = (s16[2,3,136,128]{3,2,1,0:T(8,128)(2,1)S(1)}, s16[2,3,136,128]{3,2,1,0:T(8,128)(2,1)S(1)}, u32[]{:S(2)}, u32[]{:S(2)}) collective-permute-start(s16[2,3,136,128]{3,2,1,0:T(8,128)(2,1)S(1)} %get-tuple-element.30), channel_id=1, source_target_pairs={{0,2},{1,3},{2,0},{3,1},{4,6},{5,7},{6,4},{7,5},{8,10},{9,11},{10,... | collective-permute-start | bytes 626696 | tf_op jit(solution)/shard_map/ppermute | solution.py:367
  51.6 18.5 %all-to-all-start.1 = ((f32[256,1,128]{2,1,0:T(1,128)}), f32[256,1,128]{2,1,0:T(1,128)S(1)}, u32[]{:S(2)}, u32[]{:S(2)}) async-start(f32[256,1,128]{2,1,0:T(1,128)} %bitcast.4), calls=%async_computation.1 | async-start | bytes 262144 | tf_op jit(solution)/shard_map/all_to_all | solution.py:447
  57.2 14.7 %collective-permute-start.7 = (s16[2,136,128]{2,1,0:T(8,128)(2,1)S(1)}, s16[2,136,128]{2,1,0:T(8,128)(2,1)S(1)}, u32[]{:S(2)}, u32[]{:S(2)}) collective-permute-start(s16[2,136,128]{2,1,0:T(8,128)(2,1)S(1)} %get-tuple-element.34), channel_id=1, source_target_pairs={{0,5},{1,6},{2,7},{3,4},{4,9},{5,10},{6,11},{7,8},{8,13},{9,14},{1... | collective-permute-start | bytes 208904 | tf_op jit(solution)/shard_map/ppermute | solution.py:486
  61.7 10.2 %collective-permute-start.5 = (s16[3,136,128]{2,1,0:T(8,128)(2,1)S(1)}, s16[3,136,128]{2,1,0:T(8,128)(2,1)S(1)}, u32[]{:S(2)}, u32[]{:S(2)}) collective-permute-start(s16[3,136,128]{2,1,0:T(8,128)(2,1)S(1)} %get-tuple-element.33), channel_id=1, source_target_pairs={{0,1},{1,2},{2,3},{3,0},{4,5},{5,6},{6,7},{7,4},{8,9},{9,10},{10,1... | collective-permute-start | bytes 313352 | tf_op jit(solution)/shard_map/ppermute | solution.py:367
  64.7 7.3 %collective-permute-start.6 = (f32[2,8,16,128]{3,2,1,0:T(8,128)S(1)}, f32[2,8,16,128]{3,2,1,0:T(8,128)S(1)}, u32[]{:S(2)}, u32[]{:S(2)}) collective-permute-start(f32[2,8,16,128]{3,2,1,0:T(8,128)S(1)} %get-tuple-element.31.head_ref), channel_id=1, source_target_pairs={{0,4},{4,8},{8,12},{12,16},{16,20},{20,24},{24,28},{28,32},{32,36}... | collective-permute-start | bytes 393224 | tf_op jit(solution)/shard_map/ppermute | solution.py:367
  70.1 1.9 %copy-start = (f32[4,1,16,16,64]{4,3,2,1,0:T(8,128)S(1)}, f32[4,1,16,16,64]{4,3,2,1,0:T(8,128)}, u32[]{:S(2)}) copy-start(f32[4,1,16,16,64]{4,3,2,1,0:T(8,128)} %state_ref.1) | copy-start | bytes 786436
  70.1 1.9 %copy-start.3 = (f32[4]{0:T(128)S(1)}, f32[4]{0:T(128)}, u32[]{:S(2)}) copy-start(f32[4]{0:T(128)} %weight_ref.1) | copy-start | bytes 52
